TPU v7x, 32 devices: a whole 2x2x4 slice. The times are simulated.
32 devices in a mesh: grp: 8 (over z, y), blk: 4 (over x, core).
Axes of the slice: x: 2, y: 2, z: 4, core: 2. Of those that a mesh axis runs over, the one named last changes fastest.
Arguments:
- frames: bfloat16 [8, 512, 1536], P('grp', 'blk'), may hold values from -6 to 6
- text_states: bfloat16 [8, 64, 1536], P('grp'), may hold values from -6 to 6
- block_table: int32 [8, 8], P('grp'), may hold values from 0 to 7, each once within a row
- inward: bfloat16 [1536, 4608], P('grp', 'blk'), may hold values from -0.21875 to 0.21875
- outward: bfloat16 [1536, 1536], P('grp', 'blk'), may hold values from -1.75 to 1.75
- querying: bfloat16 [1536, 1536], P('grp', 'blk'), may hold values from -0.21875 to 0.21875
- keying: bfloat16 [1536, 3072], P('grp', 'blk'), may hold values from -0.21875 to 0.21875
- returning: bfloat16 [1536, 1536], P('grp', 'blk'), may hold values from -0.875 to 0.875
- expand: bfloat16 [1536, 6144], P('grp', 'blk'), may hold values from -0.15625 to 0.15625
- contract: bfloat16 [6144, 1536], P('blk', 'grp'), may hold values from -0.078125 to 0.078125
- gains: bfloat16 [3, 1536], P(None, ('grp', 'blk')), may hold values from 0.099609375 to 1.8984375
- shifts: bfloat16 [3, 1536], P(None, ('grp', 'blk')), may hold values from -1.1953125 to 1.1953125
- out_grad: bfloat16 [8, 512, 1536], P('grp', 'blk'), may hold values from -6 to 6
Outputs:
- block_out: bfloat16 [8, 512, 1536], P('grp', 'blk')
- frames_grad: float32 [8, 512, 1536], P('grp', 'blk')
- text_grad: float32 [8, 64, 1536], P('grp', 'blk')
- inward_grad: float32 [1536, 4608], P('grp', 'blk')
- outward_grad: float32 [1536, 1536], P('grp', 'blk')
- querying_grad: float32 [1536, 1536], P('grp', 'blk')
- keying_grad: float32 [1536, 3072], P('grp', 'blk')
- returning_grad: float32 [1536, 1536], P('grp', 'blk')
- expand_grad: float32 [1536, 6144], P('grp', 'blk')
- contract_grad: float32 [6144, 1536], P('blk', 'grp')
- gains_grad: float32 [3, 1536], P(None, ('grp', 'blk'))
- shifts_grad: float32 [3, 1536], P(None, ('grp', 'blk'))
Inputs may be any that keep to these rules, and one draw needn't show every extreme that they name: Each row is an ordering of the clip's 8 frame blocks: storage block s of clip c holds frames block_table[c, s] * 64 to block_table[c, s] * 64 + 63.
All inputs are finite; a program needn't handle non-finite values.
Results may differ from a plain program's by a relative error of at most 0.028.
Values may be sent and summed in bfloat16 or wider, within the bound.
A program may use at most 320 MiB of HBM per device.

v0:
```python
import math

import jax
import jax.numpy as jnp
from jax import lax
from jax.sharding import PartitionSpec as P

HEADS = 24
HEAD = 64
TEXT = 64
SEG = 64


def layer_norm(values, gain, shift):
    center = values - jnp.mean(values, axis=-1, keepdims=True)
    spread = jnp.mean(center * center, axis=-1, keepdims=True)
    return center * lax.rsqrt(spread + 1e-05) * gain + shift


def norm_pull(values, gain, shift, incoming):
    unused, pullback = jax.vjp(layer_norm, values, gain, shift)
    return pullback(incoming)


def gelu_slope(upward):
    return (
        0.5 * (1.0 + lax.erf(upward * 0.7071067811865476))
        + upward * jnp.exp(-0.5 * upward * upward) * 0.3989422804014327
    )


def gather_weights(inward, outward, querying, keying, returning, expand, contract, gains, shifts):
    inward, outward, querying, keying, returning, expand, contract, gains, shifts = (
        lax.all_gather(inward, "blk", axis=1, tiled=True),
        lax.all_gather(outward, "blk", axis=1, tiled=True),
        lax.all_gather(querying, "blk", axis=1, tiled=True),
        lax.all_gather(keying, "blk", axis=1, tiled=True),
        lax.all_gather(returning, "blk", axis=1, tiled=True),
        lax.all_gather(expand, "blk", axis=1, tiled=True),
        lax.all_gather(contract, "blk", axis=0, tiled=True),
        lax.all_gather(gains, "blk", axis=1, tiled=True),
        lax.all_gather(shifts, "blk", axis=1, tiled=True),
    )
    return (
        lax.all_gather(inward, "grp", axis=0, tiled=True),
        lax.all_gather(outward, "grp", axis=0, tiled=True),
        lax.all_gather(querying, "grp", axis=0, tiled=True),
        lax.all_gather(keying, "grp", axis=0, tiled=True),
        lax.all_gather(returning, "grp", axis=0, tiled=True),
        lax.all_gather(expand, "grp", axis=0, tiled=True),
        lax.all_gather(contract, "grp", axis=1, tiled=True),
        lax.all_gather(gains, "grp", axis=1, tiled=True),
        lax.all_gather(shifts, "grp", axis=1, tiled=True),
    )


def shards(
    frames,
    text_states,
    block_table,
    inward,
    outward,
    querying,
    keying,
    returning,
    expand,
    contract,
    gains,
    shifts,
    out_grad,
):
    (
        full_inward,
        full_outward,
        full_query,
        full_keys,
        full_return,
        full_expand,
        full_contract,
        full_gains,
        full_shifts,
    ) = gather_weights(
        inward, outward, querying, keying, returning, expand, contract, gains, shifts
    )
    width = frames.shape[2]
    rows = frames.shape[1]
    length = block_table.shape[1] * SEG
    group = lax.axis_size("blk")
    member = lax.axis_index("blk")
    span = math.gcd(length, 512)
    steps = length // span
    gain_rows = full_gains.astype(jnp.float32)
    shift_rows = full_shifts.astype(jnp.float32)
    key_frames = (
        block_table[0][:, None] * SEG + jnp.arange(SEG, dtype=jnp.int32)[None, :]
    ).reshape(length)
    own_frames = lax.dynamic_slice_in_dim(key_frames, member * rows, rows, 0)
    inputs = frames[0].astype(jnp.float32)
    first = layer_norm(inputs, gain_rows[0], shift_rows[0]).astype(jnp.bfloat16)
    joint = jnp.dot(first, full_inward, preferred_element_type=jnp.float32).astype(jnp.bfloat16)
    queries = joint[:, :width].reshape(rows, HEADS, HEAD)
    pairs = lax.all_gather(joint[:, width:], "blk", axis=0, tiled=True)
    pair_blocks = pairs.reshape(steps, span, 2 * width)
    frame_blocks = key_frames.reshape(steps, span)

    def scores_of(block, block_frames):
        keys = block[:, :width].reshape(span, HEADS, HEAD)
        raw = jnp.einsum("qhd,khd->hqk", queries, keys, preferred_element_type=jnp.float32) * 0.125
        allowed = block_frames[None, :] <= own_frames[:, None]
        return jnp.where(allowed[None], raw, -1e30)

    def stat_step(carry, items):
        peak, total = carry
        scores = scores_of(items[0], items[1])
        higher = jnp.maximum(peak, jnp.max(scores, axis=2))
        total = total * jnp.exp(peak - higher) + jnp.sum(
            jnp.exp(scores - higher[:, :, None]), axis=2
        )
        return ((higher, total), None)

    start_peak = jnp.full((HEADS, rows), -1e30, jnp.float32)
    (peak, total), unused = lax.scan(
        stat_step, (start_peak, jnp.zeros((HEADS, rows), jnp.float32)), (pair_blocks, frame_blocks)
    )
    log_total = peak + jnp.log(total)

    def out_step(carry, items):
        weighting = jnp.exp(scores_of(items[0], items[1]) - log_total[:, :, None]).astype(
            jnp.bfloat16
        )
        values = items[0][:, width:].reshape(span, HEADS, HEAD)
        return (
            carry
            + jnp.einsum("hqk,khd->qhd", weighting, values, preferred_element_type=jnp.float32),
            None,
        )

    mixed, unused = lax.scan(
        out_step, jnp.zeros((rows, HEADS, HEAD), jnp.float32), (pair_blocks, frame_blocks)
    )
    attended = mixed.reshape(rows, width).astype(jnp.bfloat16)
    hidden_one = inputs + jnp.dot(attended, full_outward, preferred_element_type=jnp.float32)
    second = layer_norm(hidden_one, gain_rows[1], shift_rows[1]).astype(jnp.bfloat16)
    cross_query = jnp.dot(second, full_query, preferred_element_type=jnp.float32).astype(
        jnp.bfloat16
    )
    cross_heads = cross_query.reshape(rows, HEADS, HEAD)
    text = text_states[0]
    text_pairs = jnp.dot(text, full_keys, preferred_element_type=jnp.float32).astype(jnp.bfloat16)
    text_keys = text_pairs[:, :width].reshape(TEXT, HEADS, HEAD)
    text_values = text_pairs[:, width:].reshape(TEXT, HEADS, HEAD)
    cross_scores = (
        jnp.einsum("qhd,khd->hqk", cross_heads, text_keys, preferred_element_type=jnp.float32)
        * 0.125
    )
    cross_soft = jax.nn.softmax(cross_scores, axis=2)
    cross_weighting = cross_soft.astype(jnp.bfloat16)
    crossed = (
        jnp.einsum("hqk,khd->qhd", cross_weighting, text_values, preferred_element_type=jnp.float32)
        .reshape(rows, width)
        .astype(jnp.bfloat16)
    )
    hidden_two = hidden_one + jnp.dot(crossed, full_return, preferred_element_type=jnp.float32)
    third = layer_norm(hidden_two, gain_rows[2], shift_rows[2]).astype(jnp.bfloat16)
    upward = jnp.dot(third, full_expand, preferred_element_type=jnp.float32)
    activated = jax.nn.gelu(upward, approximate=False).astype(jnp.bfloat16)
    branch = jnp.dot(activated, full_contract, preferred_element_type=jnp.float32)
    block_out = (hidden_two + branch).astype(jnp.bfloat16)[None]
    (
        full_inward,
        full_outward,
        full_query,
        full_keys,
        full_return,
        full_expand,
        full_contract,
        full_gains,
        full_shifts,
    ) = gather_weights(
        inward, outward, querying, keying, returning, expand, contract, gains, shifts
    )
    incoming = out_grad[0].astype(jnp.float32)
    branch_grad = out_grad[0]
    act_grad = jnp.dot(branch_grad, full_contract.T, preferred_element_type=jnp.float32)
    contract_grad = jnp.dot(activated.T, branch_grad, preferred_element_type=jnp.float32)
    up_grad = (act_grad * gelu_slope(upward)).astype(jnp.bfloat16)
    expand_grad = jnp.dot(third.T, up_grad, preferred_element_type=jnp.float32)
    third_grad = jnp.dot(up_grad, full_expand.T, preferred_element_type=jnp.float32)
    two_grad, gain_two, shift_two = norm_pull(hidden_two, gain_rows[2], shift_rows[2], third_grad)
    hidden_two_grad = incoming + two_grad
    branch_two = hidden_two_grad.astype(jnp.bfloat16)
    crossed_grad = jnp.dot(branch_two, full_return.T, preferred_element_type=jnp.float32).astype(
        jnp.bfloat16
    )
    crossed_grad = crossed_grad.reshape(rows, HEADS, HEAD)
    prob_grad = jnp.einsum(
        "qhd,khd->hqk", crossed_grad, text_values, preferred_element_type=jnp.float32
    )
    text_value_grad = jnp.einsum(
        "hqk,qhd->khd", cross_weighting, crossed_grad, preferred_element_type=jnp.float32
    )
    cross_score_grad = (
        cross_soft * (prob_grad - jnp.sum(prob_grad * cross_soft, axis=2, keepdims=True))
    ).astype(jnp.bfloat16)
    cross_query_grad = (
        (
            jnp.einsum(
                "hqk,khd->qhd", cross_score_grad, text_keys, preferred_element_type=jnp.float32
            )
            * 0.125
        )
        .reshape(rows, width)
        .astype(jnp.bfloat16)
    )
    text_key_grad = (
        jnp.einsum(
            "hqk,qhd->khd", cross_score_grad, cross_heads, preferred_element_type=jnp.float32
        )
        * 0.125
    )
    text_terms = jnp.concatenate(
        [text_key_grad.reshape(TEXT, width), text_value_grad.reshape(TEXT, width)], axis=1
    )
    text_share = lax.psum_scatter(
        text_terms.astype(jnp.bfloat16), "blk", scatter_dimension=0, tiled=True
    )
    share = TEXT // group
    text_grad = jnp.dot(text_share, full_keys.T, preferred_element_type=jnp.float32)[None]
    one_grad, gain_one, shift_one = norm_pull(
        hidden_one,
        gain_rows[1],
        shift_rows[1],
        jnp.dot(cross_query_grad, full_query.T, preferred_element_type=jnp.float32),
    )
    hidden_one_grad = hidden_two_grad + one_grad
    branch_one = hidden_one_grad.astype(jnp.bfloat16)
    attended_grad = jnp.dot(branch_one, full_outward.T, preferred_element_type=jnp.float32).astype(
        jnp.bfloat16
    )
    attended_grad = attended_grad.reshape(rows, HEADS, HEAD)
    delta = jnp.sum(attended_grad.astype(jnp.float32) * mixed, axis=2).T

    def back_step(carry, items):
        block = items[0]
        weighting = jnp.exp(scores_of(block, items[1]) - log_total[:, :, None])
        keys = block[:, :width].reshape(span, HEADS, HEAD)
        values = block[:, width:].reshape(span, HEADS, HEAD)
        value_grad = jnp.einsum(
            "hqk,qhd->khd",
            weighting.astype(jnp.bfloat16),
            attended_grad,
            preferred_element_type=jnp.float32,
        )
        weight_grad = jnp.einsum(
            "qhd,khd->hqk", attended_grad, values, preferred_element_type=jnp.float32
        )
        score_grad = (weighting * (weight_grad - delta[:, :, None])).astype(jnp.bfloat16)
        carry = carry + jnp.einsum(
            "hqk,khd->qhd", score_grad, keys, preferred_element_type=jnp.float32
        )
        key_grad = (
            jnp.einsum("hqk,qhd->khd", score_grad, queries, preferred_element_type=jnp.float32)
            * 0.125
        )
        return (
            carry,
            jnp.concatenate(
                [key_grad.reshape(span, width), value_grad.reshape(span, width)], axis=1
            ),
        )

    query_sum, pair_terms = lax.scan(
        back_step, jnp.zeros((rows, HEADS, HEAD), jnp.float32), (pair_blocks, frame_blocks)
    )
    pair_grad = lax.psum_scatter(
        pair_terms.reshape(length, 2 * width).astype(jnp.bfloat16),
        "blk",
        scatter_dimension=0,
        tiled=True,
    )
    joint_grad = jnp.concatenate(
        [(query_sum * 0.125).reshape(rows, width).astype(jnp.bfloat16), pair_grad], axis=1
    )
    zero_grad, gain_zero, shift_zero = norm_pull(
        inputs,
        gain_rows[0],
        shift_rows[0],
        jnp.dot(joint_grad, full_inward.T, preferred_element_type=jnp.float32),
    )
    frames_grad = (hidden_one_grad + zero_grad)[None]
    across = lax.axis_size("grp")
    gains_grad = (
        jnp.stack([gain_zero, gain_one, gain_two])
        .reshape(3, across, group, -1)
        .transpose(0, 2, 1, 3)
        .reshape(3, width)
    )
    shifts_grad = (
        jnp.stack([shift_zero, shift_one, shift_two])
        .reshape(3, across, group, -1)
        .transpose(0, 2, 1, 3)
        .reshape(3, width)
    )
    expand_grad, contract_grad = (
        lax.psum_scatter(
            expand_grad.astype(jnp.bfloat16), "blk", scatter_dimension=1, tiled=True
        ).astype(jnp.float32),
        lax.psum_scatter(
            contract_grad.astype(jnp.bfloat16), "blk", scatter_dimension=0, tiled=True
        ).astype(jnp.float32),
    )
    own_text = lax.dynamic_slice_in_dim(text, member * share, share, 0)
    inward_grad = jnp.dot(first.T, joint_grad, preferred_element_type=jnp.float32)
    outward_grad = jnp.dot(attended.T, branch_one, preferred_element_type=jnp.float32)
    querying_grad = jnp.dot(second.T, cross_query_grad, preferred_element_type=jnp.float32)
    keying_grad = jnp.dot(own_text.T, text_share, preferred_element_type=jnp.float32)
    returning_grad = jnp.dot(crossed.T, branch_two, preferred_element_type=jnp.float32)
    (
        inward_grad,
        outward_grad,
        querying_grad,
        keying_grad,
        returning_grad,
        gains_grad,
        shifts_grad,
    ) = (
        lax.psum_scatter(
            inward_grad.astype(jnp.bfloat16), "blk", scatter_dimension=1, tiled=True
        ).astype(jnp.float32),
        lax.psum_scatter(
            outward_grad.astype(jnp.bfloat16), "blk", scatter_dimension=1, tiled=True
        ).astype(jnp.float32),
        lax.psum_scatter(
            querying_grad.astype(jnp.bfloat16), "blk", scatter_dimension=1, tiled=True
        ).astype(jnp.float32),
        lax.psum_scatter(
            keying_grad.astype(jnp.bfloat16), "blk", scatter_dimension=1, tiled=True
        ).astype(jnp.float32),
        lax.psum_scatter(
            returning_grad.astype(jnp.bfloat16), "blk", scatter_dimension=1, tiled=True
        ).astype(jnp.float32),
        lax.psum_scatter(
            gains_grad.astype(jnp.bfloat16), "blk", scatter_dimension=1, tiled=True
        ).astype(jnp.float32),
        lax.psum_scatter(
            shifts_grad.astype(jnp.bfloat16), "blk", scatter_dimension=1, tiled=True
        ).astype(jnp.float32),
    )
    (
        inward_grad,
        outward_grad,
        querying_grad,
        keying_grad,
        returning_grad,
        expand_grad,
        contract_grad,
        gains_grad,
        shifts_grad,
    ) = (
        lax.psum_scatter(
            inward_grad.astype(jnp.bfloat16), "grp", scatter_dimension=0, tiled=True
        ).astype(jnp.float32),
        lax.psum_scatter(
            outward_grad.astype(jnp.bfloat16), "grp", scatter_dimension=0, tiled=True
        ).astype(jnp.float32),
        lax.psum_scatter(
            querying_grad.astype(jnp.bfloat16), "grp", scatter_dimension=0, tiled=True
        ).astype(jnp.float32),
        lax.psum_scatter(
            keying_grad.astype(jnp.bfloat16), "grp", scatter_dimension=0, tiled=True
        ).astype(jnp.float32),
        lax.psum_scatter(
            returning_grad.astype(jnp.bfloat16), "grp", scatter_dimension=0, tiled=True
        ).astype(jnp.float32),
        lax.psum_scatter(
            expand_grad.astype(jnp.bfloat16), "grp", scatter_dimension=0, tiled=True
        ).astype(jnp.float32),
        lax.psum_scatter(
            contract_grad.astype(jnp.bfloat16), "grp", scatter_dimension=1, tiled=True
        ).astype(jnp.float32),
        lax.psum_scatter(
            gains_grad.astype(jnp.bfloat16), "grp", scatter_dimension=1, tiled=True
        ).astype(jnp.float32),
        lax.psum_scatter(
            shifts_grad.astype(jnp.bfloat16), "grp", scatter_dimension=1, tiled=True
        ).astype(jnp.float32),
    )
    return (
        block_out,
        frames_grad,
        text_grad,
        inward_grad,
        outward_grad,
        querying_grad,
        keying_grad,
        returning_grad,
        expand_grad,
        contract_grad,
        gains_grad,
        shifts_grad,
    )


def solution(mesh):
    return jax.shard_map(
        shards,
        mesh=mesh,
        in_specs=(
            P("grp", "blk", None),
            P("grp", None, None),
            P("grp", None),
            P("grp", "blk"),
            P("grp", "blk"),
            P("grp", "blk"),
            P("grp", "blk"),
            P("grp", "blk"),
            P("grp", "blk"),
            P("blk", "grp"),
            P(None, ("grp", "blk")),
            P(None, ("grp", "blk")),
            P("grp", "blk", None),
        ),
        out_specs=(
            P("grp", "blk", None),
            P("grp", "blk", None),
            P("grp", "blk", None),
            P("grp", "blk"),
            P("grp", "blk"),
            P("grp", "blk"),
            P("grp", "blk"),
            P("grp", "blk"),
            P("grp", "blk"),
            P("blk", "grp"),
            P(None, ("grp", "blk")),
            P(None, ("grp", "blk")),
        ),
        check_vma=False,
    )
```

profile of v0, /device:TPU:0, one launch (start us, length us, event | category | flops | bytes accessed | tf_op | source)
XLA Modules:
  0.0 2924.7 jit_solution(8243646183512234769)
XLA Ops:
  8.8 24.3 all-gather.17.cloned.1.call-done
  34.3 17.8 all-gather.25.cloned.1.call-done
  62.6 26.5 all-gather.3
  89.2 26.6 all-gather.1
  116.4 134.1 %all-gather.19.cloned.1.call-done = bf16[1536,4608]{1,0:T(8,128)(2,1)} async-done(((bf16[192,4608]{1,0:T(8,128)(2,1)}), bf16[1536,4608]{1,0:T(8,128)(2,1)}) %all-gather.19.cloned.1.call-update) | async-done | bytes 14155792 | tf_op jit(solution)/shard_map/all_gather | solution.py:45
  250.5 7.2 convolution_convert_fusion.7
  258.7 11.6 all_gather.78
  270.4 9.9 all_gather.82
  280.4 8.1 all_gather.84
  289.3 16.7 all-gather.37.cloned.1.call-done
  306.4 139.7 %all-gather.27.cloned.1.call-done = bf16[1536,3072]{1,0:T(8,128)(2,1)} async-done(((bf16[192,3072]{1,0:T(8,128)(2,1)}), bf16[1536,3072]{1,0:T(8,128)(2,1)}) %all-gather.27.cloned.1.call-update) | async-done | bytes 9437200 | tf_op jit(solution)/shard_map/all_gather | solution.py:48
  453.1 21.9 all-gather.21.cloned.1.call-done
  490.6 66.5 %all-gather.23.cloned.1.call-done = bf16[1536,1536]{1,0:T(8,128)(2,1)} async-done(((bf16[192,1536]{1,0:T(8,128)(2,1)}), bf16[1536,1536]{1,0:T(8,128)(2,1)}) %all-gather.23.cloned.1.call-update) | async-done | bytes 4718608 | tf_op jit(solution)/shard_map/all_gather | solution.py:46
  560.6 76.8 %all-gather.29.cloned.1.call-done = bf16[1536,1536]{1,0:T(8,128)(2,1)} async-done(((bf16[192,1536]{1,0:T(8,128)(2,1)}), bf16[1536,1536]{1,0:T(8,128)(2,1)}) %all-gather.29.cloned.1.call-update) | async-done | bytes 4718608 | tf_op jit(solution)/shard_map/all_gather | solution.py:47
  643.5 74.0 %all-gather.31.cloned.1.call-done = bf16[1536,1536]{1,0:T(8,128)(2,1)} async-done(((bf16[192,1536]{1,0:T(8,128)(2,1)}), bf16[1536,1536]{1,0:T(8,128)(2,1)}) %all-gather.31.cloned.1.call-update) | async-done | bytes 4718608 | tf_op jit(solution)/shard_map/all_gather | solution.py:49
  721.1 358.6 %all-gather.35.cloned.1.call-done = bf16[1536,6144]{1,0:T(8,128)(2,1)} async-done(((bf16[192,6144]{1,0:T(8,128)(2,1)}), bf16[1536,6144]{1,0:T(8,128)(2,1)}) %all-gather.35.cloned.1.call-update) | async-done | bytes 18874384 | tf_op jit(solution)/shard_map/all_gather | solution.py:50
  1079.6 10.8 fusion.68
  1090.4 353.1 %all-gather.39.cloned.1.call-done = bf16[6144,1536]{0,1:T(8,128)(2,1)} async-done(((bf16[6144,192]{0,1:T(8,128)(2,1)}), bf16[6144,1536]{0,1:T(8,128)(2,1)}) %all-gather.39.cloned.1.call-update) | async-done | bytes 18874384 | tf_op jit(solution)/shard_map/all_gather | solution.py:51
  1443.5 10.8 fusion.1
  1454.3 14.2 multiply_reduce_fusion
  1519.6 24.8 reduce-scatter.61.cloned.1.call-done
  1546.7 11.0 fusion.71
  1567.0 6.7 copy.113
  1578.1 6.9 copy.111
  1589.6 6.7 copy.115
  1596.4 6.1 convolution_convert_fusion.3
  1603.6 8.3 convolution_convert_fusion.2
  1611.9 18.8 copy.109
  1631.7 16.2 convolution_convert_fusion
  1648.0 10.9 convolution_convert_fusion.1
  1668.5 47.8 %reduce-scatter.67.cloned.1.call-done = bf16[384,1536]{1,0:T(8,128)(2,1)} async-done(((bf16[1536,1536]{1,0:T(8,128)(2,1)}), bf16[384,1536]{1,0:T(8,128)(2,1)}) %reduce-scatter.67.cloned.1.call-update) | async-done | bytes 1179664
  1718.8 48.1 %reduce-scatter.71.cloned.1.call-done = bf16[384,1536]{1,0:T(8,128)(2,1)} async-done(((bf16[1536,1536]{1,0:T(8,128)(2,1)}), bf16[384,1536]{1,0:T(8,128)(2,1)}) %reduce-scatter.71.cloned.1.call-update) | async-done | bytes 1179664
  1769.3 78.4 %reduce-scatter.49.cloned.1.call-done = bf16[1536,768]{1,0:T(8,128)(2,1)} async-done(((bf16[1536,3072]{1,0:T(8,128)(2,1)}), bf16[1536,768]{1,0:T(8,128)(2,1)}) %reduce-scatter.49.cloned.1.call-update) | async-done | bytes 2359312 | tf_op jit(solution)/shard_map/reduce_scatter | solution.py:336
  1847.8 111.9 %reduce-scatter.65.cloned.1.call-done = bf16[1152,1536]{1,0:T(8,128)(2,1)} async-done(((bf16[4608,1536]{1,0:T(8,128)(2,1)}), bf16[1152,1536]{1,0:T(8,128)(2,1)}) %reduce-scatter.65.cloned.1.call-update) | async-done | bytes 3538960
  1959.7 5.8 copy.110
  1965.6 136.1 %reduce-scatter.59.cloned.1.call-done = bf16[1536,1536]{1,0:T(8,128)(2,1)} async-done(((bf16[6144,1536]{1,0:T(8,128)(2,1)}), bf16[1536,1536]{1,0:T(8,128)(2,1)}) %reduce-scatter.59.cloned.1.call-update) | async-done | bytes 4718608 | tf_op jit(solution)/shard_map/reduce_scatter | solution.py:308
  2101.8 6.7 copy.117
  2108.5 135.6 %reduce-scatter.55.cloned.1.call-done = bf16[1536,1536]{1,0:T(8,128)(2,1)} async-done(((bf16[1536,6144]{1,0:T(8,128)(2,1)}), bf16[1536,1536]{1,0:T(8,128)(2,1)}) %reduce-scatter.55.cloned.1.call-update) | async-done | bytes 4718608 | tf_op jit(solution)/shard_map/reduce_scatter | solution.py:305
  2244.1 16.5 fusion.19
  2265.1 39.7 %reduce-scatter.77.cloned.1.call-done = bf16[48,3]{1,0:T(8,128)(2,1)} async-done(((bf16[384,3]{1,0:T(8,128)(2,1)}), bf16[48,3]{1,0:T(8,128)(2,1)}) %reduce-scatter.77.cloned.1.call-update) | async-done | bytes 304
  2306.2 58.6 %reduce-scatter.81.cloned.1.call-done = bf16[48,3]{1,0:T(8,128)(2,1)} async-done(((bf16[384,3]{1,0:T(8,128)(2,1)}), bf16[48,3]{1,0:T(8,128)(2,1)}) %reduce-scatter.81.cloned.1.call-update) | async-done | bytes 304
  2366.1 65.5 %reduce-scatter.47.cloned.1.call-done = bf16[192,384]{1,0:T(8,128)(2,1)} async-done(((bf16[1536,384]{1,0:T(8,128)(2,1)}), bf16[192,384]{1,0:T(8,128)(2,1)}) %reduce-scatter.47.cloned.1.call-update) | async-done | bytes 147472 | tf_op jit(solution)/shard_map/reduce_scatter | solution.py:366
  2433.3 65.2 %reduce-scatter.45.cloned.1.call-done = bf16[192,384]{1,0:T(8,128)(2,1)} async-done(((bf16[1536,384]{1,0:T(8,128)(2,1)}), bf16[192,384]{1,0:T(8,128)(2,1)}) %reduce-scatter.45.cloned.1.call-update) | async-done | bytes 147472 | tf_op jit(solution)/shard_map/reduce_scatter | solution.py:363
  2500.2 64.8 %reduce-scatter.53.cloned.1.call-done = bf16[192,384]{1,0:T(8,128)(2,1)} async-done(((bf16[1536,384]{1,0:T(8,128)(2,1)}), bf16[192,384]{1,0:T(8,128)(2,1)}) %reduce-scatter.53.cloned.1.call-update) | async-done | bytes 147472 | tf_op jit(solution)/shard_map/reduce_scatter | solution.py:372
  2566.6 69.9 %reduce-scatter.51.cloned.1.call-done = bf16[192,768]{1,0:T(8,128)(2,1)} async-done(((bf16[1536,768]{1,0:T(8,128)(2,1)}), bf16[192,768]{1,0:T(8,128)(2,1)}) %reduce-scatter.51.cloned.1.call-update) | async-done | bytes 294928 | tf_op jit(solution)/shard_map/reduce_scatter | solution.py:369
  2638.4 79.8 %reduce-scatter.43.cloned.1.call-done = bf16[192,1152]{1,0:T(8,128)(2,1)} async-done(((bf16[1536,1152]{1,0:T(8,128)(2,1)}), bf16[192,1152]{1,0:T(8,128)(2,1)}) %reduce-scatter.43.cloned.1.call-update) | async-done | bytes 442384 | tf_op jit(solution)/shard_map/reduce_scatter | solution.py:360
  2720.2 96.5 %reduce-scatter.73.cloned.1.call-done = bf16[192,1536]{1,0:T(8,128)(2,1)} async-done(((bf16[1536,1536]{1,0:T(8,128)(2,1)}), bf16[192,1536]{1,0:T(8,128)(2,1)}) %reduce-scatter.73.cloned.1.call-update) | async-done | bytes 589840
  2819.3 96.2 %reduce-scatter.57.cloned.1.call-done = bf16[192,1536]{1,0:T(8,128)(2,1)} async-done(((bf16[1536,1536]{1,0:T(8,128)(2,1)}), bf16[192,1536]{1,0:T(8,128)(2,1)}) %reduce-scatter.57.cloned.1.call-update) | async-done | bytes 589840 | tf_op jit(solution)/shard_map/reduce_scatter | solution.py:375
  (269 shorter events, 160.6 us)
Async XLA Ops:
  7.2 439.0 %copy-start = (bf16[1,64,1536]{2,1,0:T(8,128)(2,1)S(1)}, bf16[1,64,1536]{2,1,0:T(8,128)(2,1)}, u32[]{:S(2)}) copy-start(bf16[1,64,1536]{2,1,0:T(8,128)(2,1)} %param.14) | copy-start | bytes 589828
  7.2 45.0 %copy-start.36 = (bf16[3,48]{1,0:T(4,128)(2,1)S(1)}, bf16[3,48]{1,0:T(4,128)(2,1)}, u32[]{:S(2)}) copy-start(bf16[3,48]{1,0:T(4,128)(2,1)} %param.23) | copy-start | bytes 868
  7.2 50.2 %copy-start.37 = (bf16[3,48]{1,0:T(4,128)(2,1)S(1)}, bf16[3,48]{1,0:T(4,128)(2,1)}, u32[]{:S(2)}) copy-start(bf16[3,48]{1,0:T(4,128)(2,1)} %param.24) | copy-start | bytes 868
  7.2 108.8 %copy-start.2 = (bf16[1,128,1536]{2,1,0:T(8,128)(2,1)S(1)}, bf16[1,128,1536]{2,1,0:T(8,128)(2,1)}, u32[]{:S(2)}) copy-start(bf16[1,128,1536]{2,1,0:T(8,128)(2,1)} %param.13) | copy-start | bytes 1179652
  7.2 25.9 all-gather.17.cloned.1.call-start
  8.0 44.2 %all-gather.25.cloned.1.call-start = ((), (), s32[]{:S(2)}) async-start(), calls=%async_computation.24 | async-start | bytes 1474560 | tf_op jit(solution)/shard_map/all_gather | solution.py:37
  8.7 241.7 %all-gather.19.cloned.1.call-start = ((), (), s32[]{:S(2)}) async-start(), calls=%async_computation.21 | async-start | bytes 15925248 | tf_op jit(solution)/shard_map/all_gather | solution.py:45
  33.1 255.4 %all-gather.33.cloned.1.call-start = ((), (), s32[]{:S(2)}) async-start(), calls=%async_computation.28 | async-start | bytes 2949120 | tf_op jit(solution)/shard_map/all_gather | solution.py:39
  33.7 272.3 %all-gather.37.cloned.1.call-start = ((), (), s32[]{:S(2)}) async-start(), calls=%async_computation.30 | async-start | bytes 2949120 | tf_op jit(solution)/shard_map/all_gather | solution.py:40
  34.3 411.8 %all-gather.27.cloned.1.call-start = ((), (), s32[]{:S(2)}) async-start(), calls=%async_computation.25 | async-start | bytes 10616832 | tf_op jit(solution)/shard_map/all_gather | solution.py:48
  52.2 422.8 %all-gather.21.cloned.1.call-start = ((), (), s32[]{:S(2)}) async-start(), calls=%async_computation.22 | async-start | bytes 3932160 | tf_op jit(solution)/shard_map/all_gather | solution.py:102
  257.7 22.7 copy-start.33
  258.7 298.5 %all-gather.23.cloned.1.call-start = ((), (), s32[]{:S(2)}) async-start(), calls=%async_computation.23 | async-start | bytes 5308416 | tf_op jit(solution)/shard_map/all_gather | solution.py:46
  270.3 367.0 %all-gather.29.cloned.1.call-start = ((), (), s32[]{:S(2)}) async-start(), calls=%async_computation.26 | async-start | bytes 5308416 | tf_op jit(solution)/shard_map/all_gather | solution.py:47
  280.3 25.8 copy-start.39
  280.3 437.2 %all-gather.31.cloned.1.call-start = ((), (), s32[]{:S(2)}) async-start(), calls=%async_computation.27 | async-start | bytes 5308416 | tf_op jit(solution)/shard_map/all_gather | solution.py:49
  288.5 791.1 %all-gather.35.cloned.1.call-start = ((), (), s32[]{:S(2)}) async-start(), calls=%async_computation.29 | async-start | bytes 21233664 | tf_op jit(solution)/shard_map/all_gather | solution.py:50
  289.2 1154.3 %all-gather.39.cloned.1.call-start = ((), (), s32[]{:S(2)}) async-start(), calls=%async_computation.31 | async-start | bytes 21233664 | tf_op jit(solution)/shard_map/all_gather | solution.py:51
  306.0 1238.4 %reduce-scatter.61.cloned.1.call-start = ((), (), s32[]{:S(2)}) async-start(), calls=%async_computation.41 | async-start | bytes 3932160
  451.8 1026.7 %copy-start.15 = (bf16[64,1536]{0,1:T(8,128)(2,1)}, bf16[64,1536]{0,1:T(8,128)(2,1)S(1)}, u32[]{:S(2)}) copy-start(bf16[64,1536]{0,1:T(8,128)(2,1)S(1)} %copy.131) | copy-start | bytes 589828
  453.1 30.7 %copy-start.10 = (bf16[128,1536]{0,1:T(8,128)(2,1)}, bf16[128,1536]{0,1:T(8,128)(2,1)S(1)}, u32[]{:S(2)}) copy-start(bf16[128,1536]{0,1:T(8,128)(2,1)S(1)} %copy.93) | copy-start | bytes 1179652
  490.6 69.8 %copy-start.19 = (bf16[128,24,64]{0,2,1:T(8,128)(2,1)}, bf16[128,24,64]{0,2,1:T(8,128)(2,1)S(1)}, u32[]{:S(2)}) copy-start(bf16[128,24,64]{0,2,1:T(8,128)(2,1)S(1)} %get-tuple-element.170) | copy-start | bytes 1179652
  640.8 80.0 %copy-start.16 = (bf16[128,1536]{0,1:T(8,128)(2,1)}, bf16[128,1536]{0,1:T(8,128)(2,1)S(1)}, u32[]{:S(2)}) copy-start(bf16[128,1536]{0,1:T(8,128)(2,1)S(1)} %copy.95) | copy-start | bytes 1179652
  1079.6 363.9 %copy-start.24 = (bf16[1,128,1536]{2,1,0:T(8,128)(2,1)S(1)}, bf16[1,128,1536]{2,1,0:T(8,128)(2,1)}, u32[]{:S(2)}) copy-start(bf16[1,128,1536]{2,1,0:T(8,128)(2,1)} %param.25) | copy-start | bytes 1179652
  1506.3 90.1 %reduce-scatter.63.cloned.1.call-start = ((), (), s32[]{:S(2)}) async-start(), calls=%async_computation.42 | async-start | bytes 491520
  1519.6 139.4 %reduce-scatter.75.cloned.1.call-start = ((), (), s32[]{:S(2)}) async-start(), calls=%async_computation.48 | async-start | bytes 491520
  1561.1 98.4 %reduce-scatter.79.cloned.1.call-start = ((), (), s32[]{:S(2)}) async-start(), calls=%async_computation.50 | async-start | bytes 491520
  1562.3 103.8 %reduce-scatter.69.cloned.1.call-start = ((), (), s32[]{:S(2)}) async-start(), calls=%async_computation.45 | async-start | bytes 5898240
  1573.7 142.6 %reduce-scatter.67.cloned.1.call-start = ((), (), s32[]{:S(2)}) async-start(), calls=%async_computation.44 | async-start | bytes 5898240
  1585.0 181.8 %reduce-scatter.71.cloned.1.call-start = ((), (), s32[]{:S(2)}) async-start(), calls=%async_computation.46 | async-start | bytes 5898240
  1596.3 251.4 %reduce-scatter.49.cloned.1.call-start = ((), (), s32[]{:S(2)}) async-start(), calls=%async_computation.35 | async-start | bytes 11796480 | tf_op jit(solution)/shard_map/reduce_scatter | solution.py:336
  1602.5 357.2 %reduce-scatter.65.cloned.1.call-start = ((), (), s32[]{:S(2)}) async-start(), calls=%async_computation.43 | async-start | bytes 17694720
  1630.8 471.0 %reduce-scatter.59.cloned.1.call-start = ((), (), s32[]{:S(2)}) async-start(), calls=%async_computation.40 | async-start | bytes 23592960 | tf_op jit(solution)/shard_map/reduce_scatter | solution.py:308
  1647.9 596.2 %reduce-scatter.55.cloned.1.call-start = ((), (), s32[]{:S(2)}) async-start(), calls=%async_computation.38 | async-start | bytes 23592960 | tf_op jit(solution)/shard_map/reduce_scatter | solution.py:305
  1658.9 645.9 %reduce-scatter.77.cloned.1.call-start = ((), (), s32[]{:S(2)}) async-start(), calls=%async_computation.49 | async-start | bytes 110592
  1659.4 705.3 %reduce-scatter.81.cloned.1.call-start = ((), (), s32[]{:S(2)}) async-start(), calls=%async_computation.51 | async-start | bytes 110592
  1660.2 771.4 %reduce-scatter.47.cloned.1.call-start = ((), (), s32[]{:S(2)}) async-start(), calls=%async_computation.34 | async-start | bytes 1327104 | tf_op jit(solution)/shard_map/reduce_scatter | solution.py:366
  1668.4 830.1 %reduce-scatter.45.cloned.1.call-start = ((), (), s32[]{:S(2)}) async-start(), calls=%async_computation.33 | async-start | bytes 1327104 | tf_op jit(solution)/shard_map/reduce_scatter | solution.py:363
  1718.7 846.2 %reduce-scatter.53.cloned.1.call-start = ((), (), s32[]{:S(2)}) async-start(), calls=%async_computation.37 | async-start | bytes 1327104 | tf_op jit(solution)/shard_map/reduce_scatter | solution.py:372
  1769.3 867.3 %reduce-scatter.51.cloned.1.call-start = ((), (), s32[]{:S(2)}) async-start(), calls=%async_computation.36 | async-start | bytes 2654208 | tf_op jit(solution)/shard_map/reduce_scatter | solution.py:369
  1847.8 870.4 %reduce-scatter.43.cloned.1.call-start = ((), (), s32[]{:S(2)}) async-start(), calls=%async_computation.32 | async-start | bytes 3981312 | tf_op jit(solution)/shard_map/reduce_scatter | solution.py:360
  1965.6 851.1 %reduce-scatter.73.cloned.1.call-start = ((), (), s32[]{:S(2)}) async-start(), calls=%async_computation.47 | async-start | bytes 5308416
  2108.4 152.2 %slice-start = ((s8[9437184]{0:T(1024)(128)(4,1)}), s8[1048576]{0:T(1024)(128)(4,1)S(1)}, s32[]{:S(2)}) async-start(s8[9437184]{0:T(1024)(128)(4,1)} %bitcast.183), calls=%async_computation.52 | async-start | bytes 2097152
  2108.4 807.1 %reduce-scatter.57.cloned.1.call-start = ((), (), s32[]{:S(2)}) async-start(), calls=%async_computation.39 | async-start | bytes 5308416 | tf_op jit(solution)/shard_map/reduce_scatter | solution.py:375
  2244.1 16.5 slice-start.1
  2244.1 16.5 slice-start.2
  2244.1 16.5 copy-start.29
  2636.5 281.2 %copy-start.1 = (bf16[1,64,1536]{2,1,0:T(8,128)(2,1)S(1)}, bf16[1,64,1536]{2,1,0:T(8,128)(2,1)}, u32[]{:S(2)}) copy-start(bf16[1,64,1536]{2,1,0:T(8,128)(2,1)} %param.14) | copy-start | bytes 589828
  (29 other events, 106.5 us)
Sparse Core Ops, SparseCore 0:
  9.6 23.4 all-gather.16
  34.7 17.4 all-gather.24
  54.4 196.0 all-gather.18
  251.9 27.2 all-gather.32
  280.5 25.4 all-gather.36
  308.0 138.0 all-gather.26
  448.3 26.7 all-gather.20
  477.2 79.8 all-gather.22
  559.3 78.0 all-gather.28
  639.4 78.0 all-gather.30
  719.0 360.5 all-gather.34
  1081.0 362.4 all-gather.38
  1506.5 37.9 reduce-scatter.60
  1547.5 20.8 reduce-scatter.62
  1571.5 20.8 reduce-scatter.74
  1594.8 20.7 reduce-scatter.78
  1618.2 47.8 reduce-scatter.68
  1668.4 47.8 reduce-scatter.66
  1719.0 47.8 reduce-scatter.70
  1769.3 78.3 reduce-scatter.48
  1850.3 109.3 reduce-scatter.64
  1962.3 139.3 reduce-scatter.58
  2104.5 139.4 reduce-scatter.54
  2247.2 57.5 reduce-scatter.76
  2308.1 56.6 reduce-scatter.80
  2368.6 62.9 reduce-scatter.46
  2435.4 63.0 reduce-scatter.44
  2501.9 62.9 reduce-scatter.52
  2568.4 68.0 reduce-scatter.50
  2640.0 78.1 reduce-scatter.42
  2721.8 94.8 reduce-scatter.72
  2820.3 95.1 reduce-scatter.56
where the time goes:
time: 2930 us; the launch traced here: 2920 us
  waiting for transfers between devices  2510 us (86%)
  matrix products  179 us (6%)
  local copies, waits for them, and re-layouts  97.7 us (3%)
  blocking collectives  92.8 us (3%)
    unnamed x43, waiting for transfers between devices  438 us
    all_gather x1, waiting for transfers between devices, gather_weights(): lax.all_gather(expand, 'grp', axis=0, tiled=True)  359 us
    all_gather x1, waiting for transfers between devices, gather_weights(): lax.all_gather(contract, 'grp', axis=1, tiled=True)  353 us
    all_gather x1, waiting for transfers between devices, gather_weights(): lax.all_gather(keying, 'grp', axis=0, tiled=True)  140 us
    reduce_scatter x1, waiting for transfers between devices, shards(): lax.psum_scatter(contract_grad.astype(jnp.bfloat16), 'blk', scatter_dimen...  136 us
    reduce_scatter x1, waiting for transfers between devices, shards(): lax.psum_scatter(expand_grad.astype(jnp.bfloat16), 'blk', scatter_dimensi...  136 us
    all_gather x1, waiting for transfers between devices, gather_weights(): lax.all_gather(inward, 'grp', axis=0, tiled=True)  134 us
    reduce_scatter x1, waiting for transfers between devices, shards(): lax.psum_scatter(expand_grad.astype(jnp.bfloat16), 'grp', scatter_dimensi...  96.2 us
  transfers between devices with their start and end apart: 32, of which 28 were waited for; matrix products, arithmetic and copies ran while one was open for 8% of the time, Pallas kernels for 0%

commit v1 on v0

--- a/solution.py
+++ b/solution.py
@@ -401,9 +401,226 @@
     )
 
 
+def tp_shards(
+    frames,
+    text_states,
+    block_table,
+    inward,
+    outward,
+    querying,
+    keying,
+    returning,
+    expand,
+    contract,
+    gains,
+    shifts,
+    out_grad,
+):
+    bf16, f32 = jnp.bfloat16, jnp.float32
+    width = frames.shape[2]
+    rows = frames.shape[1]
+    group = lax.axis_size("blk")
+    member = lax.axis_index("blk")
+    length = rows * group
+    heads = HEADS // group
+    wide = heads * HEAD
+
+    def mm(left, right):
+        return jnp.dot(left, right, preferred_element_type=f32)
+
+    def mm_t(left, right):
+        return lax.dot_general(left, right, (((1,), (1,)), ((), ())), preferred_element_type=f32)
+
+    def t_mm(left, right):
+        return lax.dot_general(left, right, (((0,), (0,)), ((), ())), preferred_element_type=f32)
+
+    def blk_rows(item):
+        return lax.all_gather(item, "blk", axis=0, tiled=True)
+
+    def blk_cols(item):
+        return lax.all_gather(item, "blk", axis=1, tiled=True)
+
+    def sum_rows(item):
+        return lax.psum_scatter(item.astype(bf16), "blk", scatter_dimension=0, tiled=True).astype(f32)
+
+    def sum_cols(item):
+        return lax.psum_scatter(item.astype(bf16), "blk", scatter_dimension=1, tiled=True)
+
+    def turn(item):
+        return lax.all_to_all(item, "blk", split_axis=1, concat_axis=0, tiled=True)
+
+    def own_rows(item):
+        return lax.dynamic_slice_in_dim(item, member * rows, rows, 0)
+
+    def own_cols(item, size):
+        return lax.dynamic_slice_in_dim(item, member * size, size, 1)
+
+    def spread(item, axis):
+        return lax.all_gather(item, "grp", axis=axis, tiled=True)
+
+    def collect(item, axis):
+        return lax.psum_scatter(
+            item.astype(bf16), "grp", scatter_dimension=axis, tiled=True
+        )
+
+    whole = blk_cols(inward)
+    aligned = jnp.concatenate(
+        [lax.dynamic_slice_in_dim(whole, part * width + member * wide, wide, 1) for part in range(3)],
+        axis=1,
+    )
+    full_inward = spread(aligned, 0)
+    full_outward = spread(outward, 0)
+    full_query = spread(querying, 0)
+    full_keys = spread(keying, 0)
+    full_return = spread(returning, 0)
+    full_expand = spread(expand, 0)
+    full_contract = spread(contract, 1)
+    norms = lax.all_gather(
+        jnp.concatenate([gains, shifts], axis=0), ("grp", "blk"), axis=1, tiled=True
+    ).astype(f32)
+    gain_rows, shift_rows = norms[:3], norms[3:]
+
+    frame_ids = (
+        block_table[0][:, None] * SEG + jnp.arange(SEG, dtype=jnp.int32)[None, :]
+    ).reshape(length)
+    allowed = frame_ids[None, :] <= frame_ids[:, None]
+
+    def split(item):
+        return item.reshape(item.shape[0], heads, HEAD)
+
+    inputs_all = blk_rows(frames[0]).astype(f32)
+    first = layer_norm(inputs_all, gain_rows[0], shift_rows[0]).astype(bf16)
+    joint = mm(first, full_inward).astype(bf16)
+    queries, keys, values = (split(joint[:, part * wide : (part + 1) * wide]) for part in range(3))
+    scores = jnp.einsum("qhd,khd->hqk", queries, keys, preferred_element_type=f32) * 0.125
+    soft = jax.nn.softmax(jnp.where(allowed[None], scores, -1e30), axis=2)
+    weighting = soft.astype(bf16)
+    attended = (
+        jnp.einsum("hqk,khd->qhd", weighting, values, preferred_element_type=f32)
+        .reshape(length, wide)
+        .astype(bf16)
+    )
+    attended_all = blk_cols(attended)
+    one = own_cols(inputs_all, wide) + mm(attended_all, full_outward)
+    one_all = blk_cols(one.astype(bf16)).astype(f32)
+    second = layer_norm(one_all, gain_rows[1], shift_rows[1]).astype(bf16)
+    cross_query = mm(second, full_query).astype(bf16)
+    cross_heads = split(cross_query)
+    text = text_states[0]
+    text_pairs = blk_cols(mm(text, full_keys).astype(bf16))
+    text_keys = split(own_cols(text_pairs[:, :width], wide))
+    text_values = split(own_cols(text_pairs[:, width:], wide))
+    cross_scores = (
+        jnp.einsum("qhd,khd->hqk", cross_heads, text_keys, preferred_element_type=f32) * 0.125
+    )
+    cross_soft = jax.nn.softmax(cross_scores, axis=2)
+    cross_weighting = cross_soft.astype(bf16)
+    crossed = (
+        jnp.einsum("hqk,khd->qhd", cross_weighting, text_values, preferred_element_type=f32)
+        .reshape(length, wide)
+        .astype(bf16)
+    )
+    crossed_all = blk_cols(crossed)
+    two = one + mm(crossed_all, full_return)
+    two_all = blk_cols(two.astype(bf16)).astype(f32)
+    third = layer_norm(two_all, gain_rows[2], shift_rows[2]).astype(bf16)
+    upward = mm(third, full_expand)
+    activated = jax.nn.gelu(upward, approximate=False).astype(bf16)
+    branch = sum_rows(mm(activated, full_contract))
+    two_rows = own_rows(two_all)
+    block_out = (two_rows + branch).astype(bf16)[None]
+
+    incoming = out_grad[0].astype(f32)
+    grad_all = blk_rows(out_grad[0])
+    act_grad = mm_t(grad_all, full_contract)
+    contract_grad = collect(t_mm(activated, grad_all), 1)
+    up_grad = (act_grad * gelu_slope(upward)).astype(bf16)
+    expand_grad = collect(t_mm(third, up_grad), 0)
+    third_grad = sum_rows(mm_t(up_grad, full_expand))
+    two_grad, gain_two, shift_two = norm_pull(two_rows, gain_rows[2], shift_rows[2], third_grad)
+    hidden_two_grad = incoming + two_grad
+    branch_two = turn(hidden_two_grad.astype(bf16))
+    returning_grad = collect(t_mm(crossed_all, branch_two), 0)
+    crossed_grad = split(sum_cols(mm_t(branch_two, full_return)))
+    prob_grad = jnp.einsum("qhd,khd->hqk", crossed_grad, text_values, preferred_element_type=f32)
+    text_value_grad = jnp.einsum(
+        "hqk,qhd->khd", cross_weighting, crossed_grad, preferred_element_type=f32
+    )
+    cross_score_grad = (
+        cross_soft * (prob_grad - jnp.sum(prob_grad * cross_soft, axis=2, keepdims=True))
+    ).astype(bf16)
+    cross_query_grad = (
+        (jnp.einsum("hqk,khd->qhd", cross_score_grad, text_keys, preferred_element_type=f32) * 0.125)
+        .reshape(length, wide)
+        .astype(bf16)
+    )
+    text_key_grad = (
+        jnp.einsum("hqk,qhd->khd", cross_score_grad, cross_heads, preferred_element_type=f32) * 0.125
+    )
+    text_terms = blk_cols(
+        jnp.concatenate(
+            [text_key_grad.reshape(TEXT, wide), text_value_grad.reshape(TEXT, wide)], axis=1
+        ).astype(bf16)
+    ).reshape(TEXT, group, 2, wide)
+    text_terms = text_terms.transpose(0, 2, 1, 3).reshape(TEXT, 2 * width)
+    own_terms = own_cols(text_terms, 2 * wide)
+    keying_grad = collect(t_mm(text, own_terms), 0)
+    text_grad = sum_rows(mm_t(own_terms, full_keys))[None]
+    querying_grad = collect(t_mm(second, cross_query_grad), 0)
+    one_rows = own_rows(one_all)
+    one_grad, gain_one, shift_one = norm_pull(
+        one_rows, gain_rows[1], shift_rows[1], sum_rows(mm_t(cross_query_grad, full_query))
+    )
+    hidden_one_grad = hidden_two_grad + one_grad
+    branch_one = turn(hidden_one_grad.astype(bf16))
+    outward_grad = collect(t_mm(attended_all, branch_one), 0)
+    attended_grad = split(sum_cols(mm_t(branch_one, full_outward)))
+    value_grad = jnp.einsum("hqk,qhd->khd", weighting, attended_grad, preferred_element_type=f32)
+    weight_grad = jnp.einsum("qhd,khd->hqk", attended_grad, values, preferred_element_type=f32)
+    score_grad = (
+        soft * (weight_grad - jnp.sum(weight_grad * soft, axis=2, keepdims=True))
+    ).astype(bf16)
+    query_grad = jnp.einsum("hqk,khd->qhd", score_grad, keys, preferred_element_type=f32) * 0.125
+    key_grad = jnp.einsum("hqk,qhd->khd", score_grad, queries, preferred_element_type=f32) * 0.125
+    joint_grad = jnp.concatenate(
+        [item.reshape(length, wide).astype(bf16) for item in (query_grad, key_grad, value_grad)],
+        axis=1,
+    )
+    inward_grad = collect(t_mm(first, joint_grad), 0)
+    zero_grad, gain_zero, shift_zero = norm_pull(
+        frames[0].astype(f32),
+        gain_rows[0],
+        shift_rows[0],
+        sum_rows(mm_t(joint_grad, full_inward)),
+    )
+    frames_grad = (hidden_one_grad + zero_grad)[None]
+    inward_all = blk_cols(inward_grad).reshape(-1, group, 3, wide).transpose(0, 2, 1, 3)
+    inward_grad = own_cols(inward_all.reshape(-1, 3 * width), 3 * wide)
+    norm_grads = lax.psum_scatter(
+        jnp.stack([gain_zero, gain_one, gain_two, shift_zero, shift_one, shift_two]),
+        ("grp", "blk"),
+        scatter_dimension=1,
+        tiled=True,
+    )
+    return (
+        block_out,
+        frames_grad,
+        text_grad,
+        inward_grad.astype(f32),
+        outward_grad.astype(f32),
+        querying_grad.astype(f32),
+        keying_grad.astype(f32),
+        returning_grad.astype(f32),
+        expand_grad.astype(f32),
+        contract_grad.astype(f32),
+        norm_grads[:3],
+        norm_grads[3:],
+    )
+
+
 def solution(mesh):
     return jax.shard_map(
-        shards,
+        tp_shards if HEADS % mesh.shape["blk"] == 0 else shards,
         mesh=mesh,
         in_specs=(
             P("grp", "blk", None),

time: 2930 us -> 1550 us (0.53)
  waiting for transfers between devices: 2510 us -> 1240 us
  matrix products: 179 us -> 119 us
  local copies, waits for them, and re-layouts: 97.7 us -> 41.3 us
    all_gather x12 -> x15, waiting for transfers between devices: 1280 us -> 465 us  [the longest x7 346 us: spread(): return lax.all_gather(item, 'grp', axis=axis, tiled=True)]
    reduce_scatter x9 -> x11, waiting for transfers between devices: 792 us -> 541 us  [the longest x6 450 us: collect(): lax.psum_scatter(item.astype(bf16), 'grp', scatter_dimension=axis, tiled=...]
    unnamed x43 -> x34, waiting for transfers between devices: 438 us -> 230 us
    dot_general x32 -> x31, matrix products: 178 us -> 111 us  [the longest x7 37.3 us: mm(): return jnp.dot(left, right, preferred_element_type=f32)]
    unnamed x110 -> x118, local copies, waits for them, and re-layouts: 82.4 us -> 26.3 us
    all_gather x7 -> x3, blocking collectives: 92.8 us -> 54 us  [the longest x1 41.1 us: tp_shards(): lax.all_gather(jnp.concatenate([gains, shifts], axis=0), ('grp', 'blk'),...]
  transfers between devices with their start and end apart: 32 -> 30, of which waited for: 28 -> 28; matrix products, arithmetic and copies ran while one was open for 8% -> 8% of each run, Pallas kernels for 0% -> 0%
where the time goes in v1:
time: 1550 us; the launch traced here: 1540 us
  waiting for transfers between devices  1240 us (80%)
  matrix products  119 us (8%)
  blocking collectives  82.1 us (5%)
  other arithmetic  48.3 us (3%)
  local copies, waits for them, and re-layouts  41.3 us (3%)
  between operations  15.7 us (1%)
    reduce_scatter x6, waiting for transfers between devices, collect(): lax.psum_scatter(item.astype(bf16), 'grp', scatter_dimension=axis, tiled=...  450 us
    all_gather x7, waiting for transfers between devices, spread(): return lax.all_gather(item, 'grp', axis=axis, tiled=True)  346 us
    unnamed x34, waiting for transfers between devices  230 us
    all_gather x6, waiting for transfers between devices, blk_cols(): return lax.all_gather(item, 'blk', axis=1, tiled=True)  113 us
    reduce_scatter x5, waiting for transfers between devices, sum_rows(): lax.psum_scatter(item.astype(bf16), 'blk', scatter_dimension=0, tiled=True)  91.2 us
    all_gather x1, blocking collectives, tp_shards(): lax.all_gather(jnp.concatenate([gains, shifts], axis=0), ('grp', 'blk'),...  41.1 us
    dot_general x7, matrix products, mm(): return jnp.dot(left, right, preferred_element_type=f32)  37.3 us
  transfers between devices with their start and end apart: 30, of which 28 were waited for; matrix products, arithmetic and copies ran while one was open for 8% of the time, Pallas kernels for 0%

profile of v1, /device:TPU:0, one launch (start us, length us, event | category | flops | bytes accessed | tf_op | source)
XLA Modules:
  0.0 1544.6 jit_solution(7152619066705357425)
XLA Ops:
  8.8 24.3 %all-gather.19.cloned.1.call-done = bf16[192,4608]{1,0:T(8,128)(2,1)} async-done(((bf16[192,1152]{1,0:T(8,128)(2,1)}), bf16[192,4608]{1,0:T(8,128)(2,1)}) %all-gather.19.cloned.1.call-update) | async-done | bytes 1769488 | tf_op jit(solution)/shard_map/all_gather | solution.py:441
  35.7 41.1 %all-gather.2 = bf16[32,48,6]{1,2,0:T(8,128)(2,1)S(1)} all-gather(bf16[1,48,6]{1,2,0:T(8,128)(2,1)S(1)} %maximum_bitcast_fusion), channel_id=1, replica_groups=mesh['grp'=8,'blk'=4] {'grp','blk'}, dimensions={0}, use_global_device_ids=true | all-gather | bytes 19008 | tf_op jit(solution)/shard_map/all_gather | solution.py:478
  82.0 40.6 %all-gather.21.cloned.1.call-done = bf16[1536,1152]{1,0:T(8,128)(2,1)} async-done(((bf16[192,1152]{1,0:T(8,128)(2,1)}), bf16[1536,1152]{1,0:T(8,128)(2,1)}) %all-gather.21.cloned.1.call-update) | async-done | bytes 3538960 | tf_op jit(solution)/shard_map/all_gather | solution.py:459
  122.6 4.4 convolution_convert_fusion.5
  127.8 6.2 fusion.90
  133.9 4.2 fusion.34
  140.9 23.3 %all-gather.25.cloned.1.call-done = bf16[1536,384]{1,0:T(8,128)(2,1)} async-done(((bf16[192,384]{1,0:T(8,128)(2,1)}), bf16[1536,384]{1,0:T(8,128)(2,1)}) %all-gather.25.cloned.1.call-update) | async-done | bytes 1179664 | tf_op jit(solution)/shard_map/all_gather | solution.py:459
  164.2 20.4 %all-gather.23.cloned.1.call-done = bf16[512,1536]{0,1:T(8,128)(2,1)} async-done(((bf16[512,384]{0,1:T(8,128)(2,1)}), bf16[512,1536]{0,1:T(8,128)(2,1)}) %all-gather.23.cloned.1.call-update) | async-done | bytes 1572880 | tf_op jit(solution)/shard_map/all_gather | solution.py:441
  184.6 4.0 fusion.91
  190.2 48.6 %all-gather.27.cloned.1.call-done = bf16[1536,768]{1,0:T(8,128)(2,1)} async-done(((bf16[192,768]{1,0:T(8,128)(2,1)}), bf16[1536,768]{1,0:T(8,128)(2,1)}) %all-gather.27.cloned.1.call-update) | async-done | bytes 2359312 | tf_op jit(solution)/shard_map/all_gather | solution.py:459
  241.0 6.7 all_gather.61
  248.7 10.5 all-gather.29.cloned.1.call-done
  262.9 39.5 %all-gather.31.cloned.1.call-done = bf16[1536,384]{1,0:T(8,128)(2,1)} async-done(((bf16[192,384]{1,0:T(8,128)(2,1)}), bf16[1536,384]{1,0:T(8,128)(2,1)}) %all-gather.31.cloned.1.call-update) | async-done | bytes 1179664 | tf_op jit(solution)/shard_map/all_gather | solution.py:459
  310.4 34.1 %all-gather.35.cloned.1.call-done = bf16[1536,384]{1,0:T(8,128)(2,1)} async-done(((bf16[192,384]{1,0:T(8,128)(2,1)}), bf16[1536,384]{1,0:T(8,128)(2,1)}) %all-gather.35.cloned.1.call-update) | async-done | bytes 1179664 | tf_op jit(solution)/shard_map/all_gather | solution.py:459
  344.5 20.4 %all-gather.33.cloned.1.call-done = bf16[512,1536]{0,1:T(8,128)(2,1)} async-done(((bf16[512,384]{0,1:T(8,128)(2,1)}), bf16[512,1536]{0,1:T(8,128)(2,1)}) %all-gather.33.cloned.1.call-update) | async-done | bytes 1572880 | tf_op jit(solution)/shard_map/all_gather | solution.py:441
  370.6 17.8 %all-gather.37.cloned.1.call-done = bf16[512,1536]{1,0:T(8,128)(2,1)} async-done(((bf16[512,384]{1,0:T(8,128)(2,1)}), bf16[512,1536]{1,0:T(8,128)(2,1)}) %all-gather.37.cloned.1.call-update) | async-done | bytes 1572880 | tf_op jit(solution)/shard_map/all_gather | solution.py:441
  392.1 78.3 %all-gather.39.cloned.1.call-done = bf16[1536,1536]{1,0:T(8,128)(2,1)} async-done(((bf16[192,1536]{1,0:T(8,128)(2,1)}), bf16[1536,1536]{1,0:T(8,128)(2,1)}) %all-gather.39.cloned.1.call-update) | async-done | bytes 4718608 | tf_op jit(solution)/shard_map/all_gather | solution.py:459
  470.4 13.2 fusion.5
  483.6 6.2 all-gather.47.cloned.1.call-done
  489.8 82.0 %all-gather.41.cloned.1.call-done = bf16[1536,1536]{0,1:T(8,128)(2,1)} async-done(((bf16[1536,192]{0,1:T(8,128)(2,1)}), bf16[1536,1536]{0,1:T(8,128)(2,1)}) %all-gather.41.cloned.1.call-update) | async-done | bytes 4718608 | tf_op jit(solution)/shard_map/all_gather | solution.py:459
  571.7 7.1 fusion.20
  580.0 3.8 convolution_convert_fusion.9
  583.8 6.6 convolution_convert_fusion.10
  594.3 15.9 %reduce-scatter.26.cloned.1.call-done = bf16[128,1536]{1,0:T(8,128)(2,1)} async-done(((bf16[512,1536]{1,0:T(8,128)(2,1)}), bf16[128,1536]{1,0:T(8,128)(2,1)}) %reduce-scatter.26.cloned.1.call-update) | async-done | bytes 393232 | tf_op jit(solution)/shard_map/reduce_scatter | solution.py:444
  611.8 29.1 %reduce-scatter.24.cloned.1.call-done = bf16[128,1536]{1,0:T(8,128)(2,1)} async-done(((bf16[512,1536]{1,0:T(8,128)(2,1)}), bf16[128,1536]{1,0:T(8,128)(2,1)}) %reduce-scatter.24.cloned.1.call-update) | async-done | bytes 393232 | tf_op jit(solution)/shard_map/reduce_scatter | solution.py:444
  645.6 18.3 %all_to_all.38 = bf16[128,4,384]{2,0,1:T(8,128)(2,1)S(1)} all-to-all(bf16[128,4,384]{2,0,1:T(8,128)(2,1)S(1)} %bitcast.192), channel_id=1, replica_groups=mesh['grp'=8,'blk'=4] {'blk'}, dimensions={1} | all-to-all | bytes 786432 | tf_op jit(solution)/shard_map/all_to_all | solution.py:450
  669.5 28.3 %reduce-scatter.46.cloned.1.call-done = bf16[384,512]{1,0:T(8,128)(2,1)} async-done(((bf16[1536,512]{1,0:T(8,128)(2,1)}), bf16[384,512]{1,0:T(8,128)(2,1)}) %reduce-scatter.46.cloned.1.call-update) | async-done | bytes 393232
  706.0 26.1 %reduce-scatter.28.cloned.1.call-done = bf16[128,1536]{1,0:T(8,128)(2,1)} async-done(((bf16[512,1536]{1,0:T(8,128)(2,1)}), bf16[128,1536]{1,0:T(8,128)(2,1)}) %reduce-scatter.28.cloned.1.call-update) | async-done | bytes 393232 | tf_op jit(solution)/shard_map/reduce_scatter | solution.py:444
  738.4 9.8 all_to_all.39
  753.8 28.2 %reduce-scatter.48.cloned.1.call-done = bf16[384,512]{1,0:T(8,128)(2,1)} async-done(((bf16[1536,512]{1,0:T(8,128)(2,1)}), bf16[384,512]{1,0:T(8,128)(2,1)}) %reduce-scatter.48.cloned.1.call-update) | async-done | bytes 393232
  782.0 4.9 fusion.37
  786.9 4.0 multiply_reduce_fusion
  800.2 5.6 convolution_convert_fusion.2
  811.8 6.1 all_gather.70
  825.6 6.1 convolution_convert_fusion.1
  833.6 4.4 convolution_convert_fusion
  841.1 4.4 copy.131
  852.4 58.7 %reduce-scatter.34.cloned.1.call-done = bf16[192,1152]{1,0:T(8,128)(2,1)} async-done(((bf16[1536,1152]{1,0:T(8,128)(2,1)}), bf16[192,1152]{1,0:T(8,128)(2,1)}) %reduce-scatter.34.cloned.1.call-update) | async-done | bytes 442384 | tf_op jit(solution)/shard_map/reduce_scatter | solution.py:462
  911.1 67.7 %reduce-scatter.40.cloned.1.call-done = bf16[192,384]{1,0:T(8,128)(2,1)} async-done(((bf16[1536,384]{1,0:T(8,128)(2,1)}), bf16[192,384]{1,0:T(8,128)(2,1)}) %reduce-scatter.40.cloned.1.call-update) | async-done | bytes 147472 | tf_op jit(solution)/shard_map/reduce_scatter | solution.py:462
  980.4 20.1 %reduce-scatter.32.cloned.1.call-done = bf16[16,1536]{1,0:T(8,128)(2,1)} async-done(((bf16[64,1536]{1,0:T(8,128)(2,1)}), bf16[16,1536]{1,0:T(8,128)(2,1)}) %reduce-scatter.32.cloned.1.call-update) | async-done | bytes 49168 | tf_op jit(solution)/shard_map/reduce_scatter | solution.py:444
  1001.9 66.6 %reduce-scatter.38.cloned.1.call-done = bf16[192,384]{1,0:T(8,128)(2,1)} async-done(((bf16[1536,384]{1,0:T(8,128)(2,1)}), bf16[192,384]{1,0:T(8,128)(2,1)}) %reduce-scatter.38.cloned.1.call-update) | async-done | bytes 147472 | tf_op jit(solution)/shard_map/reduce_scatter | solution.py:462
  1070.2 96.4 %reduce-scatter.42.cloned.1.call-done = bf16[192,1536]{1,0:T(8,128)(2,1)} async-done(((bf16[1536,1536]{1,0:T(8,128)(2,1)}), bf16[192,1536]{1,0:T(8,128)(2,1)}) %reduce-scatter.42.cloned.1.call-update) | async-done | bytes 589840 | tf_op jit(solution)/shard_map/reduce_scatter | solution.py:462
  1168.8 96.5 %reduce-scatter.44.cloned.1.call-done = bf16[1536,192]{0,1:T(8,128)(2,1)} async-done(((bf16[1536,1536]{0,1:T(8,128)(2,1)}), bf16[1536,192]{0,1:T(8,128)(2,1)}) %reduce-scatter.44.cloned.1.call-update) | async-done | bytes 589840 | tf_op jit(solution)/shard_map/reduce_scatter | solution.py:462
  1267.4 69.9 %reduce-scatter.50.cloned.1.call-done = bf16[192,768]{1,0:T(8,128)(2,1)} async-done(((bf16[1536,768]{1,0:T(8,128)(2,1)}), bf16[192,768]{1,0:T(8,128)(2,1)}) %reduce-scatter.50.cloned.1.call-update) | async-done | bytes 294928
  1339.5 64.5 %reduce-scatter.36.cloned.1.call-done = bf16[192,384]{1,0:T(8,128)(2,1)} async-done(((bf16[1536,384]{1,0:T(8,128)(2,1)}), bf16[192,384]{1,0:T(8,128)(2,1)}) %reduce-scatter.36.cloned.1.call-update) | async-done | bytes 147472 | tf_op jit(solution)/shard_map/reduce_scatter | solution.py:462
  1406.8 97.3 %reduce-scatter.52.cloned.1.call-done = f32[48,6]{1,0:T(8,128)} async-done(((f32[1536,6]{1,0:T(8,128)}), f32[48,6]{1,0:T(8,128)}) %reduce-scatter.52.cloned.1.call-update) | async-done | bytes 1168
  1506.3 19.1 %all-gather.43.cloned.1.call-done = bf16[192,4608]{1,0:T(8,128)(2,1)} async-done(((bf16[192,1152]{1,0:T(8,128)(2,1)}), bf16[192,4608]{1,0:T(8,128)(2,1)}) %all-gather.43.cloned.1.call-update) | async-done | bytes 1769488 | tf_op jit(solution)/shard_map/all_gather | solution.py:441
  1525.4 5.2 reshape.305
  (283 shorter events, 132.4 us)
Async XLA Ops:
  7.2 231.6 %copy-start = (bf16[1,64,1536]{2,1,0:T(8,128)(2,1)S(1)}, bf16[1,64,1536]{2,1,0:T(8,128)(2,1)}, u32[]{:S(2)}) copy-start(bf16[1,64,1536]{2,1,0:T(8,128)(2,1)} %param.14) | copy-start | bytes 589828
  7.2 28.5 %copy-start.41 = (bf16[3,48]{1,0:T(4,128)(2,1)S(1)}, bf16[3,48]{1,0:T(4,128)(2,1)}, u32[]{:S(2)}) copy-start(bf16[3,48]{1,0:T(4,128)(2,1)} %param.24) | copy-start | bytes 868
  7.2 28.5 %copy-start.42 = (bf16[3,48]{1,0:T(4,128)(2,1)S(1)}, bf16[3,48]{1,0:T(4,128)(2,1)}, u32[]{:S(2)}) copy-start(bf16[3,48]{1,0:T(4,128)(2,1)} %param.23) | copy-start | bytes 868
  7.2 69.8 %copy-start.49 = (s32[1,8]{1,0:T(1,128)S(1)}, s32[1,8]{1,0:T(1,128)}, u32[]{:S(2)}) copy-start(s32[1,8]{1,0:T(1,128)} %param.15) | copy-start | bytes 100
  7.2 25.9 %all-gather.19.cloned.1.call-start = ((), (), s32[]{:S(2)}) async-start(), calls=%async_computation.17 | async-start | bytes 2211840 | tf_op jit(solution)/shard_map/all_gather | solution.py:441
  8.0 70.2 %all-gather.45.cloned.1.call-start = ((), (), s32[]{:S(2)}) async-start(), calls=%async_computation.41 | async-start | bytes 1966080 | tf_op jit(solution)/shard_map/all_gather | solution.py:438
  8.7 113.9 %all-gather.21.cloned.1.call-start = ((), (), s32[]{:S(2)}) async-start(), calls=%async_computation.18 | async-start | bytes 3981312 | tf_op jit(solution)/shard_map/all_gather | solution.py:459
  35.0 129.2 %all-gather.25.cloned.1.call-start = ((), (), s32[]{:S(2)}) async-start(), calls=%async_computation.20 | async-start | bytes 1327104 | tf_op jit(solution)/shard_map/all_gather | solution.py:459
  35.6 149.0 %all-gather.23.cloned.1.call-start = ((), (), s32[]{:S(2)}) async-start(), calls=%async_computation.19 | async-start | bytes 1966080 | tf_op jit(solution)/shard_map/all_gather | solution.py:441
  77.1 49.9 %copy-start.32 = (f32[1536]{0:T(1024)}, f32[1536]{0:T(1024)S(1)}, u32[]{:S(2)}) copy-start(f32[1536]{0:T(1024)S(1)} %get-tuple-element.89) | copy-start | bytes 18436
  77.1 225.3 %copy-start.30 = (f32[1536]{0:T(1024)}, f32[1536]{0:T(1024)S(1)}, u32[]{:S(2)}) copy-start(f32[1536]{0:T(1024)S(1)} %get-tuple-element.87) | copy-start | bytes 18436
  78.2 44.4 %copy-start.1 = (bf16[1,512,1536]{2,1,0:T(8,128)(2,1)S(1)}, bf16[1,512,1536]{2,1,0:T(8,128)(2,1)}, u32[]{:S(2)}) copy-start(bf16[1,512,1536]{2,1,0:T(8,128)(2,1)} %all-gather.45.cloned.1.call-done) | copy-start | bytes 4718596
  82.0 45.0 %copy-start.35 = (f32[512]{0:T(512)}, f32[512]{0:T(512)S(1)}, u32[]{:S(2)}) copy-start(f32[512]{0:T(512)S(1)} %add_rsqrt_fusion.2) | copy-start | bytes 6148
  138.2 100.6 %all-gather.27.cloned.1.call-start = ((), (), s32[]{:S(2)}) async-start(), calls=%async_computation.21 | async-start | bytes 2654208 | tf_op jit(solution)/shard_map/all_gather | solution.py:459
  138.7 120.4 %all-gather.29.cloned.1.call-start = ((), (), s32[]{:S(2)}) async-start(), calls=%async_computation.22 | async-start | bytes 1966080 | tf_op jit(solution)/shard_map/all_gather | solution.py:441
  188.7 113.7 %all-gather.31.cloned.1.call-start = ((), (), s32[]{:S(2)}) async-start(), calls=%async_computation.23 | async-start | bytes 1327104 | tf_op jit(solution)/shard_map/all_gather | solution.py:459
  189.4 155.0 %all-gather.35.cloned.1.call-start = ((), (), s32[]{:S(2)}) async-start(), calls=%async_computation.25 | async-start | bytes 1327104 | tf_op jit(solution)/shard_map/all_gather | solution.py:459
  190.2 174.7 %all-gather.33.cloned.1.call-start = ((), (), s32[]{:S(2)}) async-start(), calls=%async_computation.24 | async-start | bytes 1966080 | tf_op jit(solution)/shard_map/all_gather | solution.py:441
  259.1 43.3 %copy-start.2 = (bf16[512,1536]{1,0:T(8,128)(2,1)S(1)}, bf16[512,1536]{1,0:T(8,128)(2,1)}, u32[]{:S(2)}) copy-start(bf16[512,1536]{1,0:T(8,128)(2,1)} %all-gather.29.cloned.1.call-done) | copy-start | bytes 4718596
  262.9 42.6 %copy-start.37 = (f32[512]{0:T(512)}, f32[512]{0:T(512)S(1)}, u32[]{:S(2)}) copy-start(f32[512]{0:T(512)S(1)} %add_rsqrt_fusion.1) | copy-start | bytes 6148
  310.3 78.1 %all-gather.37.cloned.1.call-start = ((), (), s32[]{:S(2)}) async-start(), calls=%async_computation.26 | async-start | bytes 1966080 | tf_op jit(solution)/shard_map/all_gather | solution.py:441
  368.6 101.8 %all-gather.39.cloned.1.call-start = ((), (), s32[]{:S(2)}) async-start(), calls=%async_computation.27 | async-start | bytes 5308416 | tf_op jit(solution)/shard_map/all_gather | solution.py:459
  369.2 120.6 %all-gather.47.cloned.1.call-start = ((), (), s32[]{:S(2)}) async-start(), calls=%async_computation.42 | async-start | bytes 1966080 | tf_op jit(solution)/shard_map/all_gather | solution.py:438
  370.0 201.8 %all-gather.41.cloned.1.call-start = ((), (), s32[]{:S(2)}) async-start(), calls=%async_computation.28 | async-start | bytes 5308416 | tf_op jit(solution)/shard_map/all_gather | solution.py:459
  370.5 239.7 %reduce-scatter.26.cloned.1.call-start = ((), (), s32[]{:S(2)}) async-start(), calls=%async_computation.30 | async-start | bytes 1966080 | tf_op jit(solution)/shard_map/reduce_scatter | solution.py:444
  392.1 91.5 %copy-start.39 = (f32[512]{0:T(512)}, f32[512]{0:T(512)S(1)}, u32[]{:S(2)}) copy-start(f32[512]{0:T(512)S(1)} %add_rsqrt_fusion) | copy-start | bytes 6148
  583.8 57.2 %reduce-scatter.24.cloned.1.call-start = ((), (), s32[]{:S(2)}) async-start(), calls=%async_computation.29 | async-start | bytes 1966080 | tf_op jit(solution)/shard_map/reduce_scatter | solution.py:444
  590.5 107.3 %reduce-scatter.46.cloned.1.call-start = ((), (), s32[]{:S(2)}) async-start(), calls=%async_computation.43 | async-start | bytes 1966080
  641.0 23.7 %copy-start.24 = (bf16[1536,384]{1,0:T(8,128)(2,1)S(1)}, bf16[1536,384]{1,0:T(8,128)(2,1)}, u32[]{:S(2)}) copy-start(bf16[1536,384]{1,0:T(8,128)(2,1)} %all-gather.35.cloned.1.call-done) | copy-start | bytes 3538948
  643.5 23.3 %copy-start.34 = (f32[128]{0:T(128)}, f32[128]{0:T(128)S(1)}, u32[]{:S(2)}) copy-start(f32[128]{0:T(128)S(1)} %negate_multiply_fusion.3) | copy-start | bytes 1540
  669.5 62.6 %reduce-scatter.28.cloned.1.call-start = ((), (), s32[]{:S(2)}) async-start(), calls=%async_computation.31 | async-start | bytes 1966080 | tf_op jit(solution)/shard_map/reduce_scatter | solution.py:444
  703.7 78.3 %reduce-scatter.48.cloned.1.call-start = ((), (), s32[]{:S(2)}) async-start(), calls=%async_computation.44 | async-start | bytes 1966080
  733.7 15.3 copy-start.22
  753.8 94.4 %reduce-scatter.30.cloned.1.call-start = ((), (), s32[]{:S(2)}) async-start(), calls=%async_computation.32 | async-start | bytes 1966080 | tf_op jit(solution)/shard_map/reduce_scatter | solution.py:444
  799.9 111.2 %reduce-scatter.34.cloned.1.call-start = ((), (), s32[]{:S(2)}) async-start(), calls=%async_computation.34 | async-start | bytes 3981312 | tf_op jit(solution)/shard_map/reduce_scatter | solution.py:462
  805.8 172.9 %reduce-scatter.40.cloned.1.call-start = ((), (), s32[]{:S(2)}) async-start(), calls=%async_computation.38 | async-start | bytes 1327104 | tf_op jit(solution)/shard_map/reduce_scatter | solution.py:462
  810.4 190.1 %reduce-scatter.32.cloned.1.call-start = ((), (), s32[]{:S(2)}) async-start(), calls=%async_computation.33 | async-start | bytes 245760 | tf_op jit(solution)/shard_map/reduce_scatter | solution.py:444
  811.6 10.5 copy-start.31
  811.7 10.5 copy-start.38
  822.1 246.5 %reduce-scatter.38.cloned.1.call-start = ((), (), s32[]{:S(2)}) async-start(), calls=%async_computation.37 | async-start | bytes 1327104 | tf_op jit(solution)/shard_map/reduce_scatter | solution.py:462
  825.5 341.0 %reduce-scatter.42.cloned.1.call-start = ((), (), s32[]{:S(2)}) async-start(), calls=%async_computation.39 | async-start | bytes 5308416 | tf_op jit(solution)/shard_map/reduce_scatter | solution.py:462
  831.7 433.5 %reduce-scatter.44.cloned.1.call-start = ((), (), s32[]{:S(2)}) async-start(), calls=%async_computation.40 | async-start | bytes 5308416 | tf_op jit(solution)/shard_map/reduce_scatter | solution.py:462
  838.0 499.4 %reduce-scatter.50.cloned.1.call-start = ((), (), s32[]{:S(2)}) async-start(), calls=%async_computation.45 | async-start | bytes 2654208
  845.5 558.4 %reduce-scatter.36.cloned.1.call-start = ((), (), s32[]{:S(2)}) async-start(), calls=%async_computation.36 | async-start | bytes 1327104 | tf_op jit(solution)/shard_map/reduce_scatter | solution.py:462
  847.7 656.5 %reduce-scatter.52.cloned.1.call-start = ((), (), s32[]{:S(2)}) async-start(), calls=%async_computation.46 | async-start | bytes 811008
  852.3 673.1 %all-gather.43.cloned.1.call-start = ((), (), s32[]{:S(2)}) async-start(), calls=%async_computation.35 | async-start | bytes 2211840 | tf_op jit(solution)/shard_map/all_gather | solution.py:441
  980.4 425.2 %copy-start.10 = (bf16[128,1536]{1,0:T(8,128)(2,1)S(1)}, bf16[128,1536]{1,0:T(8,128)(2,1)}, u32[]{:S(2)}) copy-start(bf16[128,1536]{1,0:T(8,128)(2,1)} %reduce-scatter.30.cloned.1.call-done) | copy-start | bytes 1179652
  980.4 425.2 %copy-start.11 = (f32[128,1536]{1,0:T(8,128)S(1)}, f32[128,1536]{1,0:T(8,128)}, u32[]{:S(2)}) copy-start(f32[128,1536]{1,0:T(8,128)} %get-tuple-element.92) | copy-start | bytes 2359300
  (37 other events, 118.9 us)
Sparse Core Ops, SparseCore 0:
  9.6 23.4 all-gather.18
  34.7 19.8 all-gather.44
  57.3 65.2 all-gather.20
  124.6 39.5 all-gather.24
  166.2 18.4 all-gather.22
  186.7 52.0 all-gather.26
  240.9 18.1 all-gather.28
  261.3 41.0 all-gather.30
  304.6 39.8 all-gather.34
  346.4 18.4 all-gather.32
  368.8 19.6 all-gather.36
  390.5 79.8 all-gather.38
  472.0 17.7 all-gather.46
  491.8 79.8 all-gather.40
  583.9 26.2 reduce-scatter.25
  612.8 28.1 reduce-scatter.23
  669.6 28.1 reduce-scatter.45
  703.8 28.1 reduce-scatter.27
  753.9 28.1 reduce-scatter.47
  800.0 28.1 reduce-scatter.29
  831.9 79.1 reduce-scatter.33
  915.0 63.6 reduce-scatter.39
  981.8 18.6 reduce-scatter.31
  1004.3 64.1 reduce-scatter.37
  1072.2 94.3 reduce-scatter.41
  1170.1 95.1 reduce-scatter.43
  1268.6 68.7 reduce-scatter.49
  1340.8 63.1 reduce-scatter.35
  1409.6 94.4 reduce-scatter.51
  1505.5 19.8 all-gather.42

commit v2 on v0

--- a/solution.py
+++ b/solution.py
@@ -1,8 +1,11 @@
+import functools
 import math
 
 import jax
 import jax.numpy as jnp
 from jax import lax
+from jax.experimental import pallas as pl
+from jax.experimental.pallas import tpu as pltpu
 from jax.sharding import PartitionSpec as P
 
 HEADS = 24
@@ -401,9 +404,1534 @@
     )
 
 
+MESH = pl.DeviceIdType.MESH
+BF16, F32 = jnp.bfloat16, jnp.float32
+
+
+class Bag:
+    def __init__(self, **items):
+        self.__dict__.update(items)
+
+
+def named(keys, items):
+    return Bag(**dict(zip(keys, items)))
+
+
+class Spot:
+    def __init__(self):
+        grp, blk = lax.axis_index("grp"), lax.axis_index("blk")
+        self.grp, self.blk = grp, blk
+        self.z, self.y = grp // 2, lax.rem(grp, 2)
+        self.x, self.core = blk // 2, lax.rem(blk, 2)
+        self.sib_blk = self.x * 2 + 1 - self.core
+        self.opp_blk = (1 - self.x) * 2 + self.core
+        self.sib = (grp, self.sib_blk)
+        self.opp = (grp, self.opp_blk)
+        self.part = (self.z * 2 + 1 - self.y, blk)
+        self.up = ((self.z + 1) * 2 + self.y, blk)
+        self.down = ((self.z - 1) * 2 + self.y, blk)
+
+        self.far_blk = (1 - self.x) * 2 + 1 - self.core
+
+    def z_peer(self, k):
+        return (lax.rem(self.z + k, 4) * 2 + self.y, self.blk)
+
+    def greet_all(self):
+        barrier = pltpu.get_barrier_semaphore()
+        peers = [self.z_peer(k) for k in (1, 2, 3)]
+        for who in [self.sib, self.opp, (self.grp, self.far_blk), self.part] + peers:
+            pl.semaphore_signal(barrier, inc=1, device_id=who, device_id_type=MESH)
+        pl.semaphore_wait(barrier, 7)
+
+    def greet(self):
+        barrier = pltpu.get_barrier_semaphore()
+        for who in (self.sib, self.opp, self.part):
+            pl.semaphore_signal(barrier, inc=1, device_id=who, device_id_type=MESH)
+
+        @pl.when(self.z > 0)
+        def _():
+            pl.semaphore_signal(barrier, inc=1, device_id=self.down, device_id_type=MESH)
+
+        @pl.when(self.z < 3)
+        def _():
+            pl.semaphore_signal(barrier, inc=1, device_id=self.up, device_id_type=MESH)
+
+        ends = (self.z == 0) | (self.z == 3)
+
+        @pl.when(ends)
+        def _():
+            pl.semaphore_wait(barrier, 4)
+
+        @pl.when(jnp.logical_not(ends))
+        def _():
+            pl.semaphore_wait(barrier, 5)
+
+
+def push(src, dst, send, recv, who):
+    return pltpu.make_async_remote_copy(
+        src_ref=src, dst_ref=dst, send_sem=send, recv_sem=recv, device_id=who, device_id_type=MESH
+    )
+
+
+class Gather:
+    def __init__(self, spot, shard, full, zsend, zrecv, ysend, yrecv, near, spread):
+        self.spot, self.shard, self.full = spot, shard, full
+        self.zsend, self.zrecv, self.ysend, self.yrecv, self.near = zsend, zrecv, ysend, yrecv, near
+        self.spread = spread
+        self.size = shard.shape[0]
+
+    def rows(self, z, flip=0):
+        spot = self.spot
+        row = z * 2 + (1 - spot.y if flip else spot.y)
+        return self.full.at[pl.ds(pl.multiple_of(row * self.size, self.size), self.size)]
+
+    def z_copy(self, src, dst, k, side, flip):
+        slot = (flip * 2 + side) * 3 + k - 1
+        who = self.spot.up if side else self.spot.down
+        return push(src, dst, self.zsend.at[slot], self.zrecv.at[slot], who)
+
+    def y_copy(self, src, dst, slot):
+        return push(src, dst, self.ysend.at[slot], self.yrecv.at[slot], self.spot.part)
+
+    def launch(self, src, flip):
+        spot = self.spot
+
+        @pl.when(spot.z > 0)
+        def _():
+            self.z_copy(src, self.rows(spot.z, flip), 1, 0, flip).start()
+
+        @pl.when(spot.z < 3)
+        def _():
+            self.z_copy(src, self.rows(spot.z, flip), 1, 1, flip).start()
+
+    def start(self):
+        here = self.rows(self.spot.z)
+        self.y_copy(self.shard, here, 0).start()
+        self.launch(self.shard, 0)
+        pltpu.make_async_copy(self.shard, here, self.near).start()
+
+    def relay(self, k):
+        spot = self.spot
+        if self.spread and k == 1:
+            other = self.rows(spot.z, 1)
+            self.y_copy(other, other, 0).wait_recv()
+            self.launch(other, 1)
+        for flip in (0, 1) if self.spread else (0,):
+            for side in (0, 1):
+                src_z = spot.z - k if side else spot.z + k
+                block = self.rows(src_z, flip)
+
+                @pl.when(src_z >= 0 if side else src_z <= 3)
+                def _():
+                    self.z_copy(block, block, k, side, flip).wait_recv()
+                    if k < 3:
+
+                        @pl.when(spot.z < 3 if side else spot.z > 0)
+                        def _():
+                            self.z_copy(block, block, k + 1, side, flip).start()
+
+                    if not self.spread:
+                        self.y_copy(block, block, 1 + side * 3 + k - 1).start()
+
+    def finish(self):
+        spot = self.spot
+        pltpu.make_async_copy(self.shard, self.rows(spot.z), self.near).wait()
+        if self.spread:
+            return
+        self.y_copy(self.shard, self.rows(spot.z, 1), 0).wait_recv()
+        for side in (0, 1):
+            for k in (1, 2, 3):
+                src_z = spot.z - k if side else spot.z + k
+                block = self.rows(src_z, 1)
+
+                @pl.when(src_z >= 0 if side else src_z <= 3)
+                def _():
+                    self.y_copy(block, block, 1 + side * 3 + k - 1).wait_recv()
+
+    def drain(self):
+        spot = self.spot
+        self.y_copy(self.shard, self.rows(spot.z), 0).wait_send()
+        for side in (0, 1):
+            for k in (1, 2, 3):
+                src_z = spot.z - k if side else spot.z + k
+                sent_z = spot.z - k + 1 if side else spot.z + k - 1
+                block = self.rows(spot.z)
+                if not self.spread:
+
+                    @pl.when(src_z >= 0 if side else src_z <= 3)
+                    def _():
+                        self.y_copy(block, block, 1 + side * 3 + k - 1).wait_send()
+
+                for flip in (0, 1) if self.spread else (0,):
+
+                    @pl.when((spot.z < 3) & (sent_z >= 0) if side else (spot.z > 0) & (sent_z <= 3))
+                    def _():
+                        self.z_copy(block, block, k, side, flip).wait_send()
+
+
+class Share:
+    def __init__(self, spot, own, where, send, recv):
+        self.spot, self.own, self.where, self.send, self.recv = spot, own, where, send, recv
+
+    def first(self):
+        return push(
+            self.own, self.where(self.spot.blk), self.send.at[0], self.recv.at[0], self.spot.opp
+        )
+
+    def second(self):
+        return push(
+            self.own, self.where(self.spot.blk), self.send.at[1], self.recv.at[1], self.spot.sib
+        )
+
+    def third(self):
+        passed = self.where(self.spot.opp_blk)
+        return push(passed, passed, self.send.at[2], self.recv.at[2], self.spot.sib)
+
+    def start(self):
+        self.first().start()
+        self.second().start()
+
+    def relay(self):
+        self.first().wait_recv()
+        self.third().start()
+
+    def finish(self):
+        self.second().wait_recv()
+        self.third().wait_recv()
+
+    def drain(self):
+        self.first().wait_send()
+        self.second().wait_send()
+        self.third().wait_send()
+
+
+def dot(left, right):
+    return jnp.dot(left, right, preferred_element_type=F32)
+
+
+def dot_t(left, right):
+    return lax.dot_general(left, right, (((1,), (1,)), ((), ())), preferred_element_type=F32)
+
+
+def tiles(count, size, body):
+    @pl.loop(0, count)
+    def _(step):
+        body(pl.ds(pl.multiple_of(step * size, size), size))
+
+
+def norm_block(values, gain, shift):
+    center = values - jnp.mean(values, axis=1, keepdims=True)
+    spread = jnp.mean(center * center, axis=1, keepdims=True)
+    return center * lax.rsqrt(spread + 1e-05) * gain + shift
+
+
+def forward_kernel(names, *refs):
+    r = named(names, refs)
+    spot = Spot()
+    rows, width = r.frames.shape
+    length = r.x_all.shape[0]
+    wide = r.outward.shape[1]
+    blk = spot.blk
+    outs = []
+
+    def save(src, dst):
+        copy = pltpu.make_async_copy(src, dst, r.local.at[len(outs)])
+        copy.start()
+        outs.append(copy)
+        return copy
+
+    def lanes(index, size):
+        return pl.ds(pl.multiple_of(index * size, 128), size)
+
+    def row_block(ref):
+        return lambda index: ref.at[pl.ds(pl.multiple_of(index * rows, rows), rows)]
+
+    def col_block(ref, size):
+        return lambda index: ref.at[:, lanes(index, size)]
+
+    def share(number, own, where):
+        return Share(spot, own, where, r.bsend.at[number], r.brecv.at[number])
+
+    def gather(number, shard, full, spread=False):
+        sems = (item.at[number] for item in (r.zsend, r.zrecv, r.ysend, r.yrecv, r.near))
+        return Gather(spot, shard, full, *sems, spread)
+
+    gathers = Bag(
+        outward=gather(0, r.outward, r.v_outward),
+        inward=gather(1, r.aligned, r.v_inward),
+        query=gather(2, r.query, r.v_query),
+        keys=gather(3, r.keys, r.v_keys, True),
+        back=gather(4, r.back, r.v_back, True),
+        expand=gather(5, r.expand, r.v_expand),
+        contract=gather(6, r.contract, r.v_contract),
+        norms=gather(7, r.v_norms, r.v_norm_all),
+    )
+
+    spot.greet()
+
+    def piece(part):
+        index = blk * 3 + part
+        owner = lax.rem(index, 4)
+        return owner, index // 4
+
+    def aligned_copy(part):
+        owner, kind = piece(part)
+        src = r.inward.at[:, part * wide : (part + 1) * wide]
+        return owner, kind, src, r.aligned.at[:, lanes(kind, wide)]
+
+    for part in range(3):
+        owner, kind, src, dst = aligned_copy(part)
+
+        @pl.when(owner == blk)
+        def _():
+            pltpu.make_async_copy(src, dst, r.arecv.at[kind]).start()
+
+        @pl.when(owner != blk)
+        def _():
+            push(src, dst, r.asend.at[part], r.arecv.at[kind], (spot.grp, owner)).start()
+
+    norm_share = share(0, r.norms, lambda index: r.v_norms.at[pl.ds(index * 16, 16)])
+    norm_own = pltpu.make_async_copy(r.norms, r.v_norms.at[pl.ds(blk * 16, 16)], r.near.at[8])
+    norm_own.start()
+    norm_share.start()
+    frame_share = share(1, r.frames, row_block(r.x_all))
+    frame_own = pltpu.make_async_copy(r.frames, row_block(r.x_all)(blk), r.near.at[9])
+    frame_own.start()
+    frame_share.start()
+    gathers.outward.start()
+    for kind in range(3):
+        dst = r.aligned.at[:, kind * wide : (kind + 1) * wide]
+        home = (kind * 4 + blk) // 3
+
+        @pl.when(home == blk)
+        def _():
+            pltpu.make_async_copy(dst, dst, r.arecv.at[kind]).wait()
+
+        @pl.when(home != blk)
+        def _():
+            push(dst, dst, r.asend.at[0], r.arecv.at[kind], spot.sib).wait_recv()
+
+    gathers.inward.start()
+    norm_share.relay()
+    norm_own.wait()
+    norm_share.finish()
+    gathers.norms.start()
+    frame_share.relay()
+    grad_share = share(2, r.incoming, row_block(r.g_all))
+    grad_own = pltpu.make_async_copy(r.incoming, row_block(r.g_all)(blk), r.near.at[10])
+    grad_own.start()
+    grad_share.start()
+    gathers.outward.relay(1)
+    gathers.norms.relay(1)
+    gathers.outward.relay(2)
+    gathers.norms.relay(2)
+    gathers.outward.relay(3)
+    gathers.norms.relay(3)
+    gathers.query.start()
+    gathers.norms.finish()
+
+    depth = 8 * 128
+    line = lax.broadcasted_iota(jnp.int32, (depth, 384), 0)
+    column = lax.broadcasted_iota(jnp.int32, (depth, 384), 1)
+    inside = line & 127
+    place = jnp.where((inside < 48) & (column == (line >> 7) * 48 + inside), 1.0, 0.0).astype(BF16)
+    for pair in range(4):
+        left = jnp.concatenate(
+            [r.v_norm_all[pair * 128 + part * 16 : pair * 128 + part * 16 + 16, :] for part in range(8)],
+            axis=1,
+        )
+        r.v_norm_rows[:, pair * 384 : (pair + 1) * 384] = dot(left, place)
+    save(r.v_norm_rows, r.norm_all)
+    gathers.inward.relay(1)
+    frame_own.wait()
+    frame_share.finish()
+    grad_share.relay()
+
+    def normed(source, index, turned):
+        gain = r.v_norm_rows[index : index + 1, :]
+        shift = r.v_norm_rows[3 + index : 4 + index, :]
+
+        def body(block):
+            result = norm_block(source[block, :].astype(F32), gain, shift).astype(BF16)
+            r.a_all[block, :] = result
+
+        tiles(length // 32, 32, body)
+
+        def flip(block):
+            turned[:, block] = r.a_all[block, :].T
+
+        tiles(length // 128, 128, flip)
+
+    normed(r.x_all, 0, r.t_first)
+    save(r.t_first, r.first_t)
+    gathers.keys.start()
+    gathers.inward.relay(2)
+    gathers.inward.relay(3)
+    gathers.query.relay(1)
+    gathers.query.relay(2)
+    gathers.query.relay(3)
+    gathers.back.start()
+    gathers.inward.finish()
+    save(r.v_inward, r.w_inward)
+
+    def joint_tile(block):
+        r.s_joint[:, block] = dot(r.a_all[...], r.v_inward[:, block]).astype(BF16)
+
+    tiles(3, wide, joint_tile)
+    save(r.s_joint, r.joint)
+    gathers.keys.relay(1)
+
+    low = lax.broadcasted_iota(jnp.int32, (1, 128), 1) < 64
+
+    def half(value, part):
+        return jnp.where(low if part == 0 else jnp.logical_not(low), value, jnp.zeros_like(value))
+
+    def attend_step(step):
+        pair, block = step // 4, lax.rem(step, 4)
+        here = pl.ds(pl.multiple_of(block * 128, 128), 128)
+        query = r.s_joint[here, lanes(pair, 128)]
+        key = r.s_joint[:, lanes(pair + 3, 128)]
+        value = r.s_joint[:, lanes(pair + 6, 128)]
+        keep = r.ids_row[...] <= r.ids_col[here, :]
+        results = []
+        for part in (0, 1):
+            scores = jnp.where(keep, dot_t(half(query, part), key) * 0.125, -1e30)
+            power = jnp.exp(scores - jnp.max(scores, axis=1, keepdims=True))
+            weighting = (power * (1.0 / jnp.sum(power, axis=1, keepdims=True))).astype(BF16)
+            results.append(dot(weighting, value))
+        r.s_attended[here, lanes(blk * 3 + pair, 128)] = jnp.where(low, *results).astype(BF16)
+
+    @pl.loop(0, 12)
+    def _(step):
+        attend_step(step)
+
+    attended_share = share(3, col_block(r.s_attended, wide)(blk), col_block(r.s_attended, wide))
+    attended_share.start()
+    gathers.keys.relay(2)
+    gathers.keys.relay(3)
+    gathers.outward.finish()
+    save(r.v_outward, r.w_outward)
+    attended_share.relay()
+    gathers.expand.start()
+    attended_share.finish()
+    r.s_one[...] = dot(r.s_attended[...], r.v_outward[...]) + r.x_all[:, lanes(blk, wide)].astype(F32)
+    r.s_one_all[:, lanes(blk, wide)] = r.s_one[...].astype(BF16)
+    one_share = share(4, col_block(r.s_one_all, wide)(blk), col_block(r.s_one_all, wide))
+    one_share.start()
+    gathers.back.relay(1)
+    gathers.back.relay(2)
+    one_share.relay()
+
+    def turn_over(source, turned):
+        def flip(block):
+            turned[:, block] = source[block, :].T
+
+        tiles(length // 128, 128, flip)
+
+    turn_over(r.s_attended, r.t_attended)
+    save(r.t_attended, r.attended_t)
+    gathers.back.relay(3)
+    gathers.contract.start()
+    gathers.keys.finish()
+    save(r.v_keys, r.w_keys)
+    r.s_text[:, lanes(blk, 2 * wide)] = dot(r.text[...], r.v_keys[...]).astype(BF16)
+    text_share = share(5, col_block(r.s_text, 2 * wide)(blk), col_block(r.s_text, 2 * wide))
+    one_share.finish()
+    text_share.start()
+    save(row_block(r.s_one_all)(blk), r.one_rows)
+    normed(r.s_one_all, 1, r.t_second)
+    save(r.t_second, r.second_t)
+    text_share.relay()
+    gathers.expand.relay(1)
+    gathers.query.finish()
+    save(r.v_query, r.w_query)
+    r.s_query[...] = dot(r.a_all[...], r.v_query[...]).astype(BF16)
+    save(r.s_query, r.cross_query)
+    text_share.finish()
+    save(r.s_text, r.text_all)
+
+    @pl.loop(0, 3)
+    def _(pair):
+        query = r.s_query[:, lanes(pair, 128)]
+        key = r.s_text[:, lanes(blk * 3 + pair, 128)]
+        value = r.s_text[:, lanes(12 + blk * 3 + pair, 128)]
+        results = []
+        for part in (0, 1):
+            scores = dot_t(half(query, part), key) * 0.125
+            power = jnp.exp(scores - jnp.max(scores, axis=1, keepdims=True))
+            weighting = (power * (1.0 / jnp.sum(power, axis=1, keepdims=True))).astype(BF16)
+            results.append(dot(weighting, value))
+        r.s_crossed[:, lanes(blk * 3 + pair, 128)] = jnp.where(low, *results).astype(BF16)
+
+    crossed_share = share(6, col_block(r.s_crossed, wide)(blk), col_block(r.s_crossed, wide))
+    crossed_share.start()
+    gathers.expand.relay(2)
+    crossed_share.relay()
+    gathers.back.finish()
+    save(r.v_back, r.w_back)
+    crossed_share.finish()
+    r.s_one[...] += dot(r.s_crossed[...], r.v_back[...])
+    r.s_two_all[:, lanes(blk, wide)] = r.s_one[...].astype(BF16)
+    two_share = share(7, col_block(r.s_two_all, wide)(blk), col_block(r.s_two_all, wide))
+    two_share.start()
+    gathers.expand.relay(3)
+    two_share.relay()
+    turn_over(r.s_crossed, r.t_crossed)
+    save(r.t_crossed, r.crossed_t)
+    two_share.finish()
+    save(row_block(r.s_two_all)(blk), r.two_rows)
+    gathers.contract.relay(1)
+    normed(r.s_two_all, 2, r.t_third)
+    save(r.t_third, r.third_t)
+    grad_share.finish()
+    grad_own.wait()
+    save(r.g_all, r.grad_all)
+    gathers.expand.finish()
+    kept = save(r.v_expand, r.w_expand)
+    gathers.contract.relay(2)
+
+    def upward_tile(block):
+        r.s_upward[:, block] = dot(r.a_all[...], r.v_expand[:, block])
+
+    tiles(4, 384, upward_tile)
+    gathers.contract.relay(3)
+
+    def gelu_tile(block):
+        upward = r.s_upward[block, :]
+        gate = 0.5 + 0.5 * lax.erf(upward * 0.7071067811865476)
+        r.s_active[block, :] = (upward * gate).astype(BF16)
+        r.s_slope[block, :] = gate + upward * jnp.exp(-0.5 * upward * upward) * 0.3989422804014327
+
+    tiles(length // 16, 16, gelu_tile)
+    save(r.s_slope, r.slope)
+    turn_over(r.g_all, r.t_grad)
+    kept.wait()
+    gathers.expand.drain()
+
+    def contract_tile(block):
+        r.v_expand[:, block] = dot(r.t_grad[...], r.s_active[:, block]).astype(BF16)
+
+    tiles(4, 384, contract_tile)
+    save(r.v_expand, r.contract_grad)
+    save(r.s_active, r.active)
+    gathers.contract.finish()
+    save(r.v_contract, r.w_contract)
+    for part in range(3):
+        owner, kind, src, dst = aligned_copy(part)
+
+        @pl.when(owner != blk)
+        def _():
+            push(src, dst, r.asend.at[part], r.arecv.at[kind], (spot.grp, owner)).wait_send()
+
+    for item in (
+        norm_share, frame_share, grad_share, attended_share, one_share, text_share, crossed_share, two_share,
+    ):
+        item.drain()
+    for item in vars(gathers).values():
+        if item is not gathers.expand:
+            item.drain()
+    for copy in outs:
+        if copy is not kept:
+            copy.wait()
+
+
+def ids_of(table):
+    ids = (table[0][:, None] * SEG + jnp.arange(SEG, dtype=jnp.int32)[None, :]).reshape(-1)
+    return ids[:, None], ids[None, :]
+
+
+def run_kernel(kernel, number, inner, outer, out, vmem, sems, credits):
+    anywhere = pl.BlockSpec(memory_space=pl.ANY)
+    inside = pl.BlockSpec(memory_space=pltpu.VMEM)
+    names = [*inner, *outer, *out, *vmem, *sems, *credits]
+    results = pl.pallas_call(
+        functools.partial(kernel, names),
+        out_shape=[jax.ShapeDtypeStruct(*item) for item in out.values()],
+        in_specs=[inside] * len(inner) + [anywhere] * len(outer),
+        out_specs=[anywhere] * len(out),
+        scratch_shapes=[pltpu.VMEM(*item) for item in vmem.values()]
+        + [pltpu.SemaphoreType.DMA(shape) for shape in sems.values()]
+        + [pltpu.SemaphoreType.REGULAR(shape) for shape in credits.values()],
+        compiler_params=pltpu.CompilerParams(
+            collective_id=number, has_side_effects=True, vmem_limit_bytes=60 * 2**20
+        ),
+    )(*inner.values(), *outer.values())
+    return named(out, results)
+
+
+def forward(frames, text, table, norms, incoming, weights):
+    rows, width = frames.shape
+    length = rows * lax.axis_size("blk")
+    wide = width // lax.axis_size("blk")
+    feed = weights["expand"].shape[1]
+    ids_col, ids_row = ids_of(table)
+    one = ((width, wide), BF16)
+    two = ((width, 2 * wide), BF16)
+    three = ((width, 3 * wide), BF16)
+    four = ((width, feed), BF16)
+    square, turned, strip = ((length, width), BF16), ((width, length), BF16), ((length, wide), BF16)
+    big = ((length, feed), F32)
+    own = ((rows, width), BF16)
+    out = dict(
+        w_outward=one,
+        w_inward=three,
+        w_query=one,
+        w_keys=two,
+        w_back=one,
+        w_expand=four,
+        w_contract=four,
+        first_t=turned,
+        second_t=turned,
+        third_t=turned,
+        attended_t=turned,
+        crossed_t=turned,
+        contract_grad=four,
+        grad_all=square,
+        joint=((length, 3 * wide), BF16),
+        cross_query=strip,
+        text_all=((TEXT, 2 * width), BF16),
+        slope=big,
+        active=((length, feed), BF16),
+        one_rows=own,
+        two_rows=own,
+        norm_all=((16, width), F32),
+        aligned=((width // lax.axis_size("grp"), 3 * wide), BF16),
+    )
+    vmem = dict(
+        v_outward=one,
+        v_inward=three,
+        v_query=one,
+        v_keys=two,
+        v_back=one,
+        v_expand=four,
+        v_contract=four,
+        x_all=square,
+        g_all=square,
+        a_all=square,
+        s_attended=square,
+        s_one_all=square,
+        s_crossed=square,
+        s_two_all=square,
+        t_first=turned,
+        t_second=turned,
+        t_third=turned,
+        t_attended=turned,
+        t_crossed=turned,
+        t_grad=turned,
+        s_joint=((length, 3 * wide), BF16),
+        s_one=((length, wide), F32),
+        s_query=strip,
+        s_text=((TEXT, 2 * width), BF16),
+        s_upward=big,
+        s_slope=big,
+        s_active=((length, feed), BF16),
+        v_norms=((64, 128), BF16),
+        v_norm_all=((512, 128), BF16),
+        v_norm_rows=((16, width), F32),
+    )
+    sems = dict(
+        zsend=(8, 12),
+        zrecv=(8, 12),
+        ysend=(8, 7),
+        yrecv=(8, 7),
+        near=(12,),
+        bsend=(8, 3),
+        brecv=(8, 3),
+        asend=(3,),
+        arecv=(3,),
+        local=(32,),
+    )
+    inner = dict(text=text, ids_col=ids_col, ids_row=ids_row)
+    outer = dict(frames=frames, norms=norms, incoming=incoming, **weights)
+    return run_kernel(forward_kernel, 1, inner, outer, out, vmem, sems, {})
+
+
+class Reduce:
+    def __init__(self, spot, grad, over, along, sems, spread, source=None):
+        self.spot, self.grad, self.over, self.along = spot, grad, over, along
+        self.ysend, self.yrecv, self.zsend, self.zrecv = sems
+        self.spread = spread
+        self.source = grad if source is None else source
+        self.size, self.cols = over.shape[-2], over.shape[-1]
+
+    def rows(self, z, flip=0, ref=None):
+        spot = self.spot
+        row = z * 2 + (1 - spot.y if flip else spot.y)
+        return (self.grad if ref is None else ref).at[pl.ds(pl.multiple_of(row * self.size, self.size), self.size)]
+
+    def add(self, target, extra):
+        step = 16
+
+        @pl.loop(0, self.size // step)
+        def _(index):
+            here = pl.ds(pl.multiple_of(index * step, step), step)
+            target[here, :] = (target[here, :].astype(F32) + extra[here, :].astype(F32)).astype(BF16)
+
+    def y_copy(self, z):
+        return push(
+            self.rows(z, 1, self.source), self.over.at[z], self.ysend.at[z], self.yrecv.at[z], self.spot.part
+        )
+
+    def y_start(self):
+        for z in (0, 3, 1, 2):
+            self.y_copy(z).start()
+
+    def z_copy(self, goal, slot, who, flip):
+        index = flip * 4 + slot
+        return push(
+            self.rows(goal, flip), self.along.at[index], self.zsend.at[flip * 4 + goal],
+            self.zrecv.at[index], (who * 2 + self.spot.y, self.spot.blk),
+        )
+
+    def z_first(self, goal, flip):
+        z = self.spot.z
+        middle, end = (2, 3) if goal == 0 else (1, 0)
+        for home in range(4):
+            if home == goal or (goal in (0, 3) and home == middle):
+                continue
+
+            @pl.when(z == home)
+            def _():
+                if goal in (0, 3) and home == end:
+                    self.z_copy(goal, 3, middle, flip).start()
+                else:
+                    self.z_copy(goal, home - (home > goal), goal, flip).start()
+
+    def z_second(self, goal, flip):
+        middle = 2 if goal == 0 else 1
+
+        @pl.when(self.spot.z == middle)
+        def _():
+            index = flip * 4 + 3
+            self.z_copy(goal, 3, goal, flip).wait_recv()
+            self.add(self.rows(goal, flip), self.along.at[index])
+            self.z_copy(goal, middle - (middle > goal), goal, flip).start()
+
+    def take(self, goal):
+        self.y_copy(goal).wait_recv()
+        self.add(self.rows(goal), self.over.at[goal])
+        self.z_first(goal, 0)
+
+    def start(self):
+        if not self.spread:
+            return self.y_start()
+        for goal in (0, 3, 1, 2):
+            for flip in (1, 0):
+                self.z_first(goal, flip)
+
+    def combine(self, flip=0):
+        self.z_second(0, flip)
+        self.z_second(3, flip)
+
+    def arrive(self, flip):
+        z = self.spot.z
+        for slot in range(3):
+            unused = 3 if slot == 2 else 0 if slot == 0 else None
+
+            def wait():
+                self.z_copy(0, slot, 0, flip).wait_recv()
+
+            if slot == 1:
+                wait()
+            else:
+                pl.when(z != (0 if slot == 2 else 3))(wait)
+
+    def total(self, flip, extra, body):
+        z = self.spot.z
+        own = self.rows(z, flip)
+
+        def add_up(slots):
+            @pl.loop(0, self.size // 16)
+            def _(index):
+                here = pl.ds(pl.multiple_of(index * 16, 16), 16)
+                value = own[here, :].astype(F32)
+                for slot in slots:
+                    value += self.along[flip * 4 + slot, here, :].astype(F32)
+                if extra is not None:
+                    value += extra[here, :].astype(F32)
+                body(here, value)
+
+        @pl.when(z == 0)
+        def _():
+            add_up((0, 1))
+
+        @pl.when(z == 3)
+        def _():
+            add_up((1, 2))
+
+        @pl.when((z == 1) | (z == 2))
+        def _():
+            add_up((0, 1, 2))
+
+    def cross(self):
+        self.arrive(1)
+        target = self.rows(self.spot.z, 1)
+
+        def keep(here, value):
+            target[here, :] = value.astype(BF16)
+
+        self.total(1, None, keep)
+        push(target, self.over.at[0], self.ysend.at[0], self.yrecv.at[0], self.spot.part).start()
+
+    def finish(self, body):
+        self.arrive(0)
+        if self.spread:
+            target = self.rows(self.spot.z, 1)
+            push(target, self.over.at[0], self.ysend.at[0], self.yrecv.at[0], self.spot.part).wait_recv()
+            self.total(0, self.over.at[0], body)
+        else:
+            self.total(0, None, body)
+
+    def drain(self):
+        z = self.spot.z
+        if self.spread:
+            target = self.rows(z, 1)
+            push(target, self.over.at[0], self.ysend.at[0], self.yrecv.at[0], self.spot.part).wait_send()
+        else:
+            for goal in range(4):
+                self.y_copy(goal).wait_send()
+        for flip in (0, 1) if self.spread else (0,):
+            for goal in range(4):
+
+                @pl.when(z != goal)
+                def _():
+                    self.z_copy(goal, 0, 0, flip).wait_send()
+
+
+class BlkSum:
+    def __init__(self, spot, piece, near, far, send, recv, step, size):
+        self.spot, self.piece, self.near, self.far = spot, piece, near, far
+        self.send, self.recv, self.step, self.size = send, recv, step, size
+
+    def to_core(self, x):
+        spot = self.spot
+        goal = x * 2 + 1 - spot.core
+        return push(self.piece(goal), self.near.at[x], self.send.at[x], self.recv.at[x], spot.sib)
+
+    def to_chip(self):
+        spot = self.spot
+        return push(self.piece(spot.opp_blk), self.far, self.send.at[2], self.recv.at[2], spot.opp)
+
+    def start(self):
+        self.to_core(0).start()
+        self.to_core(1).start()
+
+    def relay(self):
+        spot = self.spot
+        for x in (0, 1):
+            self.to_core(x).wait_recv()
+        target, extra = self.piece(spot.opp_blk), self.near.at[1 - spot.x]
+
+        @pl.loop(0, self.size // self.step)
+        def _(index):
+            here = pl.ds(pl.multiple_of(index * self.step, self.step), self.step)
+            target[here, :] = (target[here, :].astype(F32) + extra[here, :].astype(F32)).astype(BF16)
+
+        self.to_chip().start()
+
+    def finish(self):
+        self.to_chip().wait_recv()
+
+    def value(self, here):
+        spot = self.spot
+        own = self.piece(spot.blk)[here, :].astype(F32)
+        return own + self.near[spot.x, here, :].astype(F32) + self.far[here, :].astype(F32)
+
+    def drain(self):
+        self.to_core(0).wait_send()
+        self.to_core(1).wait_send()
+        self.to_chip().wait_send()
+
+
+class Turn:
+    def __init__(self, spot, source, target, send, recv):
+        self.spot, self.source, self.target, self.send, self.recv = spot, source, target, send, recv
+        self.rows, self.wide = source.shape[0], target.shape[1]
+
+    def copy(self, number):
+        spot = self.spot
+        goal = (spot.sib_blk, spot.opp_blk, spot.far_blk)[number]
+        src = self.source.at[:, pl.ds(pl.multiple_of(goal * self.wide, 128), self.wide)]
+        return push(src, self.place(spot.blk), self.send.at[number], self.recv.at[number], (spot.grp, goal))
+
+    def place(self, index):
+        return self.target.at[pl.ds(pl.multiple_of(index * self.rows, self.rows), self.rows)]
+
+    def start(self):
+        for number in (2, 1, 0):
+            self.copy(number).start()
+        spot = self.spot
+        src = self.source.at[:, pl.ds(pl.multiple_of(spot.blk * self.wide, 128), self.wide)]
+        self.place(spot.blk)[...] = src[...]
+
+    def finish(self):
+        for number in range(3):
+            self.copy(number).wait_recv()
+
+    def drain(self):
+        for number in range(3):
+            self.copy(number).wait_send()
+
+
+def t_dot(left, right):
+    return lax.dot_general(left, right, (((0,), (0,)), ((), ())), preferred_element_type=F32)
+
+
+def backward_kernel(names, *refs):
+    r = named(names, refs)
+    spot = Spot()
+    rows, width = r.frames.shape
+    length = r.v_grad.shape[0]
+    wide = r.v_query_grad.shape[1]
+    blk = spot.blk
+    spot.greet_all()
+
+    def lanes(index, size):
+        return pl.ds(pl.multiple_of(index * size, 128), size)
+
+    def part(ref, first, size):
+        return ref.at[:, first : first + size]
+
+    def row_piece(ref, size):
+        return lambda index: ref.at[pl.ds(pl.multiple_of(index * size, size), size)]
+
+    loads = []
+
+    def load(src, dst):
+        copy = pltpu.make_async_copy(src, dst, r.local.at[len(loads)])
+        copy.start()
+        loads.append(copy)
+        return copy
+
+    grads = Bag(
+        contract=r.g_contract,
+        expand=r.g_expand,
+        back=part(r.g_rest, 0, wide),
+        keys=part(r.g_rest, wide, 2 * wide),
+        query=part(r.g_rest, 3 * wide, wide),
+        outward=part(r.g_rest, 4 * wide, wide),
+        inward=part(r.g_contract, 0, 3 * wide),
+    )
+
+    def reduce(number, grad, over, along, spread=False, source=None):
+        sems = tuple(item.at[number] for item in (r.ysend, r.yrecv, r.zsend, r.zrecv))
+        return Reduce(spot, grad, over, along, sems, spread, source)
+
+    reduces = Bag(
+        contract=reduce(0, grads.contract, r.y_contract, r.z_contract, False, r.contract_grad),
+        expand=reduce(1, grads.expand, r.y_expand, r.z_expand),
+        back=reduce(2, grads.back, r.y_back, r.z_back, True),
+        keys=reduce(3, grads.keys, r.y_keys, r.z_keys, True),
+        query=reduce(4, grads.query, r.y_query, r.z_query),
+        outward=reduce(5, grads.outward, r.y_outward, r.z_outward),
+        inward=reduce(
+            6,
+            grads.inward,
+            r.y_contract.at[:, :, 0 : 3 * wide],
+            r.z_contract.at[:, :, 0 : 3 * wide],
+        ),
+    )
+    reduces.contract.start()
+    load_grad = load(r.grad_all, r.v_grad)
+    load_contract = load(r.w_contract, r.v_one)
+    load_slope = load(r.slope, r.v_slope)
+    load_third = load(r.third_t, r.v_left)
+    load_expand = load(r.w_expand, r.v_two)
+    load_own = load(r.contract_grad, r.g_contract)
+    load_norm = load(r.norm_all.at[0:8], r.v_norm)
+    load_crossed = load(r.crossed_t, r.v_right)
+    load_two = load(r.two_rows, r.v_two_rows)
+    load_incoming = load(r.incoming, r.v_rows)
+    cross_query = part(r.v_joint, 0, wide)
+    load_query = load(r.cross_query, cross_query)
+    load_text = load(r.text_all.at[:, lanes(blk, wide)], part(r.v_text, 0, wide))
+    load_values = load(r.text_all.at[:, lanes(blk + 4, wide)], part(r.v_text, wide, wide))
+
+    def blk_sum(number, piece, near, far, size):
+        return BlkSum(spot, piece, near, far, r.bsend.at[number], r.brecv.at[number], 16, size)
+
+    load_grad.wait()
+    load_contract.wait()
+    load_slope.wait()
+
+    def up_tile(block):
+        r.v_up[:, block] = (dot(r.v_grad[...], r.v_one[:, block]) * r.v_slope[:, block]).astype(BF16)
+
+    tiles(4, 384, up_tile)
+    load_back = load(r.w_back, part(r.v_one, 0, wide))
+    load_keys = load(r.w_keys, part(r.v_one, wide, 2 * wide))
+    load_outward = load(r.w_outward, part(r.v_one, 3 * wide, wide))
+    load_expand.wait()
+
+    def back_rows(left, right):
+        def body(block):
+            r.v_part[:, block] = dot_t(left[...], right[block, :]).astype(BF16)
+
+        tiles(4, 384, body)
+
+    def back_cols(left, right):
+        for core in (1 - spot.core, spot.core):
+            for x in (0, 1):
+                goal = x * 2 + core
+                here = pl.ds(pl.multiple_of(goal * wide, 128), wide)
+                mine = pl.ds(pl.multiple_of(goal * wide, wide), wide)
+                r.v_part[:, here] = dot_t(left[...], right[mine, :]).astype(BF16)
+
+    def outer(target, left, right):
+        def body(block):
+            target[block, :] = dot(left[block, :], right[...]).astype(BF16)
+
+        tiles(4, 384, body)
+
+    row_parts = row_piece(r.v_part, rows)
+
+    def col_parts(index):
+        return r.v_part.at[:, lanes(index, wide)]
+
+    back_rows(r.v_up, r.v_two)
+    third_sum = blk_sum(0, row_parts, r.near_rows, r.far_rows, rows)
+    third_sum.start()
+    load_third.wait()
+
+    def expand_tile(block):
+        r.g_expand[:, block] = dot(r.v_left[...], r.v_up[:, block]).astype(BF16)
+
+    third_sum.relay()
+    tiles(4, 384, expand_tile)
+    reduces.expand.start()
+    load_wquery = load(r.w_query, part(r.v_two, 0, wide))
+    load_winward = load(r.w_inward, part(r.v_two, wide, 3 * wide))
+    load_second = load(r.second_t, r.v_left)
+    load_own.wait()
+    reduces.contract.take(0)
+    for copy in (load_norm, load_two, load_incoming):
+        copy.wait()
+    r.v_norm_grads[...] = jnp.zeros_like(r.v_norm_grads)
+    hidden = r.v_slope.at[pl.ds(3 * rows, rows)]
+
+    def norm_back(total, values, number, base, keep):
+        gain = r.v_norm[number : number + 1, :]
+
+        @pl.loop(0, rows // 16)
+        def _(index):
+            here = pl.ds(pl.multiple_of(index * 16, 16), 16)
+            incoming = total.value(here)
+            value = values[here, :].astype(F32)
+            center = value - jnp.mean(value, axis=1, keepdims=True)
+            scale = lax.rsqrt(jnp.mean(center * center, axis=1, keepdims=True) + 1e-05)
+            normal = center * scale
+            scaled = incoming * gain
+            mean = jnp.mean(scaled, axis=1, keepdims=True)
+            match = jnp.mean(scaled * normal, axis=1, keepdims=True)
+            keep(here, base(here) + (scaled - mean - normal * match) * scale)
+            for place, term in ((number, incoming * normal), (3 + number, incoming)):
+                spread = pl.ds(place * 8, 8)
+                r.v_norm_grads[spread, :] += term[0:8, :] + term[8:16, :]
+
+    def keep_branch(here, value):
+        hidden[here, :] = value
+        r.v_branch[here, :] = value.astype(BF16)
+
+    third_sum.finish()
+    norm_back(
+        third_sum, r.v_two_rows, 2, lambda here: r.v_rows[here, :].astype(F32), keep_branch
+    )
+    load_one = load(r.one_rows, r.v_rows)
+    turn_two = Turn(spot, r.v_branch, r.v_turn_two, r.tsend.at[0], r.trecv.at[0])
+    turn_two.start()
+    reduces.contract.take(3)
+    load_back.wait()
+    turn_two.finish()
+    third_sum.drain()
+    back_cols(r.v_turn_two, part(r.v_one, 0, wide))
+    crossed_sum = blk_sum(1, col_parts, r.near_cols, r.far_cols, length)
+    crossed_sum.start()
+    load_crossed.wait()
+    crossed_sum.relay()
+    outer(grads.back, r.v_right, r.v_turn_two)
+    reduces.back.start()
+    load_attended = load(r.attended_t, r.v_right)
+    reduces.contract.take(1)
+    crossed_sum.finish()
+    load_query.wait()
+    load_text.wait()
+    load_values.wait()
+
+    def merge(total, target):
+        @pl.loop(0, length // 16)
+        def _(index):
+            here = pl.ds(pl.multiple_of(index * 16, 16), 16)
+            target[here, :] = total.value(here).astype(BF16)
+
+    merge(crossed_sum, r.v_head_grad)
+    low = lax.broadcasted_iota(jnp.int32, (1, 128), 1) < 64
+
+    def half(value, side):
+        return jnp.where(low if side == 0 else jnp.logical_not(low), value, jnp.zeros_like(value))
+
+    def soft(scores):
+        power = jnp.exp(scores - jnp.max(scores, axis=1, keepdims=True))
+        return power * (1.0 / jnp.sum(power, axis=1, keepdims=True))
+
+    @pl.loop(0, 3)
+    def _(pair):
+        query = cross_query[:, lanes(pair, 128)]
+        key = r.v_text[:, lanes(pair, 128)]
+        value = r.v_text[:, lanes(3 + pair, 128)]
+        head_grad = r.v_head_grad[:, lanes(pair, 128)]
+        results = []
+        for side in (0, 1):
+            weights = soft(dot_t(half(query, side), key) * 0.125)
+            slope = dot_t(half(head_grad, side), value)
+            score = (weights * (slope - jnp.sum(slope * weights, axis=1, keepdims=True))).astype(BF16)
+            results.append(
+                (
+                    dot(score, key) * 0.125,
+                    t_dot(score, query) * 0.125,
+                    t_dot(weights.astype(BF16), head_grad),
+                )
+            )
+        merged = [jnp.where(low, *item).astype(BF16) for item in zip(*results)]
+        r.v_query_grad[:, lanes(pair, 128)] = merged[0]
+        r.v_terms[0:TEXT, lanes(blk * 3 + pair, 128)] = merged[1]
+        r.v_terms[TEXT : 2 * TEXT, lanes(blk * 3 + pair, 128)] = merged[2]
+
+    load_joint = load(r.joint, r.v_joint)
+    own_terms = r.v_terms.at[:, lanes(blk, wide)]
+    terms_share = Share(
+        spot, own_terms, lambda index: r.v_terms.at[:, lanes(index, wide)], r.csend.at[0], r.crecv.at[0]
+    )
+    terms_share.start()
+    load_wquery.wait()
+    crossed_sum.drain()
+    back_rows(r.v_query_grad, part(r.v_two, 0, wide))
+    second_sum = blk_sum(2, row_parts, r.near_rows, r.far_rows, rows)
+    second_sum.start()
+    load_second.wait()
+    second_sum.relay()
+    outer(grads.query, r.v_left, r.v_query_grad)
+    load_first = load(r.first_t, r.v_left)
+    reduces.query.start()
+    reduces.back.combine(1)
+    reduces.back.combine(0)
+    reduces.contract.combine()
+    reduces.contract.take(2)
+    pl.semaphore_signal(r.credit.at[0], inc=1, device_id=spot.part, device_id_type=MESH)
+    terms_share.relay()
+    load_one.wait()
+    second_sum.finish()
+    norm_back(second_sum, r.v_rows, 1, lambda here: hidden[here, :], keep_branch_after(turn_two, keep_branch))
+    load_frames = load(r.frames, r.v_rows)
+    turn_one = Turn(spot, r.v_branch, r.v_turn_one, r.tsend.at[1], r.trecv.at[1])
+    turn_one.start()
+    terms_share.finish()
+    load_keys.wait()
+    own_rows = pl.ds(pl.multiple_of((blk // 2) * TEXT, TEXT), TEXT)
+    terms = r.v_terms[own_rows, lanes(lax.rem(blk, 2), 2 * wide)]
+
+    def keys_tile(block):
+        product = t_dot(r.text[:, block], r.v_terms[own_rows, lanes(lax.rem(blk, 2), 2 * wide)])
+        grads.keys[block, :] = product.astype(BF16)
+
+    tiles(6, 256, keys_tile)
+    reduces.keys.start()
+    turn_one.finish()
+    second_sum.drain()
+    load_outward.wait()
+    back_cols(r.v_turn_one, part(r.v_one, 3 * wide, wide))
+    attended_sum = blk_sum(3, col_parts, r.near_cols, r.far_cols, length)
+    attended_sum.start()
+    load_attended.wait()
+    attended_sum.relay()
+    outer(grads.outward, r.v_right, r.v_turn_one)
+    reduces.outward.start()
+    r.v_text_part[...] = dot_t(terms, r.v_one[:, wide : 3 * wide]).astype(BF16)
+    text_rows = TEXT // 4
+    text_sum = blk_sum(4, row_piece(r.v_text_part, text_rows), r.near_text, r.far_text, text_rows)
+    text_sum.start()
+    text_sum.relay()
+    reduces.expand.take(0)
+    load_joint.wait()
+    attended_sum.finish()
+    merge(attended_sum, r.v_head_grad)
+
+    @pl.loop(0, 3)
+    def _(pair):
+        r.v_key_sum[...] = jnp.zeros_like(r.v_key_sum)
+        r.v_value_sum[...] = jnp.zeros_like(r.v_value_sum)
+
+        @pl.loop(0, 4)
+        def _(block):
+            here = pl.ds(pl.multiple_of(block * 128, 128), 128)
+            query = r.v_joint[here, lanes(pair, 128)]
+            key = r.v_joint[:, lanes(pair + 3, 128)]
+            value = r.v_joint[:, lanes(pair + 6, 128)]
+            head_grad = r.v_head_grad[here, lanes(pair, 128)]
+            keep = r.ids_row[...] <= r.ids_col[here, :]
+            results = []
+            for side in (0, 1):
+                weights = soft(jnp.where(keep, dot_t(half(query, side), key) * 0.125, -1e30))
+                slope = dot_t(half(head_grad, side), value)
+                score = (weights * (slope - jnp.sum(slope * weights, axis=1, keepdims=True))).astype(BF16)
+                results.append(
+                    (dot(score, key), t_dot(score, query), t_dot(weights.astype(BF16), head_grad))
+                )
+            merged = [jnp.where(low, *item) for item in zip(*results)]
+            r.v_up[here, lanes(pair, 128)] = (merged[0] * 0.125).astype(BF16)
+            r.v_key_sum[...] += merged[1]
+            r.v_value_sum[...] += merged[2]
+
+        r.v_up[:, lanes(pair + 3, 128)] = (r.v_key_sum[...] * 0.125).astype(BF16)
+        r.v_up[:, lanes(pair + 6, 128)] = r.v_value_sum[...].astype(BF16)
+
+    stores = []
+
+    def store(item, goal):
+        size = goal.shape[1]
+        slot = len(stores) % 2
+        if len(stores) >= 2:
+            stores[-2].wait()
+        stage = r.v_slope.at[pl.ds(slot * 192, 192), pl.ds(0, size)]
+
+        def keep(here, value):
+            stage[here, :] = value
+
+        item.finish(keep)
+        copy = pltpu.make_async_copy(stage, goal, r.stored.at[len(stores)])
+        copy.start()
+        stores.append(copy)
+
+    reduces.back.cross()
+    reduces.keys.combine(1)
+    reduces.keys.combine(0)
+    store(reduces.contract, r.contract_out)
+    for k in (1, 2, 3):
+        pl.semaphore_signal(r.credit.at[1], inc=1, device_id=spot.z_peer(k), device_id_type=MESH)
+    reduces.contract.drain()
+    attended_sum.drain()
+    load_winward.wait()
+    load_first.wait()
+    joint_grad = part(r.v_up, 0, 3 * wide)
+    back_rows(joint_grad, part(r.v_two, wide, 3 * wide))
+    first_sum = blk_sum(5, row_parts, r.near_rows, r.far_rows, rows)
+    first_sum.start()
+
+    def inward_tile(block):
+        grads.inward[:, block] = dot(r.v_left[...], r.v_up[:, block]).astype(BF16)
+
+    tiles(3, 384, inward_tile)
+    pl.semaphore_wait(r.credit.at[0], 1)
+    reduces.inward.start()
+    first_sum.relay()
+    load_again = load(r.w_contract, r.v_one)
+    load_active = load(r.active, r.v_grad)
+    reduces.expand.take(3)
+    reduces.expand.take(1)
+    reduces.expand.combine()
+    reduces.expand.take(2)
+    load_frames.wait()
+    first_sum.finish()
+
+    def keep_frames(here, value):
+        hidden[here, :] = value
+
+    norm_back(first_sum, r.v_rows, 0, lambda here: hidden[here, :], keep_frames)
+    for who in (spot.sib, spot.opp):
+        pl.semaphore_signal(r.credit.at[2], inc=1, device_id=who, device_id_type=MESH)
+    frames_copy = pltpu.make_async_copy(hidden, r.frames_out, r.stored.at[8])
+    frames_copy.start()
+
+    for place in range(6):
+        r.v_norm_sum[place : place + 1, :] = jnp.sum(
+            r.v_norm_grads[place * 8 : place * 8 + 8, :], axis=0, keepdims=True
+        )
+    r.v_norm_sum[6:8, :] = jnp.zeros((2, width), F32)
+
+    def norm_hop(number, who):
+        return push(r.v_norm_sum, r.v_norm_in.at[number], r.nsend.at[number], r.nrecv.at[number], who)
+
+    norm_hop(0, spot.sib).start()
+    text_sum.finish()
+    r.v_text_out[...] = text_sum.value(pl.ds(0, text_rows))
+    text_copy = pltpu.make_async_copy(r.v_text_out, r.text_out, r.stored.at[9])
+    text_copy.start()
+    reduces.query.take(0)
+    reduces.query.take(3)
+    reduces.query.take(1)
+    reduces.query.take(2)
+
+    def norm_step(number, who):
+        norm_hop(number, who).wait()
+        r.v_norm_sum[...] += r.v_norm_in[number]
+
+    norm_step(0, spot.sib)
+    norm_hop(1, spot.opp).start()
+    load_again.wait()
+    load_active.wait()
+    first_sum.drain()
+    back_rows(r.v_grad, r.v_one)
+    out_sum = blk_sum(6, row_parts, r.near_rows, r.far_rows, rows)
+    pl.semaphore_wait(r.credit.at[2], 2)
+    out_sum.start()
+    norm_step(1, spot.opp)
+    norm_hop(2, spot.part).start()
+    reduces.query.combine()
+    for goal in (0, 3, 1, 2):
+        reduces.outward.take(goal)
+    out_sum.relay()
+    reduces.keys.cross()
+    norm_step(2, spot.part)
+    for k in (1, 2, 3):
+        norm_hop(2 + k, spot.z_peer(k)).start()
+    reduces.outward.combine()
+    pl.semaphore_wait(r.credit.at[1], 3)
+    for goal in (0, 3):
+        reduces.inward.take(goal)
+    out_sum.finish()
+    turn_one.drain()
+
+    @pl.loop(0, rows // 16)
+    def _(index):
+        here = pl.ds(pl.multiple_of(index * 16, 16), 16)
+        r.v_branch[here, :] = (out_sum.value(here) + r.v_two_rows[here, :].astype(F32)).astype(BF16)
+
+    block_copy = pltpu.make_async_copy(r.v_branch, r.block_out, r.stored.at[10])
+    block_copy.start()
+    store(reduces.expand, r.expand_out)
+    store(reduces.back, r.returning_out)
+    reduces.inward.take(1)
+    reduces.inward.take(2)
+    reduces.inward.combine()
+    store(reduces.query, r.querying_out)
+    store(reduces.outward, r.outward_out)
+    store(reduces.keys, r.keying_out)
+    for k in (1, 2, 3):
+        norm_hop(2 + k, spot.z_peer(k)).wait()
+    r.v_norm_sum[...] += r.v_norm_in[3] + r.v_norm_in[4] + r.v_norm_in[5]
+    norm_copy = pltpu.make_async_copy(r.v_norm_sum, r.norm_out, r.stored.at[11])
+    norm_copy.start()
+
+    out_sum.drain()
+    inward_sum = r.v_part.at[pl.ds(0, 192), pl.ds(0, 3 * wide)]
+
+    def keep_inward(here, value):
+        inward_sum[here, :] = value.astype(BF16)
+
+    reduces.inward.finish(keep_inward)
+
+    def inward_copy(kind):
+        index = kind * 4 + blk
+        owner, place = index // 3, lax.rem(index, 3)
+        src = inward_sum.at[:, kind * wide : (kind + 1) * wide]
+        return owner, place, src, r.v_inward_in.at[:, lanes(place, wide)]
+
+    for kind in range(3):
+        owner, place, src, dst = inward_copy(kind)
+
+        @pl.when(owner == blk)
+        def _():
+            pltpu.make_async_copy(src, dst, r.arecv.at[place]).start()
+
+        @pl.when(owner != blk)
+        def _():
+            push(src, dst, r.asend.at[kind], r.arecv.at[place], (spot.grp, owner)).start()
+
+    for place in range(3):
+        dst = r.v_inward_in.at[:, place * wide : (place + 1) * wide]
+        home = lax.rem(blk * 3 + place, 4)
+
+        @pl.when(home == blk)
+        def _():
+            pltpu.make_async_copy(dst, dst, r.arecv.at[place]).wait()
+
+        @pl.when(home != blk)
+        def _():
+            push(dst, dst, r.asend.at[0], r.arecv.at[place], spot.sib).wait_recv()
+
+    for copy in stores[-2:]:
+        copy.wait()
+    final = r.v_slope.at[pl.ds(0, 192), pl.ds(0, 3 * wide)]
+
+    @pl.loop(0, 192 // 16)
+    def _(index):
+        here = pl.ds(pl.multiple_of(index * 16, 16), 16)
+        final[here, :] = r.v_inward_in[here, :].astype(F32)
+
+    inward_done = pltpu.make_async_copy(final, r.inward_out, r.stored.at[12])
+    inward_done.start()
+    for kind in range(3):
+        owner, place, src, dst = inward_copy(kind)
+
+        @pl.when(owner != blk)
+        def _():
+            push(src, dst, r.asend.at[kind], r.arecv.at[place], (spot.grp, owner)).wait_send()
+
+    for item in vars(reduces).values():
+        if item is not reduces.contract:
+            item.drain()
+    terms_share.drain()
+    text_sum.drain()
+    for copy in (frames_copy, text_copy, block_copy, norm_copy, inward_done):
+        copy.wait()
+
+
+def keep_branch_after(turn, keep):
+    turn.drain()
+    return keep
+
+
+def backward(ahead, frames, text, table, incoming):
+    rows, width = frames.shape
+    length = rows * lax.axis_size("blk")
+    wide = width // lax.axis_size("blk")
+    shard = width // lax.axis_size("grp")
+    feed = ahead.w_expand.shape[1]
+    ids_col, ids_row = ids_of(table)
+    out = dict(
+        contract_out=((shard, feed), F32),
+        expand_out=((shard, feed), F32),
+        returning_out=((shard, wide), F32),
+        keying_out=((shard, 2 * wide), F32),
+        querying_out=((shard, wide), F32),
+        outward_out=((shard, wide), F32),
+        inward_out=((shard, 3 * wide), F32),
+        frames_out=((rows, width), F32),
+        block_out=((rows, width), BF16),
+        text_out=((TEXT // 4, width), F32),
+        norm_out=((8, width), F32),
+    )
+    square, turned, strip = (length, width), (width, length), (length, wide)
+    vmem = dict(
+        v_one=((width, feed), BF16),
+        v_two=((width, feed), BF16),
+        g_contract=((width, feed), BF16),
+        g_expand=((width, feed), BF16),
+        g_rest=((width, 5 * wide), BF16),
+        v_left=(turned, BF16),
+        v_right=(turned, BF16),
+        v_grad=(square, BF16),
+        v_up=(square, BF16),
+        v_part=(square, BF16),
+        v_slope=(square, F32),
+        v_joint=((length, 3 * wide), BF16),
+        v_query_grad=(strip, BF16),
+        v_head_grad=(strip, BF16),
+        v_turn_one=(strip, BF16),
+        v_turn_two=(strip, BF16),
+        v_text=((TEXT, 2 * wide), BF16),
+        v_terms=((2 * TEXT, width), BF16),
+        v_text_part=((TEXT, width), BF16),
+        v_text_out=((TEXT // 4, width), F32),
+        near_rows=((2, rows, width), BF16),
+        far_rows=((rows, width), BF16),
+        near_cols=((2, length, wide), BF16),
+        far_cols=(strip, BF16),
+        near_text=((2, TEXT // 4, width), BF16),
+        far_text=((TEXT // 4, width), BF16),
+        v_branch=((rows, width), BF16),
+        v_rows=((rows, width), BF16),
+        v_two_rows=((rows, width), BF16),
+        v_norm=((8, width), F32),
+        v_norm_grads=((48, width), F32),
+        v_norm_sum=((8, width), F32),
+        v_norm_in=((6, 8, width), F32),
+        v_key_sum=((length, 128), F32),
+        v_value_sum=((length, 128), F32),
+        v_inward_in=((shard, 3 * wide), BF16),
+    )
+    vmem.update(
+        y_contract=((4, shard, feed), BF16),
+        y_expand=((4, shard, feed), BF16),
+        y_back=((1, shard, wide), BF16),
+        y_keys=((1, shard, 2 * wide), BF16),
+        y_query=((4, shard, wide), BF16),
+        y_outward=((4, shard, wide), BF16),
+        z_contract=((4, shard, feed), BF16),
+        z_expand=((4, shard, feed), BF16),
+        z_back=((8, shard, wide), BF16),
+        z_keys=((8, shard, 2 * wide), BF16),
+        z_query=((4, shard, wide), BF16),
+        z_outward=((4, shard, wide), BF16),
+    )
+    sems = dict(
+        ysend=(7, 4),
+        yrecv=(7, 4),
+        zsend=(7, 8),
+        zrecv=(7, 8),
+        bsend=(7, 3),
+        brecv=(7, 3),
+        tsend=(2, 3),
+        trecv=(2, 3),
+        csend=(1, 3),
+        crecv=(1, 3),
+        nsend=(6,),
+        nrecv=(6,),
+        asend=(3,),
+        arecv=(3,),
+        local=(32,),
+        stored=(16,),
+    )
+    inner = dict(text=text, ids_col=ids_col, ids_row=ids_row)
+    outer = dict(frames=frames, incoming=incoming, **vars(ahead))
+    del outer["aligned"]
+    return run_kernel(backward_kernel, 2, inner, outer, out, vmem, sems, dict(credit=(3,)))
+
+
+def tp_shards(
+    frames,
+    text_states,
+    block_table,
+    inward,
+    outward,
+    querying,
+    keying,
+    returning,
+    expand,
+    contract,
+    gains,
+    shifts,
+    out_grad,
+):
+    ahead = forward(
+        frames[0],
+        text_states[0],
+        block_table,
+        jnp.pad(jnp.concatenate([gains, shifts], axis=0), ((0, 10), (0, 80))),
+        out_grad[0],
+        dict(
+            inward=inward,
+            outward=outward,
+            query=querying,
+            keys=keying,
+            back=returning,
+            expand=expand,
+            contract=contract.T,
+        ),
+    )
+    done = backward(ahead, frames[0], text_states[0], block_table, out_grad[0])
+    share = gains.shape[1]
+    place = (lax.axis_index("grp") * lax.axis_size("blk") + lax.axis_index("blk")) * share
+    norm_grads = lax.dynamic_slice_in_dim(done.norm_out, place, share, 1)
+    return (
+        done.block_out[None],
+        done.frames_out[None],
+        done.text_out[None],
+        done.inward_out,
+        done.outward_out,
+        done.querying_out,
+        done.keying_out,
+        done.returning_out,
+        done.expand_out,
+        done.contract_out.T,
+        norm_grads[:3],
+        norm_grads[3:6],
+    )
+
+
 def solution(mesh):
+    small = mesh.shape["grp"] == 8 and mesh.shape["blk"] == 4
     return jax.shard_map(
-        shards,
+        tp_shards if small else shards,
         mesh=mesh,
         in_specs=(
             P("grp", "blk", None),

time: 2930 us -> 485 us (0.17)
  waiting for transfers between devices: 2510 us -> 0 us
  Pallas kernels: 0 us -> 461 us
  matrix products: 179 us -> 0 us
  blocking collectives: 92.8 us -> 0 us
  local copies, waits for them, and re-layouts: 97.7 us -> 13.4 us
    all_gather x12 -> x0, waiting for transfers between devices: 1280 us -> none  [the longest x1 359 us: gather_weights(): lax.all_gather(expand, 'grp', axis=0, tiled=True)]
    reduce_scatter x9 -> x0, waiting for transfers between devices: 792 us -> none  [the longest x1 136 us: shards(): lax.psum_scatter(contract_grad.astype(jnp.bfloat16), 'blk', scatter_dimen...]
    pallas_call x0 -> x2, Pallas kernels: none -> 461 us  [run_kernel(): pl.pallas_call(functools.partial(kernel, names), out_shape=[jax.ShapeDtyp...]
    unnamed x43 -> x0, waiting for transfers between devices: 438 us -> none
    dot_general x32 -> x0, matrix products: 178 us -> none  [the longest x1 16.5 us: shards(): jnp.dot(activated, full_contract, preferred_element_type=jnp.float32)]
    all_gather x7 -> x0, blocking collectives: 92.8 us -> none  [the longest x1 26.6 us: gather_weights(): lax.all_gather(gains, 'grp', axis=1, tiled=True)]
    unnamed x110 -> x26, local copies, waits for them, and re-layouts: 82.4 us -> 10.4 us
  transfers between devices with their start and end apart: 32 -> 0, of which waited for: 28 -> 0; matrix products, arithmetic and copies ran while one was open for 8% -> 0% of each run, Pallas kernels for 0% -> 0%
where the time goes in v2:
time: 485 us; the launch traced here: 477 us
  Pallas kernels  461 us (95%)
  local copies, waits for them, and re-layouts  13.4 us (3%)
    pallas_call x2, Pallas kernels, run_kernel(): pl.pallas_call(functools.partial(kernel, names), out_shape=[jax.ShapeDtyp...  461 us
    unnamed x26, local copies, waits for them, and re-layouts  10.4 us

profile of v2, /device:TPU:0, one launch (start us, length us, event | category | flops | bytes accessed | tf_op | source)
XLA Modules:
  0.0 477.0 jit_solution(17281749099528280655)
XLA Ops:
  0.6 0.7 multiply_bitcast_fusion
  1.3 0.1 iota_add_fusion
  1.4 0.9 add.55.refs_1_
  2.3 0.7 add.52.refs_2_
  2.9 1.3 fusion.5.refs_4_
  4.2 228.5 %shard_map.220 = (bf16[1536,384]{1,0:T(8,128)(2,1)}, bf16[1536,1152]{1,0:T(8,128)(2,1)}, bf16[1536,384]{1,0:T(8,128)(2,1)}, bf16[1536,768]{1,0:T(8,128)(2,1)}, b...) custom-call(bf16[64,1536]{1,0:T(8,128)(2,1)} %bitcast.15, ...), custom_call_target="tpu_custom_call" | custom-call | tf_op jit(solution)/shard_map/pallas_call | solution.py:947
  232.7 232.4 %shard_map.221 = (f32[192,1536]{1,0:T(8,128)}, f32[192,1536]{1,0:T(8,128)}, f32[192,384]{1,0:T(8,128)}, f32[192,768]{1,0:T(8,128)}, f32[192,384]{1,0:T(8,128)}, ...) custom-call(bf16[64,1536]{1,0:T(8,128)(2,1)} %bitcast.16, ...), custom_call_target="tpu_custom_call" | custom-call | tf_op jit(solution)/shard_map/pallas_call | solution.py:947
  465.1 0.0 copy-start.7
  465.1 0.0 copy-start.2
  465.1 0.9 constant_dynamic-slice_fusion
  466.0 0.6 fusion.6
  466.6 1.8 copy.37
  468.3 0.0 copy-start.6
  468.3 2.1 copy.38
  470.5 0.0 copy-done.7
  470.5 0.0 copy-start.5
  470.5 0.0 copy-start.3
  470.5 0.6 copy.39
  471.1 0.0 copy-done.2
  471.1 0.9 copy.40
  472.0 0.0 copy-done.6
  472.0 0.0 copy-start.4
  472.0 0.0 copy-start.1
  472.0 0.7 copy.41
  472.7 0.0 copy-done.5
  472.7 0.7 copy.42
  473.5 0.0 copy-done.3
  473.5 0.8 copy.43
  474.3 0.0 copy-done.4
  474.3 0.0 copy-start
  474.3 0.7 copy.44
  475.0 0.0 copy-done.1
  475.0 1.0 copy.45
  476.0 0.0 copy-done
  476.0 1.0 copy.46
Async XLA Ops:
  465.1 5.4 %copy-start.7 = (f32[16,1536]{1,0:T(8,128)S(1)}, f32[16,1536]{1,0:T(8,128)}, u32[]{:S(2)}) copy-start(f32[16,1536]{1,0:T(8,128)} %get-tuple-element.69) | copy-start | bytes 294916
  465.1 6.0 %copy-start.2 = (f32[192,1152]{1,0:T(8,128)S(1)}, f32[192,1152]{1,0:T(8,128)}, u32[]{:S(2)}) copy-start(f32[192,1152]{1,0:T(8,128)} %get-tuple-element.95) | copy-start | bytes 2654212
  468.3 3.7 copy-start.6
  470.5 2.3 copy-start.5
  470.5 3.0 copy-start.3
  472.0 2.3 copy-start.4
  472.0 3.0 copy-start.1
  474.3 1.7 copy-start

commit v3 on v2

--- a/solution.py
+++ b/solution.py
@@ -510,28 +510,27 @@
         self.launch(self.shard, 0)
         pltpu.make_async_copy(self.shard, here, self.near).start()
 
-    def relay(self, k):
+    def pass_on(self):
+        other = self.rows(self.spot.z, 1)
+        self.y_copy(other, other, 0).wait_recv()
+        self.launch(other, 1)
+
+    def relay(self, k, side, flip):
         spot = self.spot
-        if self.spread and k == 1:
-            other = self.rows(spot.z, 1)
-            self.y_copy(other, other, 0).wait_recv()
-            self.launch(other, 1)
-        for flip in (0, 1) if self.spread else (0,):
-            for side in (0, 1):
-                src_z = spot.z - k if side else spot.z + k
-                block = self.rows(src_z, flip)
-
-                @pl.when(src_z >= 0 if side else src_z <= 3)
+        src_z = spot.z - k if side else spot.z + k
+        block = self.rows(src_z, flip)
+
+        @pl.when(src_z >= 0 if side else src_z <= 3)
+        def _():
+            self.z_copy(block, block, k, side, flip).wait_recv()
+            if k < 3:
+
+                @pl.when(spot.z < 3 if side else spot.z > 0)
                 def _():
-                    self.z_copy(block, block, k, side, flip).wait_recv()
-                    if k < 3:
-
-                        @pl.when(spot.z < 3 if side else spot.z > 0)
-                        def _():
-                            self.z_copy(block, block, k + 1, side, flip).start()
-
-                    if not self.spread:
-                        self.y_copy(block, block, 1 + side * 3 + k - 1).start()
+                    self.z_copy(block, block, k + 1, side, flip).start()
+
+            if not self.spread:
+                self.y_copy(block, block, 1 + side * 3 + k - 1).start()
 
     def finish(self):
         spot = self.spot
@@ -625,6 +624,33 @@
     return center * lax.rsqrt(spread + 1e-05) * gain + shift
 
 
+FORWARD_ORDER = (
+    (0, 1), (0, 0), (3, 28), (0, 2), (2, 0, 1, 0, 0), (2, 0, 1, 1, 0), (2, 1, 1, 0, 0),
+    (2, 1, 1, 1, 0), (2, 2, 1, 0, 0), (2, 2, 1, 1, 0), (2, 0, 2, 1, 0), (2, 0, 2, 0, 0), (0, 3),
+    (3, 29), (2, 1, 2, 1, 0), (3, 31), (2, 2, 2, 0, 0), (2, 2, 2, 1, 0), (2, 1, 2, 0, 0),
+    (2, 0, 3, 1, 0), (3, 30), (2, 0, 3, 0, 0), (0, 4), (2, 3, 1, 1, 0), (2, 3, 1, 0, 0),
+    (2, 2, 3, 0, 0), (2, 1, 3, 1, 0), (2, 2, 3, 1, 0), (2, 1, 3, 0, 0), (3, 0), (3, 32),
+    (2, 4, 1, 1, 0), (2, 3, 2, 0, 0), (2, 3, 2, 1, 0), (2, 4, 1, 0, 0), (0, 5), (2, 4, 2, 1, 0),
+    (2, 3, 3, 0, 0), (3, 33), (3, 36), (2, 3, 3, 1, 0), (2, 4, 2, 0, 0), (0, 6), (2, 5, 1, 0, 0),
+    (2, 5, 1, 1, 0), (2, 4, 3, 1, 0), (2, 4, 3, 0, 0), (2, 6, 1, 1, 0), (2, 6, 1, 0, 0),
+    (2, 5, 2, 1, 0), (2, 5, 2, 0, 0), (0, 7), (0, 8), (2, 6, 2, 1, 0), (2, 6, 2, 0, 0),
+    (2, 5, 3, 1, 0), (2, 5, 3, 0, 0), (2, 7, 1, 1, 0), (2, 7, 1, 0, 0), (3, 1), (3, 2), (3, 3),
+    (2, 6, 3, 1, 0), (2, 8, 1, 0, 0), (2, 6, 3, 0, 0), (2, 7, 2, 1, 0), (2, 7, 2, 0, 0), (0, 9),
+    (2, 8, 1, 1, 0), (0, 10), (2, 7, 3, 1, 0), (2, 8, 2, 0, 0), (3, 4), (2, 9, 1, 1, 0),
+    (2, 7, 3, 0, 0), (3, 5), (3, 6), (3, 7), (2, 8, 2, 1, 0), (2, 9, 1, 0, 0), (0, 11), (3, 34),
+    (2, 10, 1, 1, 0), (2, 10, 1, 0, 0), (1, 8), (3, 10), (3, 11), (2, 9, 2, 1, 0),
+    (2, 8, 3, 0, 0), (3, 8), (3, 9), (3, 12), (3, 13), (2, 8, 3, 1, 0), (2, 9, 2, 0, 0), (3, 14),
+    (2, 11, 1, 0, 0), (2, 10, 2, 0, 0), (0, 12), (3, 15), (3, 16), (2, 8, 1, 1, 1), (3, 17),
+    (2, 8, 1, 0, 1), (0, 13), (2, 10, 2, 1, 0), (2, 11, 1, 1, 0), (2, 9, 3, 0, 0),
+    (2, 9, 3, 1, 0), (2, 11, 2, 0, 0), (2, 12, 1, 1, 0), (3, 18), (2, 10, 3, 0, 0), (3, 19),
+    (2, 8, 2, 1, 1), (2, 12, 1, 0, 0), (3, 20), (3, 21), (2, 13, 1, 1, 0), (3, 35),
+    (2, 8, 2, 0, 1), (2, 10, 3, 1, 0), (2, 11, 2, 1, 0), (2, 13, 1, 0, 0), (2, 11, 3, 0, 0),
+    (2, 12, 2, 1, 0), (3, 22), (2, 12, 2, 0, 0), (3, 23), (2, 8, 3, 1, 1), (3, 24),
+    (2, 8, 3, 0, 1), (2, 13, 2, 1, 0), (2, 11, 3, 1, 0), (2, 13, 2, 0, 0), (3, 25),
+    (2, 12, 3, 0, 0), (2, 12, 3, 1, 0), (2, 13, 3, 0, 0), (2, 13, 3, 1, 0), (3, 26), (3, 27),
+)
+
+
 def forward_kernel(names, *refs):
     r = named(names, refs)
     spot = Spot()
@@ -652,20 +678,25 @@
     def share(number, own, where):
         return Share(spot, own, where, r.bsend.at[number], r.brecv.at[number])
 
-    def gather(number, shard, full, spread=False):
-        sems = (item.at[number] for item in (r.zsend, r.zrecv, r.ysend, r.yrecv, r.near))
-        return Gather(spot, shard, full, *sems, spread)
-
-    gathers = Bag(
-        outward=gather(0, r.outward, r.v_outward),
-        inward=gather(1, r.aligned, r.v_inward),
-        query=gather(2, r.query, r.v_query),
-        keys=gather(3, r.keys, r.v_keys, True),
-        back=gather(4, r.back, r.v_back, True),
-        expand=gather(5, r.expand, r.v_expand),
-        contract=gather(6, r.contract, r.v_contract),
-        norms=gather(7, r.v_norms, r.v_norm_all),
-    )
+    gathers = []
+
+    def gather(shard, full, spread):
+        wide = full.shape[1] // len(spread)
+        first = len(gathers)
+        for number, flag in enumerate(spread):
+            here = slice(number * wide, (number + 1) * wide)
+            sems = (item.at[first + number] for item in (r.zsend, r.zrecv, r.ysend, r.yrecv, r.near))
+            gathers.append(Gather(spot, shard.at[:, here], full.at[:, here], *sems, flag))
+        return gathers[first:]
+
+    g_norms = gather(r.v_norms, r.v_norm_all, (False,))
+    g_outward = gather(r.outward, r.v_outward, (False,))
+    g_inward = gather(r.aligned, r.v_inward, (False, False, False))
+    g_query = gather(r.query, r.v_query, (False,))
+    g_keys = gather(r.keys, r.v_keys, (False,))
+    g_back = gather(r.back, r.v_back, (False,))
+    g_expand = gather(r.expand, r.v_expand, (True, False))
+    g_contract = gather(r.contract, r.v_contract, (False, False, False, False))
 
     spot.greet()
 
@@ -691,14 +722,21 @@
             push(src, dst, r.asend.at[part], r.arecv.at[kind], (spot.grp, owner)).start()
 
     norm_share = share(0, r.norms, lambda index: r.v_norms.at[pl.ds(index * 16, 16)])
-    norm_own = pltpu.make_async_copy(r.norms, r.v_norms.at[pl.ds(blk * 16, 16)], r.near.at[8])
+    norm_own = pltpu.make_async_copy(r.norms, r.v_norms.at[pl.ds(blk * 16, 16)], r.near.at[16])
     norm_own.start()
     norm_share.start()
     frame_share = share(1, r.frames, row_block(r.x_all))
-    frame_own = pltpu.make_async_copy(r.frames, row_block(r.x_all)(blk), r.near.at[9])
+    frame_own = pltpu.make_async_copy(r.frames, row_block(r.x_all)(blk), r.near.at[17])
     frame_own.start()
     frame_share.start()
-    gathers.outward.start()
+    grad_share = share(2, r.incoming, row_block(r.g_all))
+    grad_own = pltpu.make_async_copy(r.incoming, row_block(r.g_all)(blk), r.near.at[18])
+    attended_share = share(3, col_block(r.s_attended, wide)(blk), col_block(r.s_attended, wide))
+    one_share = share(4, col_block(r.s_one_all, wide)(blk), col_block(r.s_one_all, wide))
+    text_share = share(5, col_block(r.s_text, 2 * wide)(blk), col_block(r.s_text, 2 * wide))
+    crossed_share = share(6, col_block(r.s_crossed, wide)(blk), col_block(r.s_crossed, wide))
+    two_share = share(7, col_block(r.s_two_all, wide)(blk), col_block(r.s_two_all, wide))
+    g_outward[0].start()
     for kind in range(3):
         dst = r.aligned.at[:, kind * wide : (kind + 1) * wide]
         home = (kind * 4 + blk) // 3
@@ -711,41 +749,21 @@
         def _():
             push(dst, dst, r.asend.at[0], r.arecv.at[kind], spot.sib).wait_recv()
 
-    gathers.inward.start()
-    norm_share.relay()
-    norm_own.wait()
-    norm_share.finish()
-    gathers.norms.start()
-    frame_share.relay()
-    grad_share = share(2, r.incoming, row_block(r.g_all))
-    grad_own = pltpu.make_async_copy(r.incoming, row_block(r.g_all)(blk), r.near.at[10])
-    grad_own.start()
-    grad_share.start()
-    gathers.outward.relay(1)
-    gathers.norms.relay(1)
-    gathers.outward.relay(2)
-    gathers.norms.relay(2)
-    gathers.outward.relay(3)
-    gathers.norms.relay(3)
-    gathers.query.start()
-    gathers.norms.finish()
-
-    depth = 8 * 128
-    line = lax.broadcasted_iota(jnp.int32, (depth, 384), 0)
-    column = lax.broadcasted_iota(jnp.int32, (depth, 384), 1)
-    inside = line & 127
-    place = jnp.where((inside < 48) & (column == (line >> 7) * 48 + inside), 1.0, 0.0).astype(BF16)
-    for pair in range(4):
-        left = jnp.concatenate(
-            [r.v_norm_all[pair * 128 + part * 16 : pair * 128 + part * 16 + 16, :] for part in range(8)],
-            axis=1,
-        )
-        r.v_norm_rows[:, pair * 384 : (pair + 1) * 384] = dot(left, place)
-    save(r.v_norm_rows, r.norm_all)
-    gathers.inward.relay(1)
-    frame_own.wait()
-    frame_share.finish()
-    grad_share.relay()
+    low = lax.broadcasted_iota(jnp.int32, (1, 128), 1) < 64
+    kept = []
+
+    def half(value, part):
+        return jnp.where(low if part == 0 else jnp.logical_not(low), value, jnp.zeros_like(value))
+
+    def finish(items):
+        for item in items:
+            item.finish()
+
+    def turn_over(source, turned):
+        def flip(block):
+            turned[:, block] = source[block, :].T
+
+        tiles(length // 128, 128, flip)
 
     def normed(source, index, turned):
         gain = r.v_norm_rows[index : index + 1, :]
@@ -756,165 +774,197 @@
             r.a_all[block, :] = result
 
         tiles(length // 32, 32, body)
-
-        def flip(block):
-            turned[:, block] = r.a_all[block, :].T
-
-        tiles(length // 128, 128, flip)
-
-    normed(r.x_all, 0, r.t_first)
-    save(r.t_first, r.first_t)
-    gathers.keys.start()
-    gathers.inward.relay(2)
-    gathers.inward.relay(3)
-    gathers.query.relay(1)
-    gathers.query.relay(2)
-    gathers.query.relay(3)
-    gathers.back.start()
-    gathers.inward.finish()
-    save(r.v_inward, r.w_inward)
-
-    def joint_tile(block):
-        r.s_joint[:, block] = dot(r.a_all[...], r.v_inward[:, block]).astype(BF16)
-
-    tiles(3, wide, joint_tile)
-    save(r.s_joint, r.joint)
-    gathers.keys.relay(1)
-
-    low = lax.broadcasted_iota(jnp.int32, (1, 128), 1) < 64
-
-    def half(value, part):
-        return jnp.where(low if part == 0 else jnp.logical_not(low), value, jnp.zeros_like(value))
-
-    def attend_step(step):
-        pair, block = step // 4, lax.rem(step, 4)
-        here = pl.ds(pl.multiple_of(block * 128, 128), 128)
-        query = r.s_joint[here, lanes(pair, 128)]
-        key = r.s_joint[:, lanes(pair + 3, 128)]
-        value = r.s_joint[:, lanes(pair + 6, 128)]
-        keep = r.ids_row[...] <= r.ids_col[here, :]
-        results = []
-        for part in (0, 1):
-            scores = jnp.where(keep, dot_t(half(query, part), key) * 0.125, -1e30)
-            power = jnp.exp(scores - jnp.max(scores, axis=1, keepdims=True))
-            weighting = (power * (1.0 / jnp.sum(power, axis=1, keepdims=True))).astype(BF16)
-            results.append(dot(weighting, value))
-        r.s_attended[here, lanes(blk * 3 + pair, 128)] = jnp.where(low, *results).astype(BF16)
-
-    @pl.loop(0, 12)
-    def _(step):
-        attend_step(step)
-
-    attended_share = share(3, col_block(r.s_attended, wide)(blk), col_block(r.s_attended, wide))
-    attended_share.start()
-    gathers.keys.relay(2)
-    gathers.keys.relay(3)
-    gathers.outward.finish()
-    save(r.v_outward, r.w_outward)
-    attended_share.relay()
-    gathers.expand.start()
-    attended_share.finish()
-    r.s_one[...] = dot(r.s_attended[...], r.v_outward[...]) + r.x_all[:, lanes(blk, wide)].astype(F32)
-    r.s_one_all[:, lanes(blk, wide)] = r.s_one[...].astype(BF16)
-    one_share = share(4, col_block(r.s_one_all, wide)(blk), col_block(r.s_one_all, wide))
-    one_share.start()
-    gathers.back.relay(1)
-    gathers.back.relay(2)
-    one_share.relay()
-
-    def turn_over(source, turned):
-        def flip(block):
-            turned[:, block] = source[block, :].T
-
-        tiles(length // 128, 128, flip)
-
-    turn_over(r.s_attended, r.t_attended)
-    save(r.t_attended, r.attended_t)
-    gathers.back.relay(3)
-    gathers.contract.start()
-    gathers.keys.finish()
-    save(r.v_keys, r.w_keys)
-    r.s_text[:, lanes(blk, 2 * wide)] = dot(r.text[...], r.v_keys[...]).astype(BF16)
-    text_share = share(5, col_block(r.s_text, 2 * wide)(blk), col_block(r.s_text, 2 * wide))
-    one_share.finish()
-    text_share.start()
-    save(row_block(r.s_one_all)(blk), r.one_rows)
-    normed(r.s_one_all, 1, r.t_second)
-    save(r.t_second, r.second_t)
-    text_share.relay()
-    gathers.expand.relay(1)
-    gathers.query.finish()
-    save(r.v_query, r.w_query)
-    r.s_query[...] = dot(r.a_all[...], r.v_query[...]).astype(BF16)
-    save(r.s_query, r.cross_query)
-    text_share.finish()
-    save(r.s_text, r.text_all)
-
-    @pl.loop(0, 3)
-    def _(pair):
-        query = r.s_query[:, lanes(pair, 128)]
-        key = r.s_text[:, lanes(blk * 3 + pair, 128)]
-        value = r.s_text[:, lanes(12 + blk * 3 + pair, 128)]
-        results = []
-        for part in (0, 1):
-            scores = dot_t(half(query, part), key) * 0.125
-            power = jnp.exp(scores - jnp.max(scores, axis=1, keepdims=True))
-            weighting = (power * (1.0 / jnp.sum(power, axis=1, keepdims=True))).astype(BF16)
-            results.append(dot(weighting, value))
-        r.s_crossed[:, lanes(blk * 3 + pair, 128)] = jnp.where(low, *results).astype(BF16)
-
-    crossed_share = share(6, col_block(r.s_crossed, wide)(blk), col_block(r.s_crossed, wide))
-    crossed_share.start()
-    gathers.expand.relay(2)
-    crossed_share.relay()
-    gathers.back.finish()
-    save(r.v_back, r.w_back)
-    crossed_share.finish()
-    r.s_one[...] += dot(r.s_crossed[...], r.v_back[...])
-    r.s_two_all[:, lanes(blk, wide)] = r.s_one[...].astype(BF16)
-    two_share = share(7, col_block(r.s_two_all, wide)(blk), col_block(r.s_two_all, wide))
-    two_share.start()
-    gathers.expand.relay(3)
-    two_share.relay()
-    turn_over(r.s_crossed, r.t_crossed)
-    save(r.t_crossed, r.crossed_t)
-    two_share.finish()
-    save(row_block(r.s_two_all)(blk), r.two_rows)
-    gathers.contract.relay(1)
-    normed(r.s_two_all, 2, r.t_third)
-    save(r.t_third, r.third_t)
-    grad_share.finish()
-    grad_own.wait()
-    save(r.g_all, r.grad_all)
-    gathers.expand.finish()
-    kept = save(r.v_expand, r.w_expand)
-    gathers.contract.relay(2)
-
-    def upward_tile(block):
-        r.s_upward[:, block] = dot(r.a_all[...], r.v_expand[:, block])
-
-    tiles(4, 384, upward_tile)
-    gathers.contract.relay(3)
-
-    def gelu_tile(block):
-        upward = r.s_upward[block, :]
-        gate = 0.5 + 0.5 * lax.erf(upward * 0.7071067811865476)
-        r.s_active[block, :] = (upward * gate).astype(BF16)
-        r.s_slope[block, :] = gate + upward * jnp.exp(-0.5 * upward * upward) * 0.3989422804014327
-
-    tiles(length // 16, 16, gelu_tile)
-    save(r.s_slope, r.slope)
-    turn_over(r.g_all, r.t_grad)
-    kept.wait()
-    gathers.expand.drain()
-
-    def contract_tile(block):
-        r.v_expand[:, block] = dot(r.t_grad[...], r.s_active[:, block]).astype(BF16)
-
-    tiles(4, 384, contract_tile)
-    save(r.v_expand, r.contract_grad)
-    save(r.s_active, r.active)
-    gathers.contract.finish()
+        turn_over(r.a_all, turned)
+
+    def side_by_side():
+        depth = 8 * 128
+        line = lax.broadcasted_iota(jnp.int32, (depth, 384), 0)
+        column = lax.broadcasted_iota(jnp.int32, (depth, 384), 1)
+        inside = line & 127
+        place = jnp.where((inside < 48) & (column == (line >> 7) * 48 + inside), 1.0, 0.0).astype(BF16)
+        for pair in range(4):
+            parts = [pl.ds(pair * 128 + part * 16, 16) for part in range(8)]
+            left = jnp.concatenate([r.v_norm_all[part, :] for part in parts], axis=1)
+            r.v_norm_rows[:, pair * 384 : (pair + 1) * 384] = dot(left, place)
+        save(r.v_norm_rows, r.norm_all)
+
+    def first_norm():
+        finish(g_norms)
+        side_by_side()
+        normed(r.x_all, 0, r.t_first)
+        save(r.t_first, r.first_t)
+
+    def joint():
+        finish(g_inward)
+        save(r.v_inward, r.w_inward)
+
+        def body(block):
+            r.s_joint[:, block] = dot(r.a_all[...], r.v_inward[:, block]).astype(BF16)
+
+        tiles(3, wide, body)
+        save(r.s_joint, r.joint)
+
+    def soft(scores):
+        power = jnp.exp(scores - jnp.max(scores, axis=1, keepdims=True))
+        return (power * (1.0 / jnp.sum(power, axis=1, keepdims=True))).astype(BF16)
+
+    def attend():
+        @pl.loop(0, 12)
+        def _(step):
+            pair, block = step // 4, lax.rem(step, 4)
+            here = pl.ds(pl.multiple_of(block * 128, 128), 128)
+            query = r.s_joint[here, lanes(pair, 128)]
+            key = r.s_joint[:, lanes(pair + 3, 128)]
+            value = r.s_joint[:, lanes(pair + 6, 128)]
+            keep = r.ids_row[...] <= r.ids_col[here, :]
+            results = []
+            for part in (0, 1):
+                scores = jnp.where(keep, dot_t(half(query, part), key) * 0.125, -1e30)
+                results.append(dot(soft(scores), value))
+            r.s_attended[here, lanes(blk * 3 + pair, 128)] = jnp.where(low, *results).astype(BF16)
+
+    def hidden_one():
+        finish(g_outward)
+        save(r.v_outward, r.w_outward)
+        own = r.x_all[:, lanes(blk, wide)].astype(F32)
+        r.s_one[...] = dot(r.s_attended[...], r.v_outward[...]) + own
+        r.s_one_all[:, lanes(blk, wide)] = r.s_one[...].astype(BF16)
+
+    def one_here():
+        one_share.finish()
+        save(row_block(r.s_one_all)(blk), r.one_rows)
+
+    def text_pairs():
+        finish(g_keys)
+        save(r.v_keys, r.w_keys)
+        r.s_text[:, lanes(blk, 2 * wide)] = dot(r.text[...], r.v_keys[...]).astype(BF16)
+
+    def second_norm():
+        normed(r.s_one_all, 1, r.t_second)
+        save(r.t_second, r.second_t)
+
+    def cross_query():
+        finish(g_query)
+        save(r.v_query, r.w_query)
+        r.s_query[...] = dot(r.a_all[...], r.v_query[...]).astype(BF16)
+        save(r.s_query, r.cross_query)
+
+    def text_here():
+        text_share.finish()
+        save(r.s_text, r.text_all)
+
+    def cross():
+        @pl.loop(0, 3)
+        def _(pair):
+            query = r.s_query[:, lanes(pair, 128)]
+            key = r.s_text[:, lanes(blk * 3 + pair, 128)]
+            value = r.s_text[:, lanes(12 + blk * 3 + pair, 128)]
+            results = []
+            for part in (0, 1):
+                results.append(dot(soft(dot_t(half(query, part), key) * 0.125), value))
+            r.s_crossed[:, lanes(blk * 3 + pair, 128)] = jnp.where(low, *results).astype(BF16)
+
+    def hidden_two():
+        finish(g_back)
+        save(r.v_back, r.w_back)
+        r.s_one[...] += dot(r.s_crossed[...], r.v_back[...])
+        r.s_two_all[:, lanes(blk, wide)] = r.s_one[...].astype(BF16)
+
+    def two_here():
+        two_share.finish()
+        save(row_block(r.s_two_all)(blk), r.two_rows)
+
+    def third_norm():
+        normed(r.s_two_all, 2, r.t_third)
+        save(r.t_third, r.third_t)
+
+    def upward():
+        finish(g_expand)
+        kept.append(save(r.v_expand, r.w_expand))
+
+        def body(block):
+            r.s_upward[:, block] = dot(r.a_all[...], r.v_expand[:, block])
+
+        tiles(4, 384, body)
+
+    def gelu():
+        def body(block):
+            value = r.s_upward[block, :]
+            gate = 0.5 + 0.5 * lax.erf(value * 0.7071067811865476)
+            r.s_active[block, :] = (value * gate).astype(BF16)
+            r.s_slope[block, :] = gate + value * jnp.exp(-0.5 * value * value) * 0.3989422804014327
+
+        tiles(length // 16, 16, body)
+        save(r.s_slope, r.slope)
+        save(r.s_active, r.active)
+
+    def contract_grad():
+        kept[0].wait()
+        for item in g_expand:
+            item.drain()
+
+        def body(block):
+            r.v_expand[:, block] = dot(r.t_grad[...], r.s_active[:, block]).astype(BF16)
+
+        tiles(4, 384, body)
+        save(r.v_expand, r.contract_grad)
+
+    def nothing():
+        pass
+
+    def frames_here():
+        frame_own.wait()
+        frame_share.finish()
+
+    def grad_start():
+        grad_own.start()
+        grad_share.start()
+
+    def grad_here():
+        grad_share.finish()
+        grad_own.wait()
+        save(r.g_all, r.grad_all)
+
+    def attended_over():
+        turn_over(r.s_attended, r.t_attended)
+        save(r.t_attended, r.attended_t)
+
+    def crossed_over():
+        turn_over(r.s_crossed, r.t_crossed)
+        save(r.t_crossed, r.crossed_t)
+
+    def grad_over():
+        turn_over(r.g_all, r.t_grad)
+
+    steps = (
+        first_norm, joint, attend,
+        attended_share.start, attended_share.relay, attended_share.finish,
+        hidden_one, one_share.start, one_share.relay, one_here,
+        text_pairs, text_share.start, text_share.relay, text_here,
+        second_norm, cross_query, cross,
+        crossed_share.start, crossed_share.relay, crossed_share.finish,
+        hidden_two, two_share.start, two_share.relay, two_here,
+        third_norm, upward, gelu, contract_grad,
+        nothing, frame_share.relay, frames_here, grad_start, grad_share.relay, grad_here,
+        attended_over, crossed_over, grad_over,
+    )
+    for kind, number, *rest in FORWARD_ORDER:
+        if kind == 3:
+            steps[number]()
+            continue
+        item = gathers[number]
+        if kind == 2:
+            item.relay(*rest)
+        elif kind == 1:
+            item.pass_on()
+        elif item is g_norms[0]:
+            norm_share.relay()
+            norm_own.wait()
+            norm_share.finish()
+            item.start()
+        elif item is not g_outward[0]:
+            item.start()
+    finish(g_contract)
     save(r.v_contract, r.w_contract)
     for part in range(3):
         owner, kind, src, dst = aligned_copy(part)
@@ -927,11 +977,11 @@
         norm_share, frame_share, grad_share, attended_share, one_share, text_share, crossed_share, two_share,
     ):
         item.drain()
-    for item in vars(gathers).values():
-        if item is not gathers.expand:
+    for item in gathers:
+        if item not in g_expand:
             item.drain()
     for copy in outs:
-        if copy is not kept:
+        if copy is not kept[0]:
             copy.wait()
 
 
@@ -1030,11 +1080,11 @@
         v_norm_rows=((16, width), F32),
     )
     sems = dict(
-        zsend=(8, 12),
-        zrecv=(8, 12),
-        ysend=(8, 7),
-        yrecv=(8, 7),
-        near=(12,),
+        zsend=(14, 12),
+        zrecv=(14, 12),
+        ysend=(14, 7),
+        yrecv=(14, 7),
+        near=(19,),
         bsend=(8, 3),
         brecv=(8, 3),
         asend=(3,),

time: 485 us -> 462 us (0.953)
  Pallas kernels: 461 us -> 439 us
    pallas_call x2, Pallas kernels: 461 us -> 439 us  [run_kernel(): pl.pallas_call(functools.partial(kernel, names), out_shape=[jax.ShapeDtyp...]
where the time goes in v3:
time: 462 us; the launch traced here: 455 us
  Pallas kernels  439 us (95%)
  local copies, waits for them, and re-layouts  13.4 us (3%)
    pallas_call x2, Pallas kernels, run_kernel(): pl.pallas_call(functools.partial(kernel, names), out_shape=[jax.ShapeDtyp...  439 us
    unnamed x26, local copies, waits for them, and re-layouts  10.4 us

profile of v3, /device:TPU:0, one launch (start us, length us, event | category | flops | bytes accessed | tf_op | source)
XLA Modules:
  0.0 455.0 jit_solution(10372823614635825282)
XLA Ops:
  0.6 0.7 multiply_bitcast_fusion
  1.3 0.1 iota_add_fusion
  1.4 0.9 add.55.refs_1_
  2.3 0.7 add.52.refs_2_
  2.9 1.3 fusion.5.refs_4_
  4.2 202.9 %shard_map.220 = (bf16[1536,384]{1,0:T(8,128)(2,1)}, bf16[1536,1152]{1,0:T(8,128)(2,1)}, bf16[1536,384]{1,0:T(8,128)(2,1)}, bf16[1536,768]{1,0:T(8,128)(2,1)}, b...) custom-call(bf16[64,1536]{1,0:T(8,128)(2,1)} %bitcast.15, ...), custom_call_target="tpu_custom_call" | custom-call | tf_op jit(solution)/shard_map/pallas_call | solution.py:997
  207.1 236.0 %shard_map.221 = (f32[192,1536]{1,0:T(8,128)}, f32[192,1536]{1,0:T(8,128)}, f32[192,384]{1,0:T(8,128)}, f32[192,768]{1,0:T(8,128)}, f32[192,384]{1,0:T(8,128)}, ...) custom-call(bf16[64,1536]{1,0:T(8,128)(2,1)} %bitcast.16, ...), custom_call_target="tpu_custom_call" | custom-call | tf_op jit(solution)/shard_map/pallas_call | solution.py:997
  443.1 0.0 copy-start.7
  443.1 0.0 copy-start.2
  443.1 0.9 constant_dynamic-slice_fusion
  444.0 0.6 fusion.6
  444.6 1.8 copy.37
  446.3 0.0 copy-start.6
  446.3 2.1 copy.38
  448.4 0.0 copy-done.7
  448.4 0.0 copy-start.5
  448.4 0.0 copy-start.3
  448.4 0.6 copy.39
  449.1 0.0 copy-done.2
  449.1 0.9 copy.40
  450.0 0.0 copy-done.6
  450.0 0.0 copy-start.4
  450.0 0.0 copy-start.1
  450.0 0.7 copy.41
  450.7 0.0 copy-done.5
  450.7 0.7 copy.42
  451.4 0.0 copy-done.3
  451.4 0.8 copy.43
  452.3 0.0 copy-done.4
  452.3 0.0 copy-start
  452.3 0.7 copy.44
  453.0 0.0 copy-done.1
  453.0 1.0 copy.45
  454.0 0.0 copy-done
  454.0 1.0 copy.46
Async XLA Ops:
  443.1 5.4 %copy-start.7 = (f32[16,1536]{1,0:T(8,128)S(1)}, f32[16,1536]{1,0:T(8,128)}, u32[]{:S(2)}) copy-start(f32[16,1536]{1,0:T(8,128)} %get-tuple-element.69) | copy-start | bytes 294916
  443.1 6.0 %copy-start.2 = (f32[192,1152]{1,0:T(8,128)S(1)}, f32[192,1152]{1,0:T(8,128)}, u32[]{:S(2)}) copy-start(f32[192,1152]{1,0:T(8,128)} %get-tuple-element.95) | copy-start | bytes 2654212
  446.3 3.7 copy-start.6
  448.4 2.3 copy-start.5
  448.4 3.0 copy-start.3
  450.0 2.3 copy-start.4
  450.0 3.0 copy-start.1
  452.3 1.7 copy-start

commit v4 on v3

--- a/solution.py
+++ b/solution.py
@@ -1126,36 +1126,32 @@
         for z in (0, 3, 1, 2):
             self.y_copy(z).start()
 
-    def z_copy(self, goal, slot, who, flip):
-        index = flip * 4 + slot
+    def z_push(self, goal, flip, who, slot):
+        index = flip * 5 + slot
         return push(
             self.rows(goal, flip), self.along.at[index], self.zsend.at[flip * 4 + goal],
             self.zrecv.at[index], (who * 2 + self.spot.y, self.spot.blk),
         )
 
+    def onward(self, goal, flip, home):
+        who = home + 1 if goal > home else home - 1
+        slot = 4 if who == goal and home > goal else goal
+        self.z_push(goal, flip, who, slot).start()
+
     def z_first(self, goal, flip):
-        z = self.spot.z
-        middle, end = (2, 3) if goal == 0 else (1, 0)
-        for home in range(4):
-            if home == goal or (goal in (0, 3) and home == middle):
-                continue
-
-            @pl.when(z == home)
-            def _():
-                if goal in (0, 3) and home == end:
-                    self.z_copy(goal, 3, middle, flip).start()
-                else:
-                    self.z_copy(goal, home - (home > goal), goal, flip).start()
-
-    def z_second(self, goal, flip):
-        middle = 2 if goal == 0 else 1
-
-        @pl.when(self.spot.z == middle)
+        for home in (0, 3):
+            if home != goal:
+
+                @pl.when(self.spot.z == home)
+                def _():
+                    self.onward(goal, flip, home)
+
+    def pass_on(self, goal, flip, home):
+        @pl.when(self.spot.z == home)
         def _():
-            index = flip * 4 + 3
-            self.z_copy(goal, 3, goal, flip).wait_recv()
-            self.add(self.rows(goal, flip), self.along.at[index])
-            self.z_copy(goal, middle - (middle > goal), goal, flip).start()
+            self.z_push(goal, flip, home, goal).wait_recv()
+            self.add(self.rows(goal, flip), self.along.at[flip * 5 + goal])
+            self.onward(goal, flip, home)
 
     def take(self, goal):
         self.y_copy(goal).wait_recv()
@@ -1169,49 +1165,32 @@
             for flip in (1, 0):
                 self.z_first(goal, flip)
 
-    def combine(self, flip=0):
-        self.z_second(0, flip)
-        self.z_second(3, flip)
+    def slots(self, home):
+        return ([home] if home > 0 else []) + ([4] if home < 3 else [])
 
     def arrive(self, flip):
-        z = self.spot.z
-        for slot in range(3):
-            unused = 3 if slot == 2 else 0 if slot == 0 else None
-
-            def wait():
-                self.z_copy(0, slot, 0, flip).wait_recv()
-
-            if slot == 1:
-                wait()
-            else:
-                pl.when(z != (0 if slot == 2 else 3))(wait)
+        for home in range(4):
+
+            @pl.when(self.spot.z == home)
+            def _():
+                for slot in self.slots(home):
+                    self.z_push(home, flip, home, slot).wait_recv()
 
     def total(self, flip, extra, body):
-        z = self.spot.z
-        own = self.rows(z, flip)
-
-        def add_up(slots):
-            @pl.loop(0, self.size // 16)
-            def _(index):
-                here = pl.ds(pl.multiple_of(index * 16, 16), 16)
-                value = own[here, :].astype(F32)
-                for slot in slots:
-                    value += self.along[flip * 4 + slot, here, :].astype(F32)
-                if extra is not None:
-                    value += extra[here, :].astype(F32)
-                body(here, value)
-
-        @pl.when(z == 0)
-        def _():
-            add_up((0, 1))
-
-        @pl.when(z == 3)
-        def _():
-            add_up((1, 2))
-
-        @pl.when((z == 1) | (z == 2))
-        def _():
-            add_up((0, 1, 2))
+        own = self.rows(self.spot.z, flip)
+        for home in range(4):
+
+            @pl.when(self.spot.z == home)
+            def _():
+                @pl.loop(0, self.size // 16)
+                def _(index):
+                    here = pl.ds(pl.multiple_of(index * 16, 16), 16)
+                    value = own[here, :].astype(F32)
+                    for slot in self.slots(home):
+                        value += self.along[flip * 5 + slot, here, :].astype(F32)
+                    if extra is not None:
+                        value += extra[here, :].astype(F32)
+                    body(here, value)
 
     def cross(self):
         self.arrive(1)
@@ -1245,7 +1224,7 @@
 
                 @pl.when(z != goal)
                 def _():
-                    self.z_copy(goal, 0, 0, flip).wait_send()
+                    self.z_push(goal, flip, 0, 0).wait_send()
 
 
 class BlkSum:
@@ -1327,14 +1306,57 @@
     return lax.dot_general(left, right, (((0,), (0,)), ((), ())), preferred_element_type=F32)
 
 
+BACKWARD_ORDER = (
+    (0, 0), (0, 1), (0, 2), (0, 3), (5, 0), (1, 0, 0), (5, 1), (1, 0, 3), (5, 5), (5, 2), (5, 6),
+    (1, 0, 1), (0, 4), (0, 5), (2, 0, 0, 0, 2), (5, 7), (0, 6), (5, 8), (0, 7), (1, 0, 2),
+    (2, 0, 3, 0, 1), (5, 3), (2, 0, 1, 0, 2), (1, 1, 0), (2, 0, 0, 0, 1), (1, 1, 3),
+    (2, 0, 3, 0, 2), (2, 1, 0, 0, 2), (2, 0, 2, 0, 1), (1, 1, 1), (5, 4), (2, 1, 3, 0, 1),
+    (1, 1, 2), (4, 0), (5, 9), (2, 1, 1, 0, 2), (2, 1, 0, 0, 1), (1, 2, 0), (2, 1, 3, 0, 2),
+    (2, 1, 2, 0, 1), (1, 2, 3), (5, 10), (2, 2, 0, 0, 2), (1, 2, 1), (5, 11), (5, 12), (5, 15),
+    (0, 8), (4, 1), (2, 2, 3, 0, 1), (1, 2, 2), (5, 13), (2, 2, 0, 0, 1), (2, 2, 1, 0, 2),
+    (1, 3, 0), (2, 2, 3, 0, 2), (2, 8, 3, 1, 1), (2, 8, 0, 1, 2), (1, 3, 3), (2, 8, 3, 0, 1),
+    (2, 8, 0, 0, 2), (1, 3, 1), (5, 14), (2, 8, 3, 1, 2), (2, 8, 0, 1, 1), (2, 8, 1, 1, 2),
+    (1, 3, 2), (5, 16), (5, 17), (2, 8, 0, 0, 1), (2, 8, 1, 0, 2), (2, 8, 3, 0, 2), (1, 4, 0),
+    (2, 8, 2, 1, 1), (5, 20), (5, 21), (1, 4, 3), (5, 24), (5, 18), (2, 8, 2, 0, 1), (1, 4, 1),
+    (5, 19), (5, 22), (5, 25), (3, 8), (0, 9), (2, 2, 2, 0, 1), (5, 26), (2, 3, 3, 0, 1),
+    (2, 3, 0, 0, 2), (5, 27), (1, 5, 0), (1, 4, 2), (4, 2), (2, 3, 1, 0, 2), (1, 5, 3), (5, 28),
+    (5, 23), (2, 3, 0, 0, 1), (2, 3, 3, 0, 2), (2, 3, 2, 0, 1), (5, 29), (1, 5, 1),
+    (2, 4, 0, 0, 2), (2, 4, 3, 0, 1), (1, 5, 2), (4, 3), (2, 4, 1, 0, 2), (1, 6, 0), (5, 30),
+    (5, 35), (2, 4, 0, 0, 1), (2, 4, 3, 0, 2), (2, 4, 2, 0, 1), (2, 5, 0, 0, 2), (5, 31),
+    (5, 32), (0, 11), (1, 6, 3), (2, 5, 3, 0, 1), (1, 6, 1), (5, 33), (2, 5, 0, 0, 1), (4, 4),
+    (2, 5, 1, 0, 2), (1, 6, 2), (2, 5, 3, 0, 2), (2, 5, 2, 0, 1), (1, 7, 0), (2, 6, 0, 0, 2),
+    (2, 11, 3, 1, 1), (1, 7, 3), (4, 5), (5, 34), (2, 11, 0, 1, 2), (2, 11, 3, 0, 1), (1, 7, 1),
+    (5, 36), (2, 11, 2, 0, 1), (2, 11, 0, 0, 2), (2, 6, 0, 0, 1), (2, 11, 3, 1, 2),
+    (2, 11, 3, 0, 2), (2, 11, 1, 1, 2), (2, 11, 1, 0, 2), (2, 11, 2, 1, 1), (2, 11, 0, 1, 1),
+    (2, 6, 3, 0, 1), (1, 9, 0), (1, 7, 2), (4, 8), (5, 41), (0, 12), (5, 42), (0, 13), (5, 43),
+    (2, 11, 0, 0, 1), (5, 37), (5, 38), (1, 9, 3), (2, 7, 0, 0, 2), (2, 7, 3, 0, 1),
+    (2, 6, 2, 0, 1), (2, 6, 1, 0, 2), (0, 14), (5, 39), (3, 11), (0, 10), (2, 7, 1, 0, 2),
+    (2, 6, 3, 0, 2), (1, 9, 1), (2, 7, 2, 0, 1), (2, 7, 3, 0, 2), (2, 9, 0, 0, 2),
+    (2, 7, 0, 0, 1), (1, 12, 0), (4, 6), (1, 9, 2), (2, 9, 3, 0, 1), (5, 40), (4, 7), (1, 12, 3),
+    (5, 44), (1, 12, 1), (5, 49), (5, 50), (5, 45), (2, 9, 1, 0, 2), (2, 9, 0, 0, 1),
+    (2, 12, 0, 0, 2), (1, 13, 0), (5, 51), (1, 12, 2), (5, 46), (2, 9, 2, 0, 1), (2, 9, 3, 0, 2),
+    (1, 13, 3), (2, 12, 3, 0, 1), (5, 47), (1, 13, 1), (2, 12, 1, 0, 2), (2, 12, 0, 0, 1),
+    (5, 52), (5, 53), (2, 12, 2, 0, 1), (1, 14, 0), (1, 13, 2), (2, 13, 0, 0, 2), (4, 9),
+    (5, 48), (2, 13, 3, 0, 1), (2, 12, 3, 0, 2), (1, 14, 3), (2, 13, 1, 0, 2), (1, 14, 1),
+    (4, 12), (2, 13, 0, 0, 1), (2, 13, 3, 0, 2), (2, 13, 2, 0, 1), (2, 14, 0, 0, 2), (1, 14, 2),
+    (2, 14, 3, 0, 1), (4, 11), (4, 13), (2, 14, 0, 0, 1), (2, 14, 1, 0, 2), (1, 10, 0),
+    (2, 14, 2, 0, 1), (2, 14, 3, 0, 2), (1, 10, 3), (2, 10, 0, 0, 2), (1, 10, 1), (4, 14),
+    (2, 10, 3, 0, 1), (1, 10, 2), (2, 10, 0, 0, 1), (2, 10, 1, 0, 2), (2, 10, 3, 0, 2),
+    (2, 10, 2, 0, 1), (4, 10),
+)
+
+
 def backward_kernel(names, *refs):
     r = named(names, refs)
     spot = Spot()
     rows, width = r.frames.shape
     length = r.v_grad.shape[0]
-    wide = r.v_query_grad.shape[1]
+    wide = width // 4
     blk = spot.blk
     spot.greet_all()
+    query_part, head_part, turn_part, turned_part = (
+        r.v_grad.at[:, index * wide : (index + 1) * wide] for index in range(4)
+    )
 
     def lanes(index, size):
         return pl.ds(pl.multiple_of(index * size, 128), size)
@@ -1353,65 +1375,51 @@
         loads.append(copy)
         return copy
 
-    grads = Bag(
-        contract=r.g_contract,
-        expand=r.g_expand,
-        back=part(r.g_rest, 0, wide),
-        keys=part(r.g_rest, wide, 2 * wide),
-        query=part(r.g_rest, 3 * wide, wide),
-        outward=part(r.g_rest, 4 * wide, wide),
-        inward=part(r.g_contract, 0, 3 * wide),
-    )
-
-    def reduce(number, grad, over, along, spread=False, source=None):
+    reduces, grads = [], []
+
+    def reduce(grad, over, along, spread=False, source=None):
+        number = len(reduces)
         sems = tuple(item.at[number] for item in (r.ysend, r.yrecv, r.zsend, r.zrecv))
-        return Reduce(spot, grad, over, along, sems, spread, source)
-
-    reduces = Bag(
-        contract=reduce(0, grads.contract, r.y_contract, r.z_contract, False, r.contract_grad),
-        expand=reduce(1, grads.expand, r.y_expand, r.z_expand),
-        back=reduce(2, grads.back, r.y_back, r.z_back, True),
-        keys=reduce(3, grads.keys, r.y_keys, r.z_keys, True),
-        query=reduce(4, grads.query, r.y_query, r.z_query),
-        outward=reduce(5, grads.outward, r.y_outward, r.z_outward),
-        inward=reduce(
-            6,
-            grads.inward,
-            r.y_contract.at[:, :, 0 : 3 * wide],
-            r.z_contract.at[:, :, 0 : 3 * wide],
-        ),
-    )
-    reduces.contract.start()
+        reduces.append(Reduce(spot, grad, over, along, sems, spread, source))
+        grads.append(grad)
+
+    def columns(index, *items):
+        here = slice(index * wide, (index + 1) * wide)
+        return [item.at[:, here] if len(item.shape) == 2 else item.at[:, :, here] for item in items]
+
+    for index in range(4):
+        *items, source = columns(index, r.g_contract, r.y_contract, r.z_contract, r.contract_grad)
+        reduce(*items, False, source)
+    for index in range(4):
+        reduce(*columns(index, r.g_expand, r.y_expand, r.z_expand))
+    reduce(part(r.g_rest, 0 * wide, 1 * wide), r.y_back, r.z_back, True)
+    reduce(part(r.g_rest, 1 * wide, 2 * wide), r.y_keys, r.z_keys, False)
+    reduce(part(r.g_rest, 3 * wide, 1 * wide), r.y_query, r.z_query, False)
+    reduce(part(r.g_rest, 4 * wide, 1 * wide), r.y_outward, r.z_outward, True)
+    for index in range(3):
+        reduce(*columns(index, r.g_contract, r.y_contract, r.z_contract))
+    back, keys, query, outward = range(8, 12)
+    inward = 12
     load_grad = load(r.grad_all, r.v_grad)
     load_contract = load(r.w_contract, r.v_one)
     load_slope = load(r.slope, r.v_slope)
-    load_third = load(r.third_t, r.v_left)
-    load_expand = load(r.w_expand, r.v_two)
-    load_own = load(r.contract_grad, r.g_contract)
-    load_norm = load(r.norm_all.at[0:8], r.v_norm)
-    load_crossed = load(r.crossed_t, r.v_right)
-    load_two = load(r.two_rows, r.v_two_rows)
-    load_incoming = load(r.incoming, r.v_rows)
+    later = Bag()
+    later.own = [
+        load(reduces[0].rows(z, 0, r.contract_grad), reduces[0].rows(z, 0, r.g_contract))
+        for z in range(4)
+    ]
     cross_query = part(r.v_joint, 0, wide)
-    load_query = load(r.cross_query, cross_query)
-    load_text = load(r.text_all.at[:, lanes(blk, wide)], part(r.v_text, 0, wide))
-    load_values = load(r.text_all.at[:, lanes(blk + 4, wide)], part(r.v_text, wide, wide))
 
     def blk_sum(number, piece, near, far, size):
         return BlkSum(spot, piece, near, far, r.bsend.at[number], r.brecv.at[number], 16, size)
 
-    load_grad.wait()
-    load_contract.wait()
-    load_slope.wait()
-
-    def up_tile(block):
-        r.v_up[:, block] = (dot(r.v_grad[...], r.v_one[:, block]) * r.v_slope[:, block]).astype(BF16)
-
-    tiles(4, 384, up_tile)
-    load_back = load(r.w_back, part(r.v_one, 0, wide))
-    load_keys = load(r.w_keys, part(r.v_one, wide, 2 * wide))
-    load_outward = load(r.w_outward, part(r.v_one, 3 * wide, wide))
-    load_expand.wait()
+    copies = []
+
+    def give(src, goal):
+        copy = pltpu.make_async_copy(src, goal, r.stored.at[len(copies)])
+        copy.start()
+        copies.append(copy)
+        return copy
 
     def back_rows(left, right):
         def body(block):
@@ -1438,28 +1446,70 @@
     def col_parts(index):
         return r.v_part.at[:, lanes(index, wide)]
 
-    back_rows(r.v_up, r.v_two)
     third_sum = blk_sum(0, row_parts, r.near_rows, r.far_rows, rows)
-    third_sum.start()
-    load_third.wait()
-
-    def expand_tile(block):
-        r.g_expand[:, block] = dot(r.v_left[...], r.v_up[:, block]).astype(BF16)
-
-    third_sum.relay()
-    tiles(4, 384, expand_tile)
-    reduces.expand.start()
-    load_wquery = load(r.w_query, part(r.v_two, 0, wide))
-    load_winward = load(r.w_inward, part(r.v_two, wide, 3 * wide))
-    load_second = load(r.second_t, r.v_left)
-    load_own.wait()
-    reduces.contract.take(0)
-    for copy in (load_norm, load_two, load_incoming):
-        copy.wait()
-    r.v_norm_grads[...] = jnp.zeros_like(r.v_norm_grads)
+    crossed_sum = blk_sum(1, col_parts, r.near_cols, r.far_cols, length)
+    second_sum = blk_sum(2, row_parts, r.near_rows, r.far_rows, rows)
+    attended_sum = blk_sum(3, col_parts, r.near_cols, r.far_cols, length)
+    text_rows = TEXT // 4
+    text_sum = blk_sum(4, row_piece(r.v_text_part, text_rows), r.near_text, r.far_text, text_rows)
+    first_sum = blk_sum(5, row_parts, r.near_rows, r.far_rows, rows)
+    out_sum = blk_sum(6, row_parts, r.near_rows, r.far_rows, rows)
+    turn_two = Turn(spot, r.v_branch, turn_part, r.tsend.at[0], r.trecv.at[0])
+    turn_one = Turn(spot, r.v_branch, turned_part, r.tsend.at[1], r.trecv.at[1])
+    terms_share = Share(
+        spot,
+        r.v_terms.at[:, lanes(blk, wide)],
+        lambda index: r.v_terms.at[:, lanes(index, wide)],
+        r.csend.at[0],
+        r.crecv.at[0],
+    )
     hidden = r.v_slope.at[pl.ds(3 * rows, rows)]
-
-    def norm_back(total, values, number, base, keep):
+    joint_grad = part(r.v_up, 0, 3 * wide)
+    own_rows = pl.ds(pl.multiple_of((blk // 2) * TEXT, TEXT), TEXT)
+    own_cols = lanes(lax.rem(blk, 2), 2 * wide)
+    low = lax.broadcasted_iota(jnp.int32, (1, 128), 1) < 64
+
+    def up():
+        load_grad.wait()
+        load_contract.wait()
+        load_slope.wait()
+        later.expand_in = load(r.w_expand, r.v_two)
+        later.third_in = load(r.third_t, r.v_left)
+        later.norm_in = load(r.norm_all.at[0:8], r.v_norm)
+        later.two_in = load(r.two_rows, r.v_two_rows)
+        later.incoming_in = load(r.incoming, r.v_rows)
+        later.crossed_in = load(r.crossed_t, r.v_right)
+        later.query_in = load(r.cross_query, cross_query)
+        later.text_in = load(r.text_all.at[:, lanes(blk, wide)], part(r.v_text, 0, wide))
+        later.values_in = load(r.text_all.at[:, lanes(blk + 4, wide)], part(r.v_text, wide, wide))
+
+        def body(block):
+            product = dot(r.v_grad[...], r.v_one[:, block])
+            r.v_up[:, block] = (product * r.v_slope[:, block]).astype(BF16)
+
+        tiles(4, 384, body)
+        later.back = load(r.w_back, part(r.v_one, 0, wide))
+        later.keys = load(r.w_keys, part(r.v_one, wide, 2 * wide))
+        later.outward = load(r.w_outward, part(r.v_one, 3 * wide, wide))
+
+    def third_back():
+        later.expand_in.wait()
+        back_rows(r.v_up, r.v_two)
+        later.query = load(r.w_query, part(r.v_two, 0, wide))
+        later.inward = load(r.w_inward, part(r.v_two, wide, 3 * wide))
+
+    expand_done = []
+
+    def expand_grad(index):
+        if not expand_done:
+            later.third_in.wait()
+        expand_done.append(index)
+        grads[4 + index][...] = dot(r.v_left[...], part(r.v_up, index * wide, wide)[...]).astype(BF16)
+        if len(expand_done) == 4:
+            later.second = load(r.second_t, r.v_left)
+
+    def norm_back(total, number, base, keep):
+        values = r.v_two_rows if number == 2 else r.v_rows
         gain = r.v_norm[number : number + 1, :]
 
         @pl.loop(0, rows // 16)
@@ -1473,39 +1523,31 @@
             scaled = incoming * gain
             mean = jnp.mean(scaled, axis=1, keepdims=True)
             match = jnp.mean(scaled * normal, axis=1, keepdims=True)
-            keep(here, base(here) + (scaled - mean - normal * match) * scale)
+            result = base[here, :].astype(F32) + (scaled - mean - normal * match) * scale
+            hidden[here, :] = result
+            if keep:
+                r.v_branch[here, :] = result.astype(BF16)
             for place, term in ((number, incoming * normal), (3 + number, incoming)):
                 spread = pl.ds(place * 8, 8)
                 r.v_norm_grads[spread, :] += term[0:8, :] + term[8:16, :]
 
-    def keep_branch(here, value):
-        hidden[here, :] = value
-        r.v_branch[here, :] = value.astype(BF16)
-
-    third_sum.finish()
-    norm_back(
-        third_sum, r.v_two_rows, 2, lambda here: r.v_rows[here, :].astype(F32), keep_branch
-    )
-    load_one = load(r.one_rows, r.v_rows)
-    turn_two = Turn(spot, r.v_branch, r.v_turn_two, r.tsend.at[0], r.trecv.at[0])
-    turn_two.start()
-    reduces.contract.take(3)
-    load_back.wait()
-    turn_two.finish()
-    third_sum.drain()
-    back_cols(r.v_turn_two, part(r.v_one, 0, wide))
-    crossed_sum = blk_sum(1, col_parts, r.near_cols, r.far_cols, length)
-    crossed_sum.start()
-    load_crossed.wait()
-    crossed_sum.relay()
-    outer(grads.back, r.v_right, r.v_turn_two)
-    reduces.back.start()
-    load_attended = load(r.attended_t, r.v_right)
-    reduces.contract.take(1)
-    crossed_sum.finish()
-    load_query.wait()
-    load_text.wait()
-    load_values.wait()
+    def third_norm():
+        for copy in (later.norm_in, later.two_in, later.incoming_in):
+            copy.wait()
+        r.v_norm_grads[...] = jnp.zeros_like(r.v_norm_grads)
+        norm_back(third_sum, 2, r.v_rows, True)
+        later.one = load(r.one_rows, r.v_rows)
+        turn_two.start()
+
+    def crossed_back():
+        third_sum.drain()
+        later.back.wait()
+        back_cols(turn_part, part(r.v_one, 0, wide))
+
+    def back_grad():
+        later.crossed_in.wait()
+        outer(grads[back], r.v_right, turn_part)
+        later.attended = load(r.attended_t, r.v_right)
 
     def merge(total, target):
         @pl.loop(0, length // 16)
@@ -1513,9 +1555,6 @@
             here = pl.ds(pl.multiple_of(index * 16, 16), 16)
             target[here, :] = total.value(here).astype(BF16)
 
-    merge(crossed_sum, r.v_head_grad)
-    low = lax.broadcasted_iota(jnp.int32, (1, 128), 1) < 64
-
     def half(value, side):
         return jnp.where(low if side == 0 else jnp.logical_not(low), value, jnp.zeros_like(value))
 
@@ -1523,260 +1562,239 @@
         power = jnp.exp(scores - jnp.max(scores, axis=1, keepdims=True))
         return power * (1.0 / jnp.sum(power, axis=1, keepdims=True))
 
-    @pl.loop(0, 3)
-    def _(pair):
-        query = cross_query[:, lanes(pair, 128)]
-        key = r.v_text[:, lanes(pair, 128)]
-        value = r.v_text[:, lanes(3 + pair, 128)]
-        head_grad = r.v_head_grad[:, lanes(pair, 128)]
-        results = []
-        for side in (0, 1):
-            weights = soft(dot_t(half(query, side), key) * 0.125)
-            slope = dot_t(half(head_grad, side), value)
-            score = (weights * (slope - jnp.sum(slope * weights, axis=1, keepdims=True))).astype(BF16)
-            results.append(
-                (
-                    dot(score, key) * 0.125,
-                    t_dot(score, query) * 0.125,
-                    t_dot(weights.astype(BF16), head_grad),
-                )
-            )
-        merged = [jnp.where(low, *item).astype(BF16) for item in zip(*results)]
-        r.v_query_grad[:, lanes(pair, 128)] = merged[0]
-        r.v_terms[0:TEXT, lanes(blk * 3 + pair, 128)] = merged[1]
-        r.v_terms[TEXT : 2 * TEXT, lanes(blk * 3 + pair, 128)] = merged[2]
-
-    load_joint = load(r.joint, r.v_joint)
-    own_terms = r.v_terms.at[:, lanes(blk, wide)]
-    terms_share = Share(
-        spot, own_terms, lambda index: r.v_terms.at[:, lanes(index, wide)], r.csend.at[0], r.crecv.at[0]
-    )
-    terms_share.start()
-    load_wquery.wait()
-    crossed_sum.drain()
-    back_rows(r.v_query_grad, part(r.v_two, 0, wide))
-    second_sum = blk_sum(2, row_parts, r.near_rows, r.far_rows, rows)
-    second_sum.start()
-    load_second.wait()
-    second_sum.relay()
-    outer(grads.query, r.v_left, r.v_query_grad)
-    load_first = load(r.first_t, r.v_left)
-    reduces.query.start()
-    reduces.back.combine(1)
-    reduces.back.combine(0)
-    reduces.contract.combine()
-    reduces.contract.take(2)
-    pl.semaphore_signal(r.credit.at[0], inc=1, device_id=spot.part, device_id_type=MESH)
-    terms_share.relay()
-    load_one.wait()
-    second_sum.finish()
-    norm_back(second_sum, r.v_rows, 1, lambda here: hidden[here, :], keep_branch_after(turn_two, keep_branch))
-    load_frames = load(r.frames, r.v_rows)
-    turn_one = Turn(spot, r.v_branch, r.v_turn_one, r.tsend.at[1], r.trecv.at[1])
-    turn_one.start()
-    terms_share.finish()
-    load_keys.wait()
-    own_rows = pl.ds(pl.multiple_of((blk // 2) * TEXT, TEXT), TEXT)
-    terms = r.v_terms[own_rows, lanes(lax.rem(blk, 2), 2 * wide)]
-
-    def keys_tile(block):
-        product = t_dot(r.text[:, block], r.v_terms[own_rows, lanes(lax.rem(blk, 2), 2 * wide)])
-        grads.keys[block, :] = product.astype(BF16)
-
-    tiles(6, 256, keys_tile)
-    reduces.keys.start()
-    turn_one.finish()
-    second_sum.drain()
-    load_outward.wait()
-    back_cols(r.v_turn_one, part(r.v_one, 3 * wide, wide))
-    attended_sum = blk_sum(3, col_parts, r.near_cols, r.far_cols, length)
-    attended_sum.start()
-    load_attended.wait()
-    attended_sum.relay()
-    outer(grads.outward, r.v_right, r.v_turn_one)
-    reduces.outward.start()
-    r.v_text_part[...] = dot_t(terms, r.v_one[:, wide : 3 * wide]).astype(BF16)
-    text_rows = TEXT // 4
-    text_sum = blk_sum(4, row_piece(r.v_text_part, text_rows), r.near_text, r.far_text, text_rows)
-    text_sum.start()
-    text_sum.relay()
-    reduces.expand.take(0)
-    load_joint.wait()
-    attended_sum.finish()
-    merge(attended_sum, r.v_head_grad)
-
-    @pl.loop(0, 3)
-    def _(pair):
-        r.v_key_sum[...] = jnp.zeros_like(r.v_key_sum)
-        r.v_value_sum[...] = jnp.zeros_like(r.v_value_sum)
-
-        @pl.loop(0, 4)
-        def _(block):
-            here = pl.ds(pl.multiple_of(block * 128, 128), 128)
-            query = r.v_joint[here, lanes(pair, 128)]
-            key = r.v_joint[:, lanes(pair + 3, 128)]
-            value = r.v_joint[:, lanes(pair + 6, 128)]
-            head_grad = r.v_head_grad[here, lanes(pair, 128)]
-            keep = r.ids_row[...] <= r.ids_col[here, :]
+    def cross():
+        later.query_in.wait()
+        later.text_in.wait()
+        later.values_in.wait()
+        merge(crossed_sum, head_part)
+
+        @pl.loop(0, 3)
+        def _(pair):
+            query = cross_query[:, lanes(pair, 128)]
+            key = r.v_text[:, lanes(pair, 128)]
+            value = r.v_text[:, lanes(3 + pair, 128)]
+            head_grad = head_part[:, lanes(pair, 128)]
             results = []
             for side in (0, 1):
-                weights = soft(jnp.where(keep, dot_t(half(query, side), key) * 0.125, -1e30))
+                weights = soft(dot_t(half(query, side), key) * 0.125)
                 slope = dot_t(half(head_grad, side), value)
                 score = (weights * (slope - jnp.sum(slope * weights, axis=1, keepdims=True))).astype(BF16)
                 results.append(
-                    (dot(score, key), t_dot(score, query), t_dot(weights.astype(BF16), head_grad))
+                    (
+                        dot(score, key) * 0.125,
+                        t_dot(score, query) * 0.125,
+                        t_dot(weights.astype(BF16), head_grad),
+                    )
                 )
-            merged = [jnp.where(low, *item) for item in zip(*results)]
-            r.v_up[here, lanes(pair, 128)] = (merged[0] * 0.125).astype(BF16)
-            r.v_key_sum[...] += merged[1]
-            r.v_value_sum[...] += merged[2]
-
-        r.v_up[:, lanes(pair + 3, 128)] = (r.v_key_sum[...] * 0.125).astype(BF16)
-        r.v_up[:, lanes(pair + 6, 128)] = r.v_value_sum[...].astype(BF16)
-
-    stores = []
-
-    def store(item, goal):
-        size = goal.shape[1]
-        slot = len(stores) % 2
-        if len(stores) >= 2:
-            stores[-2].wait()
-        stage = r.v_slope.at[pl.ds(slot * 192, 192), pl.ds(0, size)]
-
-        def keep(here, value):
-            stage[here, :] = value
-
-        item.finish(keep)
-        copy = pltpu.make_async_copy(stage, goal, r.stored.at[len(stores)])
-        copy.start()
-        stores.append(copy)
-
-    reduces.back.cross()
-    reduces.keys.combine(1)
-    reduces.keys.combine(0)
-    store(reduces.contract, r.contract_out)
-    for k in (1, 2, 3):
-        pl.semaphore_signal(r.credit.at[1], inc=1, device_id=spot.z_peer(k), device_id_type=MESH)
-    reduces.contract.drain()
-    attended_sum.drain()
-    load_winward.wait()
-    load_first.wait()
-    joint_grad = part(r.v_up, 0, 3 * wide)
-    back_rows(joint_grad, part(r.v_two, wide, 3 * wide))
-    first_sum = blk_sum(5, row_parts, r.near_rows, r.far_rows, rows)
-    first_sum.start()
-
-    def inward_tile(block):
-        grads.inward[:, block] = dot(r.v_left[...], r.v_up[:, block]).astype(BF16)
-
-    tiles(3, 384, inward_tile)
-    pl.semaphore_wait(r.credit.at[0], 1)
-    reduces.inward.start()
-    first_sum.relay()
-    load_again = load(r.w_contract, r.v_one)
-    load_active = load(r.active, r.v_grad)
-    reduces.expand.take(3)
-    reduces.expand.take(1)
-    reduces.expand.combine()
-    reduces.expand.take(2)
-    load_frames.wait()
-    first_sum.finish()
-
-    def keep_frames(here, value):
-        hidden[here, :] = value
-
-    norm_back(first_sum, r.v_rows, 0, lambda here: hidden[here, :], keep_frames)
-    for who in (spot.sib, spot.opp):
-        pl.semaphore_signal(r.credit.at[2], inc=1, device_id=who, device_id_type=MESH)
-    frames_copy = pltpu.make_async_copy(hidden, r.frames_out, r.stored.at[8])
-    frames_copy.start()
-
-    for place in range(6):
-        r.v_norm_sum[place : place + 1, :] = jnp.sum(
-            r.v_norm_grads[place * 8 : place * 8 + 8, :], axis=0, keepdims=True
-        )
-    r.v_norm_sum[6:8, :] = jnp.zeros((2, width), F32)
+            merged = [jnp.where(low, *item).astype(BF16) for item in zip(*results)]
+            query_part[:, lanes(pair, 128)] = merged[0]
+            r.v_terms[0:TEXT, lanes(blk * 3 + pair, 128)] = merged[1]
+            r.v_terms[TEXT : 2 * TEXT, lanes(blk * 3 + pair, 128)] = merged[2]
+
+        later.joint = load(r.joint, r.v_joint)
+
+    def second_back():
+        later.query.wait()
+        crossed_sum.drain()
+        back_rows(query_part, part(r.v_two, 0, wide))
+
+    def query_grad():
+        later.second.wait()
+        outer(grads[query], r.v_left, query_part)
+        later.first = load(r.first_t, r.v_left)
+
+    def keys_grad():
+        def body(block):
+            product = t_dot(r.text[:, block], r.v_terms[own_rows, own_cols])
+            grads[keys][block, :] = product.astype(BF16)
+
+        tiles(6, 256, body)
+
+    def text_start():
+        later.keys.wait()
+        terms = r.v_terms[own_rows, own_cols]
+        r.v_text_part[...] = dot_t(terms, r.v_one[:, wide : 3 * wide]).astype(BF16)
+        text_sum.start()
+
+    def text_done():
+        text_sum.finish()
+        r.v_text_out[...] = text_sum.value(pl.ds(0, text_rows))
+        give(r.v_text_out, r.text_out)
+
+    def second_norm():
+        later.one.wait()
+        turn_two.drain()
+        norm_back(second_sum, 1, hidden, True)
+        later.frames = load(r.frames, r.v_rows)
+        turn_one.start()
+
+    def attended_back():
+        second_sum.drain()
+        later.outward.wait()
+        back_cols(turned_part, part(r.v_one, 3 * wide, wide))
+
+    def outward_grad():
+        later.attended.wait()
+        outer(grads[outward], r.v_right, turned_part)
+
+    def attend():
+        later.joint.wait()
+        merge(attended_sum, head_part)
+
+        @pl.loop(0, 3)
+        def _(pair):
+            r.v_key_sum[...] = jnp.zeros_like(r.v_key_sum)
+            r.v_value_sum[...] = jnp.zeros_like(r.v_value_sum)
+
+            @pl.loop(0, 4)
+            def _(block):
+                here = pl.ds(pl.multiple_of(block * 128, 128), 128)
+                query = r.v_joint[here, lanes(pair, 128)]
+                key = r.v_joint[:, lanes(pair + 3, 128)]
+                value = r.v_joint[:, lanes(pair + 6, 128)]
+                head_grad = head_part[here, lanes(pair, 128)]
+                keep = r.ids_row[...] <= r.ids_col[here, :]
+                results = []
+                for side in (0, 1):
+                    weights = soft(jnp.where(keep, dot_t(half(query, side), key) * 0.125, -1e30))
+                    slope = dot_t(half(head_grad, side), value)
+                    score = weights * (slope - jnp.sum(slope * weights, axis=1, keepdims=True))
+                    score = score.astype(BF16)
+                    results.append(
+                        (dot(score, key), t_dot(score, query), t_dot(weights.astype(BF16), head_grad))
+                    )
+                merged = [jnp.where(low, *item) for item in zip(*results)]
+                r.v_up[here, lanes(pair, 128)] = (merged[0] * 0.125).astype(BF16)
+                r.v_key_sum[...] += merged[1]
+                r.v_value_sum[...] += merged[2]
+
+            r.v_up[:, lanes(pair + 3, 128)] = (r.v_key_sum[...] * 0.125).astype(BF16)
+            r.v_up[:, lanes(pair + 6, 128)] = r.v_value_sum[...].astype(BF16)
+
+    def first_back():
+        attended_sum.drain()
+        later.inward.wait()
+        back_rows(joint_grad, part(r.v_two, wide, 3 * wide))
+
+    inward_done = []
+
+    def inward_grad(index):
+        if not inward_done:
+            later.first.wait()
+        inward_done.append(index)
+        reduces[index].drain()
+        product = dot(r.v_left[...], part(r.v_up, index * wide, wide)[...])
+        grads[inward + index][...] = product.astype(BF16)
 
     def norm_hop(number, who):
         return push(r.v_norm_sum, r.v_norm_in.at[number], r.nsend.at[number], r.nrecv.at[number], who)
 
-    norm_hop(0, spot.sib).start()
-    text_sum.finish()
-    r.v_text_out[...] = text_sum.value(pl.ds(0, text_rows))
-    text_copy = pltpu.make_async_copy(r.v_text_out, r.text_out, r.stored.at[9])
-    text_copy.start()
-    reduces.query.take(0)
-    reduces.query.take(3)
-    reduces.query.take(1)
-    reduces.query.take(2)
+    def first_norm():
+        later.again = load(r.w_contract, r.v_one)
+        later.active = load(r.active, r.v_grad)
+        later.frames.wait()
+        norm_back(first_sum, 0, hidden, False)
+        for who in (spot.sib, spot.opp):
+            pl.semaphore_signal(r.credit.at[6], inc=1, device_id=who, device_id_type=MESH)
+        give(hidden, r.frames_out)
+        for place in range(6):
+            r.v_norm_sum[place : place + 1, :] = jnp.sum(
+                r.v_norm_grads[place * 8 : place * 8 + 8, :], axis=0, keepdims=True
+            )
+        r.v_norm_sum[6:8, :] = jnp.zeros((2, width), F32)
+        norm_hop(0, spot.sib).start()
 
     def norm_step(number, who):
         norm_hop(number, who).wait()
         r.v_norm_sum[...] += r.v_norm_in[number]
 
-    norm_step(0, spot.sib)
-    norm_hop(1, spot.opp).start()
-    load_again.wait()
-    load_active.wait()
-    first_sum.drain()
-    back_rows(r.v_grad, r.v_one)
-    out_sum = blk_sum(6, row_parts, r.near_rows, r.far_rows, rows)
-    pl.semaphore_wait(r.credit.at[2], 2)
-    out_sum.start()
-    norm_step(1, spot.opp)
-    norm_hop(2, spot.part).start()
-    reduces.query.combine()
-    for goal in (0, 3, 1, 2):
-        reduces.outward.take(goal)
-    out_sum.relay()
-    reduces.keys.cross()
-    norm_step(2, spot.part)
-    for k in (1, 2, 3):
-        norm_hop(2 + k, spot.z_peer(k)).start()
-    reduces.outward.combine()
-    pl.semaphore_wait(r.credit.at[1], 3)
-    for goal in (0, 3):
-        reduces.inward.take(goal)
-    out_sum.finish()
-    turn_one.drain()
-
-    @pl.loop(0, rows // 16)
-    def _(index):
-        here = pl.ds(pl.multiple_of(index * 16, 16), 16)
-        r.v_branch[here, :] = (out_sum.value(here) + r.v_two_rows[here, :].astype(F32)).astype(BF16)
-
-    block_copy = pltpu.make_async_copy(r.v_branch, r.block_out, r.stored.at[10])
-    block_copy.start()
-    store(reduces.expand, r.expand_out)
-    store(reduces.back, r.returning_out)
-    reduces.inward.take(1)
-    reduces.inward.take(2)
-    reduces.inward.combine()
-    store(reduces.query, r.querying_out)
-    store(reduces.outward, r.outward_out)
-    store(reduces.keys, r.keying_out)
-    for k in (1, 2, 3):
-        norm_hop(2 + k, spot.z_peer(k)).wait()
-    r.v_norm_sum[...] += r.v_norm_in[3] + r.v_norm_in[4] + r.v_norm_in[5]
-    norm_copy = pltpu.make_async_copy(r.v_norm_sum, r.norm_out, r.stored.at[11])
-    norm_copy.start()
-
-    out_sum.drain()
-    inward_sum = r.v_part.at[pl.ds(0, 192), pl.ds(0, 3 * wide)]
-
-    def keep_inward(here, value):
-        inward_sum[here, :] = value.astype(BF16)
-
-    reduces.inward.finish(keep_inward)
+    def norm_sib():
+        norm_step(0, spot.sib)
+        norm_hop(1, spot.opp).start()
+
+    def norm_opp():
+        norm_step(1, spot.opp)
+        norm_hop(2, spot.part).start()
+
+    def norm_part():
+        norm_step(2, spot.part)
+        for k in (1, 2, 3):
+            norm_hop(2 + k, spot.z_peer(k)).start()
+
+    def norm_peers():
+        for k in (1, 2, 3):
+            norm_hop(2 + k, spot.z_peer(k)).wait()
+        r.v_norm_sum[...] += r.v_norm_in[3] + r.v_norm_in[4] + r.v_norm_in[5]
+        give(r.v_norm_sum, r.norm_out)
+
+    def out_product():
+        later.again.wait()
+        later.active.wait()
+        first_sum.drain()
+        back_rows(r.v_grad, r.v_one)
+
+    def out_start():
+        pl.semaphore_wait(r.credit.at[6], 2)
+        out_sum.start()
+
+    def out_done():
+        turn_one.drain()
+
+        @pl.loop(0, rows // 16)
+        def _(index):
+            here = pl.ds(pl.multiple_of(index * 16, 16), 16)
+            r.v_branch[here, :] = (out_sum.value(here) + r.v_two_rows[here, :].astype(F32)).astype(BF16)
+
+        give(r.v_branch, r.block_out)
+
+    steps = (
+        up, third_back, third_sum.start, third_sum.relay, third_sum.finish,
+        *(functools.partial(expand_grad, index) for index in range(4)),
+        third_norm, turn_two.finish, crossed_back,
+        crossed_sum.start, crossed_sum.relay, crossed_sum.finish,
+        back_grad, cross, terms_share.start, terms_share.relay, terms_share.finish,
+        second_back, second_sum.start, second_sum.relay, second_sum.finish,
+        query_grad, keys_grad, text_start, text_sum.relay, text_done,
+        second_norm, turn_one.finish, attended_back,
+        attended_sum.start, attended_sum.relay, attended_sum.finish,
+        outward_grad, attend, first_back, first_sum.start, first_sum.relay, first_sum.finish,
+        *(functools.partial(inward_grad, index) for index in range(3)),
+        first_norm, norm_sib, norm_opp, norm_part, norm_peers,
+        out_product, out_start, out_sum.relay, out_sum.finish, out_done,
+    )
+    goals = [r.contract_out.at[:, index * wide : (index + 1) * wide] for index in range(4)]
+    goals += [r.expand_out.at[:, index * wide : (index + 1) * wide] for index in range(4)]
+    goals += [r.returning_out, r.keying_out, r.querying_out, r.outward_out]
+    stores = []
+
+    def store(number):
+        goal = goals[number]
+        slot = len(stores)
+        if slot >= 4:
+            stores[slot - 4].wait()
+        columns = pl.ds(slot // 2 % 2 * 2 * wide, goal.shape[1])
+        stage = r.v_slope.at[pl.ds(slot % 2 * 192, 192), columns]
+
+        def keep(here, value):
+            stage[here, :] = value
+
+        reduces[number].finish(keep)
+        stores.append(give(stage, goal))
 
     def inward_copy(kind):
         index = kind * 4 + blk
-        owner, place = index // 3, lax.rem(index, 3)
-        src = inward_sum.at[:, kind * wide : (kind + 1) * wide]
-        return owner, place, src, r.v_inward_in.at[:, lanes(place, wide)]
-
-    for kind in range(3):
+        src = r.v_left.at[kind * 192 : (kind + 1) * 192, 0:wide]
+        place = lax.rem(index, 3)
+        lines = pl.ds(pl.multiple_of(place * 192, 192), 192)
+        return index // 3, place, src, r.v_right.at[lines, 0:wide]
+
+    def hand_over(kind):
         owner, place, src, dst = inward_copy(kind)
+
+        def keep(here, value):
+            src[here, :] = value.astype(BF16)
+
+        reduces[inward + kind].finish(keep)
 
         @pl.when(owner == blk)
         def _():
@@ -1786,8 +1804,43 @@
         def _():
             push(src, dst, r.asend.at[kind], r.arecv.at[place], (spot.grp, owner)).start()
 
+    taken = [0] * len(reduces)
+    for kind, number, *rest in BACKWARD_ORDER:
+        if kind == 5:
+            steps[number]()
+            continue
+        item = reduces[number]
+        if kind == 0:
+            if number >= inward:
+                pl.semaphore_wait(r.credit.at[number - inward], 1)
+            item.start()
+        elif kind == 1:
+            if number < 4 and sum(taken) == 0:
+                for copy in later.own:
+                    copy.wait()
+            if number >= inward and taken[number] == 0:
+                pl.semaphore_wait(r.credit.at[3 + number - inward], 3)
+            item.take(*rest)
+            taken[number] += 1
+            if number < 3 and taken[number] == 4:
+                pl.semaphore_signal(r.credit.at[number], inc=1, device_id=spot.part, device_id_type=MESH)
+        elif kind == 2:
+            item.pass_on(*rest)
+        elif kind == 3:
+            item.cross()
+        elif number >= inward:
+            hand_over(number - inward)
+        else:
+            store(number)
+            for k in (1, 2, 3) if number < 3 else ():
+                pl.semaphore_signal(
+                    r.credit.at[3 + number], inc=1, device_id=spot.z_peer(k), device_id_type=MESH
+                )
+    for copy in stores[-4:]:
+        copy.wait()
     for place in range(3):
-        dst = r.v_inward_in.at[:, place * wide : (place + 1) * wide]
+        here = slice(place * wide, (place + 1) * wide)
+        dst = r.v_right.at[place * 192 : (place + 1) * 192, 0:wide]
         home = lax.rem(blk * 3 + place, 4)
 
         @pl.when(home == blk)
@@ -1798,17 +1851,14 @@
         def _():
             push(dst, dst, r.asend.at[0], r.arecv.at[place], spot.sib).wait_recv()
 
-    for copy in stores[-2:]:
-        copy.wait()
-    final = r.v_slope.at[pl.ds(0, 192), pl.ds(0, 3 * wide)]
-
-    @pl.loop(0, 192 // 16)
-    def _(index):
-        here = pl.ds(pl.multiple_of(index * 16, 16), 16)
-        final[here, :] = r.v_inward_in[here, :].astype(F32)
-
-    inward_done = pltpu.make_async_copy(final, r.inward_out, r.stored.at[12])
-    inward_done.start()
+        stage = r.v_slope.at[pl.ds(0, 192), pl.ds(place * wide, wide)]
+
+        @pl.loop(0, 192 // 16)
+        def _(index):
+            lines = pl.ds(pl.multiple_of(index * 16, 16), 16)
+            stage[lines, :] = dst[lines, :].astype(F32)
+
+        give(stage, r.inward_out.at[:, here])
     for kind in range(3):
         owner, place, src, dst = inward_copy(kind)
 
@@ -1816,18 +1866,14 @@
         def _():
             push(src, dst, r.asend.at[kind], r.arecv.at[place], (spot.grp, owner)).wait_send()
 
-    for item in vars(reduces).values():
-        if item is not reduces.contract:
-            item.drain()
+    for item in reduces[3:]:
+        item.drain()
     terms_share.drain()
     text_sum.drain()
-    for copy in (frames_copy, text_copy, block_copy, norm_copy, inward_done):
-        copy.wait()
-
-
-def keep_branch_after(turn, keep):
-    turn.drain()
-    return keep
+    out_sum.drain()
+    for copy in copies:
+        if all(copy is not item for item in stores):
+            copy.wait()
 
 
 def backward(ahead, frames, text, table, incoming):
@@ -1864,10 +1910,6 @@
         v_part=(square, BF16),
         v_slope=(square, F32),
         v_joint=((length, 3 * wide), BF16),
-        v_query_grad=(strip, BF16),
-        v_head_grad=(strip, BF16),
-        v_turn_one=(strip, BF16),
-        v_turn_two=(strip, BF16),
         v_text=((TEXT, 2 * wide), BF16),
         v_terms=((2 * TEXT, width), BF16),
         v_text_part=((TEXT, width), BF16),
@@ -1887,27 +1929,26 @@
         v_norm_in=((6, 8, width), F32),
         v_key_sum=((length, 128), F32),
         v_value_sum=((length, 128), F32),
-        v_inward_in=((shard, 3 * wide), BF16),
     )
     vmem.update(
         y_contract=((4, shard, feed), BF16),
         y_expand=((4, shard, feed), BF16),
         y_back=((1, shard, wide), BF16),
-        y_keys=((1, shard, 2 * wide), BF16),
+        y_keys=((4, shard, 2 * wide), BF16),
         y_query=((4, shard, wide), BF16),
-        y_outward=((4, shard, wide), BF16),
-        z_contract=((4, shard, feed), BF16),
-        z_expand=((4, shard, feed), BF16),
-        z_back=((8, shard, wide), BF16),
-        z_keys=((8, shard, 2 * wide), BF16),
-        z_query=((4, shard, wide), BF16),
-        z_outward=((4, shard, wide), BF16),
+        y_outward=((1, shard, wide), BF16),
+        z_contract=((5, shard, feed), BF16),
+        z_expand=((5, shard, feed), BF16),
+        z_back=((10, shard, wide), BF16),
+        z_keys=((5, shard, 2 * wide), BF16),
+        z_query=((5, shard, wide), BF16),
+        z_outward=((10, shard, wide), BF16),
     )
     sems = dict(
-        ysend=(7, 4),
-        yrecv=(7, 4),
-        zsend=(7, 8),
-        zrecv=(7, 8),
+        ysend=(15, 4),
+        yrecv=(15, 4),
+        zsend=(15, 8),
+        zrecv=(15, 10),
         bsend=(7, 3),
         brecv=(7, 3),
         tsend=(2, 3),
@@ -1919,12 +1960,44 @@
         asend=(3,),
         arecv=(3,),
         local=(32,),
-        stored=(16,),
+        stored=(24,),
     )
     inner = dict(text=text, ids_col=ids_col, ids_row=ids_row)
     outer = dict(frames=frames, incoming=incoming, **vars(ahead))
     del outer["aligned"]
-    return run_kernel(backward_kernel, 2, inner, outer, out, vmem, sems, dict(credit=(3,)))
+    return run_kernel(backward_kernel, 2, inner, outer, out, vmem, sems, dict(credit=(7,)))
+
+
+def closing_kernel(count, *refs):
+    given, out, held, sems = refs[:count], refs[count : 2 * count], refs[2 * count : -1], refs[-1]
+    loads = [
+        pltpu.make_async_copy(src, dst, sems.at[0, index])
+        for index, (src, dst) in enumerate(zip(given, held))
+    ]
+    stores = [
+        pltpu.make_async_copy(src, dst, sems.at[1, index])
+        for index, (src, dst) in enumerate(zip(held, out))
+    ]
+    for copy in loads:
+        copy.start()
+    for load, store in zip(loads, stores):
+        load.wait()
+        store.start()
+    for copy in stores:
+        copy.wait()
+
+
+def closing(*items):
+    anywhere = pl.BlockSpec(memory_space=pl.ANY)
+    count = len(items)
+    return pl.pallas_call(
+        functools.partial(closing_kernel, count),
+        out_shape=[jax.ShapeDtypeStruct(item.shape, item.dtype) for item in items],
+        in_specs=[anywhere] * count,
+        out_specs=[anywhere] * count,
+        scratch_shapes=[pltpu.VMEM(item.shape, item.dtype) for item in items]
+        + [pltpu.SemaphoreType.DMA((2, count))],
+    )(*items)
 
 
 def tp_shards(
@@ -1962,17 +2035,40 @@
     share = gains.shape[1]
     place = (lax.axis_index("grp") * lax.axis_size("blk") + lax.axis_index("blk")) * share
     norm_grads = lax.dynamic_slice_in_dim(done.norm_out, place, share, 1)
+    (
+        contract_grad,
+        expand_grad,
+        returning_grad,
+        keying_grad,
+        querying_grad,
+        outward_grad,
+        inward_grad,
+        frames_grad,
+        block_out,
+        text_grad,
+    ) = closing(
+        done.contract_out,
+        done.expand_out,
+        done.returning_out,
+        done.keying_out,
+        done.querying_out,
+        done.outward_out,
+        done.inward_out,
+        done.frames_out,
+        done.block_out,
+        done.text_out,
+    )
     return (
-        done.block_out[None],
-        done.frames_out[None],
-        done.text_out[None],
-        done.inward_out,
-        done.outward_out,
-        done.querying_out,
-        done.keying_out,
-        done.returning_out,
-        done.expand_out,
-        done.contract_out.T,
+        block_out[None],
+        frames_grad[None],
+        text_grad[None],
+        inward_grad,
+        outward_grad,
+        querying_grad,
+        keying_grad,
+        returning_grad,
+        expand_grad,
+        contract_grad.T,
         norm_grads[:3],
         norm_grads[3:6],
     )

time: 462 us -> 444 us (0.961); the launches traced: 455 us -> 444 us
  local copies, waits for them, and re-layouts: 13.4 us -> 2.92 us
    unnamed x26 -> x0, local copies, waits for them, and re-layouts: 10.4 us -> none
    pallas_call x2, Pallas kernels: 439 us -> 433 us  [run_kernel(): pl.pallas_call(functools.partial(kernel, names), out_shape=[jax.ShapeDtyp...]
    pallas_call x0 -> x1, Pallas kernels: none -> 4.78 us  [closing(): pl.pallas_call(functools.partial(closing_kernel, count), out_shape=[jax.S...]
where the time goes in v4:
time: 444 us
  Pallas kernels  438 us (99%)
    pallas_call x2, Pallas kernels, run_kernel(): pl.pallas_call(functools.partial(kernel, names), out_shape=[jax.ShapeDtyp...  433 us

profile of v4, /device:TPU:0, one launch (start us, length us, event | category | flops | bytes accessed | tf_op | source)
XLA Modules:
  0.0 443.5 jit_solution(11587664373426800774)
XLA Ops:
  0.6 0.7 multiply_bitcast_fusion
  1.3 0.1 iota_add_fusion
  1.4 0.9 add.55.refs_1_
  2.3 0.7 add.52.refs_2_
  2.9 1.3 fusion.5.refs_4_
  4.2 202.8 %shard_map.220 = (bf16[1536,384]{1,0:T(8,128)(2,1)}, bf16[1536,1152]{1,0:T(8,128)(2,1)}, bf16[1536,384]{1,0:T(8,128)(2,1)}, bf16[1536,768]{1,0:T(8,128)(2,1)}, b...) custom-call(bf16[64,1536]{1,0:T(8,128)(2,1)} %bitcast.14, ...), custom_call_target="tpu_custom_call" | custom-call | tf_op jit(solution)/shard_map/pallas_call | solution.py:997
  207.1 230.3 %shard_map.221 = (f32[192,1536]{1,0:T(8,128)}, f32[192,1536]{1,0:T(8,128)}, f32[192,384]{1,0:T(8,128)}, f32[192,768]{1,0:T(8,128)}, f32[192,384]{1,0:T(8,128)}, ...) custom-call(bf16[64,1536]{1,0:T(8,128)(2,1)} %bitcast.15, ...), custom_call_target="tpu_custom_call" | custom-call | tf_op jit(solution)/shard_map/pallas_call | solution.py:997
  437.4 4.8 %shard_map.222 = (f32[192,1536]{1,0:T(8,128)}, f32[192,1536]{1,0:T(8,128)}, f32[192,384]{1,0:T(8,128)}, f32[192,768]{1,0:T(8,128)}, f32[192,384]{1,0:T(8,128)}, ...) custom-call(f32[192,1536]{1,0:T(8,128)} %get-tuple-element.77.refs_0, ...), custom_call_target="tpu_custom_call" | custom-call | tf_op jit(solution)/shard_map/pallas_call | solution.py:1993
  442.2 0.8 constant_dynamic-slice_fusion
  442.9 0.6 fusion.6

commit v5 on v4

--- a/solution.py
+++ b/solution.py
@@ -1307,42 +1307,42 @@
 
 
 BACKWARD_ORDER = (
-    (0, 0), (0, 1), (0, 2), (0, 3), (5, 0), (1, 0, 0), (5, 1), (1, 0, 3), (5, 5), (5, 2), (5, 6),
-    (1, 0, 1), (0, 4), (0, 5), (2, 0, 0, 0, 2), (5, 7), (0, 6), (5, 8), (0, 7), (1, 0, 2),
-    (2, 0, 3, 0, 1), (5, 3), (2, 0, 1, 0, 2), (1, 1, 0), (2, 0, 0, 0, 1), (1, 1, 3),
-    (2, 0, 3, 0, 2), (2, 1, 0, 0, 2), (2, 0, 2, 0, 1), (1, 1, 1), (5, 4), (2, 1, 3, 0, 1),
-    (1, 1, 2), (4, 0), (5, 9), (2, 1, 1, 0, 2), (2, 1, 0, 0, 1), (1, 2, 0), (2, 1, 3, 0, 2),
-    (2, 1, 2, 0, 1), (1, 2, 3), (5, 10), (2, 2, 0, 0, 2), (1, 2, 1), (5, 11), (5, 12), (5, 15),
-    (0, 8), (4, 1), (2, 2, 3, 0, 1), (1, 2, 2), (5, 13), (2, 2, 0, 0, 1), (2, 2, 1, 0, 2),
-    (1, 3, 0), (2, 2, 3, 0, 2), (2, 8, 3, 1, 1), (2, 8, 0, 1, 2), (1, 3, 3), (2, 8, 3, 0, 1),
-    (2, 8, 0, 0, 2), (1, 3, 1), (5, 14), (2, 8, 3, 1, 2), (2, 8, 0, 1, 1), (2, 8, 1, 1, 2),
-    (1, 3, 2), (5, 16), (5, 17), (2, 8, 0, 0, 1), (2, 8, 1, 0, 2), (2, 8, 3, 0, 2), (1, 4, 0),
-    (2, 8, 2, 1, 1), (5, 20), (5, 21), (1, 4, 3), (5, 24), (5, 18), (2, 8, 2, 0, 1), (1, 4, 1),
-    (5, 19), (5, 22), (5, 25), (3, 8), (0, 9), (2, 2, 2, 0, 1), (5, 26), (2, 3, 3, 0, 1),
-    (2, 3, 0, 0, 2), (5, 27), (1, 5, 0), (1, 4, 2), (4, 2), (2, 3, 1, 0, 2), (1, 5, 3), (5, 28),
-    (5, 23), (2, 3, 0, 0, 1), (2, 3, 3, 0, 2), (2, 3, 2, 0, 1), (5, 29), (1, 5, 1),
-    (2, 4, 0, 0, 2), (2, 4, 3, 0, 1), (1, 5, 2), (4, 3), (2, 4, 1, 0, 2), (1, 6, 0), (5, 30),
-    (5, 35), (2, 4, 0, 0, 1), (2, 4, 3, 0, 2), (2, 4, 2, 0, 1), (2, 5, 0, 0, 2), (5, 31),
-    (5, 32), (0, 11), (1, 6, 3), (2, 5, 3, 0, 1), (1, 6, 1), (5, 33), (2, 5, 0, 0, 1), (4, 4),
-    (2, 5, 1, 0, 2), (1, 6, 2), (2, 5, 3, 0, 2), (2, 5, 2, 0, 1), (1, 7, 0), (2, 6, 0, 0, 2),
-    (2, 11, 3, 1, 1), (1, 7, 3), (4, 5), (5, 34), (2, 11, 0, 1, 2), (2, 11, 3, 0, 1), (1, 7, 1),
-    (5, 36), (2, 11, 2, 0, 1), (2, 11, 0, 0, 2), (2, 6, 0, 0, 1), (2, 11, 3, 1, 2),
-    (2, 11, 3, 0, 2), (2, 11, 1, 1, 2), (2, 11, 1, 0, 2), (2, 11, 2, 1, 1), (2, 11, 0, 1, 1),
-    (2, 6, 3, 0, 1), (1, 9, 0), (1, 7, 2), (4, 8), (5, 41), (0, 12), (5, 42), (0, 13), (5, 43),
-    (2, 11, 0, 0, 1), (5, 37), (5, 38), (1, 9, 3), (2, 7, 0, 0, 2), (2, 7, 3, 0, 1),
-    (2, 6, 2, 0, 1), (2, 6, 1, 0, 2), (0, 14), (5, 39), (3, 11), (0, 10), (2, 7, 1, 0, 2),
-    (2, 6, 3, 0, 2), (1, 9, 1), (2, 7, 2, 0, 1), (2, 7, 3, 0, 2), (2, 9, 0, 0, 2),
-    (2, 7, 0, 0, 1), (1, 12, 0), (4, 6), (1, 9, 2), (2, 9, 3, 0, 1), (5, 40), (4, 7), (1, 12, 3),
-    (5, 44), (1, 12, 1), (5, 49), (5, 50), (5, 45), (2, 9, 1, 0, 2), (2, 9, 0, 0, 1),
-    (2, 12, 0, 0, 2), (1, 13, 0), (5, 51), (1, 12, 2), (5, 46), (2, 9, 2, 0, 1), (2, 9, 3, 0, 2),
-    (1, 13, 3), (2, 12, 3, 0, 1), (5, 47), (1, 13, 1), (2, 12, 1, 0, 2), (2, 12, 0, 0, 1),
-    (5, 52), (5, 53), (2, 12, 2, 0, 1), (1, 14, 0), (1, 13, 2), (2, 13, 0, 0, 2), (4, 9),
-    (5, 48), (2, 13, 3, 0, 1), (2, 12, 3, 0, 2), (1, 14, 3), (2, 13, 1, 0, 2), (1, 14, 1),
-    (4, 12), (2, 13, 0, 0, 1), (2, 13, 3, 0, 2), (2, 13, 2, 0, 1), (2, 14, 0, 0, 2), (1, 14, 2),
-    (2, 14, 3, 0, 1), (4, 11), (4, 13), (2, 14, 0, 0, 1), (2, 14, 1, 0, 2), (1, 10, 0),
-    (2, 14, 2, 0, 1), (2, 14, 3, 0, 2), (1, 10, 3), (2, 10, 0, 0, 2), (1, 10, 1), (4, 14),
-    (2, 10, 3, 0, 1), (1, 10, 2), (2, 10, 0, 0, 1), (2, 10, 1, 0, 2), (2, 10, 3, 0, 2),
-    (2, 10, 2, 0, 1), (4, 10),
+    (0, 0), (0, 1), (0, 2), (0, 3), (5, 0), (1, 0, 0), (1, 0, 3), (5, 1), (5, 2), (1, 0, 1),
+    (5, 5), (0, 4), (5, 6), (1, 0, 2), (2, 0, 0, 0, 2), (0, 5), (2, 0, 3, 0, 1), (5, 7), (5, 3),
+    (5, 8), (0, 6), (0, 7), (1, 1, 0), (2, 0, 1, 0, 2), (1, 1, 3), (2, 0, 0, 0, 1),
+    (2, 0, 2, 0, 1), (2, 0, 3, 0, 2), (1, 1, 1), (2, 1, 0, 0, 2), (2, 1, 3, 0, 1), (1, 1, 2),
+    (4, 0), (2, 1, 1, 0, 2), (1, 2, 0), (2, 1, 0, 0, 1), (5, 4), (5, 9), (2, 1, 3, 0, 2),
+    (2, 1, 2, 0, 1), (1, 2, 3), (2, 2, 0, 0, 2), (1, 2, 1), (2, 2, 3, 0, 1), (1, 2, 2), (4, 1),
+    (5, 10), (2, 2, 1, 0, 2), (2, 2, 0, 0, 1), (1, 3, 0), (5, 15), (5, 11), (2, 2, 3, 0, 2),
+    (2, 2, 2, 0, 1), (5, 12), (1, 3, 3), (0, 8), (2, 3, 0, 0, 2), (1, 3, 1), (5, 13), (4, 2),
+    (2, 3, 3, 0, 1), (2, 3, 0, 0, 1), (2, 8, 0, 1, 2), (2, 8, 3, 1, 1), (2, 8, 0, 0, 2),
+    (1, 4, 0), (1, 3, 2), (2, 8, 0, 1, 1), (2, 3, 3, 0, 2), (2, 8, 1, 1, 2), (2, 8, 3, 0, 1),
+    (1, 4, 3), (2, 8, 3, 1, 2), (2, 8, 1, 0, 2), (2, 8, 0, 0, 1), (1, 4, 1), (5, 14),
+    (2, 8, 3, 0, 2), (1, 4, 2), (5, 16), (5, 17), (2, 8, 2, 1, 1), (5, 20), (2, 8, 2, 0, 1),
+    (2, 3, 1, 0, 2), (5, 21), (1, 5, 0), (1, 5, 3), (5, 24), (0, 10), (2, 4, 0, 0, 2), (1, 5, 1),
+    (5, 18), (5, 22), (3, 8), (5, 19), (2, 3, 2, 0, 1), (5, 26), (1, 5, 2), (5, 25), (0, 9),
+    (5, 27), (2, 4, 3, 0, 1), (2, 4, 1, 0, 2), (2, 4, 0, 0, 1), (1, 6, 0), (4, 3), (1, 6, 3),
+    (2, 4, 3, 0, 2), (2, 4, 2, 0, 1), (2, 5, 0, 0, 2), (1, 6, 1), (5, 28), (2, 5, 3, 0, 1),
+    (2, 5, 1, 0, 2), (5, 23), (1, 6, 2), (5, 29), (2, 5, 0, 0, 1), (4, 4), (1, 7, 0),
+    (2, 5, 3, 0, 2), (2, 5, 2, 0, 1), (2, 6, 0, 0, 2), (1, 7, 3), (2, 6, 1, 0, 2),
+    (2, 6, 3, 0, 1), (1, 7, 1), (5, 30), (5, 31), (5, 32), (5, 35), (4, 5), (1, 7, 2), (0, 11),
+    (2, 6, 0, 0, 1), (2, 6, 3, 0, 2), (2, 6, 2, 0, 1), (2, 7, 0, 0, 2), (5, 33), (1, 10, 0),
+    (2, 7, 3, 0, 1), (2, 7, 1, 0, 2), (1, 10, 3), (4, 6), (2, 7, 0, 0, 1), (1, 10, 1),
+    (2, 7, 3, 0, 2), (2, 7, 2, 0, 1), (2, 11, 0, 1, 2), (1, 10, 2), (2, 11, 3, 1, 1),
+    (2, 11, 0, 0, 2), (4, 8), (5, 34), (2, 11, 0, 1, 1), (2, 11, 3, 0, 1), (2, 11, 1, 1, 2),
+    (5, 36), (2, 11, 3, 1, 2), (2, 10, 1, 0, 2), (2, 11, 3, 0, 2), (2, 10, 0, 0, 2),
+    (2, 11, 2, 1, 1), (2, 11, 0, 0, 1), (2, 10, 3, 0, 1), (2, 11, 1, 0, 2), (2, 11, 2, 0, 1),
+    (1, 9, 0), (4, 7), (1, 9, 3), (1, 9, 1), (5, 41), (5, 43), (3, 11), (2, 10, 2, 0, 1),
+    (0, 12), (5, 37), (5, 38), (5, 42), (2, 10, 3, 0, 2), (2, 10, 0, 0, 1), (0, 13), (0, 14),
+    (2, 9, 0, 0, 2), (1, 9, 2), (5, 39), (2, 9, 3, 0, 1), (4, 11), (1, 12, 0), (4, 10),
+    (2, 9, 1, 0, 2), (1, 12, 3), (2, 9, 0, 0, 1), (1, 12, 1), (2, 9, 3, 0, 2), (1, 12, 2),
+    (2, 9, 2, 0, 1), (2, 12, 0, 0, 2), (5, 40), (5, 44), (2, 12, 3, 0, 1), (1, 13, 0),
+    (2, 12, 1, 0, 2), (5, 49), (5, 45), (5, 50), (2, 12, 2, 0, 1), (2, 13, 0, 0, 2), (1, 13, 3),
+    (2, 12, 0, 0, 1), (1, 13, 1), (4, 9), (1, 13, 2), (2, 12, 3, 0, 2), (2, 13, 3, 0, 1),
+    (5, 51), (5, 46), (2, 13, 1, 0, 2), (1, 14, 0), (2, 13, 0, 0, 1), (1, 14, 3),
+    (2, 13, 2, 0, 1), (2, 13, 3, 0, 2), (4, 12), (2, 14, 0, 0, 2), (5, 47), (2, 14, 3, 0, 1),
+    (1, 14, 1), (1, 14, 2), (4, 13), (2, 14, 0, 0, 1), (5, 52), (5, 53), (2, 14, 3, 0, 2),
+    (2, 14, 2, 0, 1), (2, 14, 1, 0, 2), (5, 48), (4, 14),
 )
 
 

time: 444 us -> 426 us (0.959); the launches traced: 444 us -> 418 us
  Pallas kernels: 438 us -> 412 us
    pallas_call x2, Pallas kernels: 433 us -> 408 us  [run_kernel(): pl.pallas_call(functools.partial(kernel, names), out_shape=[jax.ShapeDtyp...]
where the time goes in v5:
time: 426 us; the launch traced here: 418 us
  Pallas kernels  412 us (97%)
    pallas_call x2, Pallas kernels, run_kernel(): pl.pallas_call(functools.partial(kernel, names), out_shape=[jax.ShapeDtyp...  408 us

profile of v5, /device:TPU:0, one launch (start us, length us, event | category | flops | bytes accessed | tf_op | source)
XLA Modules:
  0.0 418.1 jit_solution(4310662650176973849)
XLA Ops:
  0.6 0.7 multiply_bitcast_fusion
  1.3 0.1 iota_add_fusion
  1.4 0.9 add.55.refs_1_
  2.3 0.7 add.52.refs_2_
  2.9 1.3 fusion.5.refs_4_
  4.2 202.8 %shard_map.220 = (bf16[1536,384]{1,0:T(8,128)(2,1)}, bf16[1536,1152]{1,0:T(8,128)(2,1)}, bf16[1536,384]{1,0:T(8,128)(2,1)}, bf16[1536,768]{1,0:T(8,128)(2,1)}, b...) custom-call(bf16[64,1536]{1,0:T(8,128)(2,1)} %bitcast.14, ...), custom_call_target="tpu_custom_call" | custom-call | tf_op jit(solution)/shard_map/pallas_call | solution.py:997
  207.1 204.9 %shard_map.221 = (f32[192,1536]{1,0:T(8,128)}, f32[192,1536]{1,0:T(8,128)}, f32[192,384]{1,0:T(8,128)}, f32[192,768]{1,0:T(8,128)}, f32[192,384]{1,0:T(8,128)}, ...) custom-call(bf16[64,1536]{1,0:T(8,128)(2,1)} %bitcast.15, ...), custom_call_target="tpu_custom_call" | custom-call | tf_op jit(solution)/shard_map/pallas_call | solution.py:997
  412.0 4.8 %shard_map.222 = (f32[192,1536]{1,0:T(8,128)}, f32[192,1536]{1,0:T(8,128)}, f32[192,384]{1,0:T(8,128)}, f32[192,768]{1,0:T(8,128)}, f32[192,384]{1,0:T(8,128)}, ...) custom-call(f32[192,1536]{1,0:T(8,128)} %get-tuple-element.77.refs_0, ...), custom_call_target="tpu_custom_call" | custom-call | tf_op jit(solution)/shard_map/pallas_call | solution.py:1993
  416.7 0.8 constant_dynamic-slice_fusion
  417.5 0.6 fusion.6

commit v6 on v5

--- a/solution.py
+++ b/solution.py
@@ -1308,41 +1308,40 @@
 
 BACKWARD_ORDER = (
     (0, 0), (0, 1), (0, 2), (0, 3), (5, 0), (1, 0, 0), (1, 0, 3), (5, 1), (5, 2), (1, 0, 1),
-    (5, 5), (0, 4), (5, 6), (1, 0, 2), (2, 0, 0, 0, 2), (0, 5), (2, 0, 3, 0, 1), (5, 7), (5, 3),
-    (5, 8), (0, 6), (0, 7), (1, 1, 0), (2, 0, 1, 0, 2), (1, 1, 3), (2, 0, 0, 0, 1),
-    (2, 0, 2, 0, 1), (2, 0, 3, 0, 2), (1, 1, 1), (2, 1, 0, 0, 2), (2, 1, 3, 0, 1), (1, 1, 2),
-    (4, 0), (2, 1, 1, 0, 2), (1, 2, 0), (2, 1, 0, 0, 1), (5, 4), (5, 9), (2, 1, 3, 0, 2),
-    (2, 1, 2, 0, 1), (1, 2, 3), (2, 2, 0, 0, 2), (1, 2, 1), (2, 2, 3, 0, 1), (1, 2, 2), (4, 1),
-    (5, 10), (2, 2, 1, 0, 2), (2, 2, 0, 0, 1), (1, 3, 0), (5, 15), (5, 11), (2, 2, 3, 0, 2),
-    (2, 2, 2, 0, 1), (5, 12), (1, 3, 3), (0, 8), (2, 3, 0, 0, 2), (1, 3, 1), (5, 13), (4, 2),
-    (2, 3, 3, 0, 1), (2, 3, 0, 0, 1), (2, 8, 0, 1, 2), (2, 8, 3, 1, 1), (2, 8, 0, 0, 2),
-    (1, 4, 0), (1, 3, 2), (2, 8, 0, 1, 1), (2, 3, 3, 0, 2), (2, 8, 1, 1, 2), (2, 8, 3, 0, 1),
-    (1, 4, 3), (2, 8, 3, 1, 2), (2, 8, 1, 0, 2), (2, 8, 0, 0, 1), (1, 4, 1), (5, 14),
-    (2, 8, 3, 0, 2), (1, 4, 2), (5, 16), (5, 17), (2, 8, 2, 1, 1), (5, 20), (2, 8, 2, 0, 1),
-    (2, 3, 1, 0, 2), (5, 21), (1, 5, 0), (1, 5, 3), (5, 24), (0, 10), (2, 4, 0, 0, 2), (1, 5, 1),
-    (5, 18), (5, 22), (3, 8), (5, 19), (2, 3, 2, 0, 1), (5, 26), (1, 5, 2), (5, 25), (0, 9),
-    (5, 27), (2, 4, 3, 0, 1), (2, 4, 1, 0, 2), (2, 4, 0, 0, 1), (1, 6, 0), (4, 3), (1, 6, 3),
-    (2, 4, 3, 0, 2), (2, 4, 2, 0, 1), (2, 5, 0, 0, 2), (1, 6, 1), (5, 28), (2, 5, 3, 0, 1),
-    (2, 5, 1, 0, 2), (5, 23), (1, 6, 2), (5, 29), (2, 5, 0, 0, 1), (4, 4), (1, 7, 0),
-    (2, 5, 3, 0, 2), (2, 5, 2, 0, 1), (2, 6, 0, 0, 2), (1, 7, 3), (2, 6, 1, 0, 2),
-    (2, 6, 3, 0, 1), (1, 7, 1), (5, 30), (5, 31), (5, 32), (5, 35), (4, 5), (1, 7, 2), (0, 11),
-    (2, 6, 0, 0, 1), (2, 6, 3, 0, 2), (2, 6, 2, 0, 1), (2, 7, 0, 0, 2), (5, 33), (1, 10, 0),
-    (2, 7, 3, 0, 1), (2, 7, 1, 0, 2), (1, 10, 3), (4, 6), (2, 7, 0, 0, 1), (1, 10, 1),
-    (2, 7, 3, 0, 2), (2, 7, 2, 0, 1), (2, 11, 0, 1, 2), (1, 10, 2), (2, 11, 3, 1, 1),
-    (2, 11, 0, 0, 2), (4, 8), (5, 34), (2, 11, 0, 1, 1), (2, 11, 3, 0, 1), (2, 11, 1, 1, 2),
-    (5, 36), (2, 11, 3, 1, 2), (2, 10, 1, 0, 2), (2, 11, 3, 0, 2), (2, 10, 0, 0, 2),
-    (2, 11, 2, 1, 1), (2, 11, 0, 0, 1), (2, 10, 3, 0, 1), (2, 11, 1, 0, 2), (2, 11, 2, 0, 1),
-    (1, 9, 0), (4, 7), (1, 9, 3), (1, 9, 1), (5, 41), (5, 43), (3, 11), (2, 10, 2, 0, 1),
-    (0, 12), (5, 37), (5, 38), (5, 42), (2, 10, 3, 0, 2), (2, 10, 0, 0, 1), (0, 13), (0, 14),
-    (2, 9, 0, 0, 2), (1, 9, 2), (5, 39), (2, 9, 3, 0, 1), (4, 11), (1, 12, 0), (4, 10),
-    (2, 9, 1, 0, 2), (1, 12, 3), (2, 9, 0, 0, 1), (1, 12, 1), (2, 9, 3, 0, 2), (1, 12, 2),
-    (2, 9, 2, 0, 1), (2, 12, 0, 0, 2), (5, 40), (5, 44), (2, 12, 3, 0, 1), (1, 13, 0),
-    (2, 12, 1, 0, 2), (5, 49), (5, 45), (5, 50), (2, 12, 2, 0, 1), (2, 13, 0, 0, 2), (1, 13, 3),
-    (2, 12, 0, 0, 1), (1, 13, 1), (4, 9), (1, 13, 2), (2, 12, 3, 0, 2), (2, 13, 3, 0, 1),
-    (5, 51), (5, 46), (2, 13, 1, 0, 2), (1, 14, 0), (2, 13, 0, 0, 1), (1, 14, 3),
-    (2, 13, 2, 0, 1), (2, 13, 3, 0, 2), (4, 12), (2, 14, 0, 0, 2), (5, 47), (2, 14, 3, 0, 1),
-    (1, 14, 1), (1, 14, 2), (4, 13), (2, 14, 0, 0, 1), (5, 52), (5, 53), (2, 14, 3, 0, 2),
-    (2, 14, 2, 0, 1), (2, 14, 1, 0, 2), (5, 48), (4, 14),
+    (5, 5), (0, 4), (5, 6), (1, 0, 2), (2, 0, 0, 0, 2), (5, 7), (2, 0, 3, 0, 1), (0, 5), (0, 6),
+    (5, 3), (1, 1, 0), (5, 8), (0, 7), (2, 0, 1, 0, 2), (1, 1, 3), (2, 0, 0, 0, 1),
+    (2, 0, 2, 0, 1), (2, 0, 3, 0, 2), (1, 1, 1), (2, 1, 3, 0, 1), (2, 1, 0, 0, 2), (1, 1, 2),
+    (4, 0), (2, 1, 1, 0, 2), (1, 2, 0), (2, 1, 0, 0, 1), (5, 4), (2, 1, 3, 0, 2),
+    (2, 1, 2, 0, 1), (1, 2, 3), (5, 9), (2, 2, 0, 0, 2), (1, 2, 1), (4, 1), (2, 2, 3, 0, 1),
+    (1, 2, 2), (2, 2, 0, 0, 1), (2, 2, 1, 0, 2), (1, 3, 0), (2, 2, 3, 0, 2), (2, 2, 2, 0, 1),
+    (5, 10), (1, 3, 3), (5, 15), (5, 11), (5, 12), (2, 3, 0, 0, 2), (1, 3, 1), (0, 8), (4, 2),
+    (5, 13), (2, 3, 3, 0, 1), (1, 3, 2), (2, 3, 1, 0, 2), (2, 3, 0, 0, 1), (1, 4, 0),
+    (2, 8, 0, 1, 2), (2, 8, 3, 1, 1), (2, 3, 3, 0, 2), (1, 4, 3), (2, 8, 0, 0, 2),
+    (2, 8, 3, 0, 1), (1, 4, 1), (2, 8, 0, 1, 1), (2, 8, 3, 1, 2), (2, 8, 1, 1, 2), (1, 4, 2),
+    (2, 8, 3, 0, 2), (5, 14), (2, 8, 1, 0, 2), (5, 16), (2, 8, 2, 1, 1), (5, 17), (5, 20),
+    (5, 21), (1, 5, 0), (1, 5, 3), (5, 24), (2, 8, 0, 0, 1), (0, 10), (2, 8, 2, 0, 1), (1, 5, 1),
+    (5, 22), (2, 3, 2, 0, 1), (5, 18), (1, 5, 2), (3, 8), (2, 4, 3, 0, 1), (2, 4, 0, 0, 2),
+    (5, 19), (5, 26), (1, 6, 0), (5, 25), (0, 9), (5, 27), (2, 4, 1, 0, 2), (1, 6, 3), (4, 3),
+    (2, 4, 0, 0, 1), (2, 4, 2, 0, 1), (1, 6, 1), (2, 4, 3, 0, 2), (5, 28), (2, 5, 3, 0, 1),
+    (2, 5, 0, 0, 2), (1, 6, 2), (5, 23), (2, 5, 1, 0, 2), (2, 5, 0, 0, 1), (2, 5, 2, 0, 1),
+    (2, 5, 3, 0, 2), (5, 29), (1, 7, 0), (1, 7, 3), (2, 6, 0, 0, 2), (2, 6, 3, 0, 1), (1, 7, 1),
+    (4, 4), (4, 5), (2, 6, 1, 0, 2), (2, 6, 3, 0, 2), (2, 6, 0, 0, 1), (2, 6, 2, 0, 1), (5, 30),
+    (5, 31), (5, 32), (1, 7, 2), (5, 35), (2, 7, 0, 0, 2), (2, 7, 3, 0, 1), (1, 10, 0), (0, 11),
+    (5, 33), (2, 7, 1, 0, 2), (1, 10, 3), (1, 10, 1), (4, 6), (2, 7, 0, 0, 1), (2, 7, 3, 0, 2),
+    (2, 7, 2, 0, 1), (1, 10, 2), (2, 11, 3, 1, 1), (2, 10, 0, 0, 2), (2, 11, 0, 1, 2), (4, 7),
+    (4, 8), (2, 11, 3, 1, 2), (2, 11, 0, 0, 2), (2, 11, 3, 0, 1), (2, 11, 3, 0, 2),
+    (2, 10, 0, 0, 1), (5, 34), (2, 11, 1, 1, 2), (2, 11, 0, 1, 1), (5, 36), (2, 11, 1, 0, 2),
+    (2, 11, 2, 1, 1), (2, 10, 3, 0, 1), (2, 10, 1, 0, 2), (1, 9, 0), (1, 9, 3), (5, 37), (3, 11),
+    (2, 11, 0, 0, 1), (2, 11, 2, 0, 1), (5, 38), (2, 10, 2, 0, 1), (2, 9, 0, 0, 2), (5, 41),
+    (2, 9, 3, 0, 1), (0, 12), (1, 9, 1), (2, 10, 3, 0, 2), (5, 42), (0, 13), (5, 39), (5, 43),
+    (0, 14), (1, 9, 2), (4, 11), (2, 9, 1, 0, 2), (1, 12, 0), (4, 10), (2, 9, 0, 0, 1),
+    (1, 12, 3), (2, 9, 2, 0, 1), (2, 9, 3, 0, 2), (2, 12, 0, 0, 2), (2, 12, 3, 0, 1), (1, 12, 1),
+    (1, 12, 2), (2, 12, 1, 0, 2), (5, 40), (5, 44), (2, 12, 0, 0, 1), (2, 12, 2, 0, 1), (5, 49),
+    (5, 50), (5, 45), (1, 13, 0), (2, 13, 0, 0, 2), (2, 12, 3, 0, 2), (1, 13, 3), (1, 13, 1),
+    (2, 13, 1, 0, 2), (2, 13, 3, 0, 1), (4, 9), (1, 13, 2), (5, 51), (2, 13, 0, 0, 1),
+    (2, 13, 2, 0, 1), (5, 46), (2, 13, 3, 0, 2), (1, 14, 0), (4, 12), (2, 14, 0, 0, 2),
+    (1, 14, 3), (2, 14, 3, 0, 1), (1, 14, 1), (2, 14, 0, 0, 1), (2, 14, 1, 0, 2), (5, 47),
+    (2, 14, 3, 0, 2), (1, 14, 2), (2, 14, 2, 0, 1), (4, 13), (5, 52), (5, 53), (4, 14), (5, 48),
 )
 
 

time: 426 us -> 422 us (level); the launches traced: 418 us -> 419 us
  no operation moved by 1% of the time
where the time goes in v6:
time: 422 us; the launch traced here: 419 us
  Pallas kernels  413 us (98%)
    pallas_call x2, Pallas kernels, run_kernel(): pl.pallas_call(functools.partial(kernel, names), out_shape=[jax.ShapeDtyp...  408 us

profile of v6, /device:TPU:0, one launch (start us, length us, event | category | flops | bytes accessed | tf_op | source)
XLA Modules:
  0.0 418.5 jit_solution(11526167353829678951)
XLA Ops:
  0.6 0.7 multiply_bitcast_fusion
  1.3 0.1 iota_add_fusion
  1.4 0.9 add.55.refs_1_
  2.3 0.7 add.52.refs_2_
  2.9 1.3 fusion.5.refs_4_
  4.2 202.8 %shard_map.220 = (bf16[1536,384]{1,0:T(8,128)(2,1)}, bf16[1536,1152]{1,0:T(8,128)(2,1)}, bf16[1536,384]{1,0:T(8,128)(2,1)}, bf16[1536,768]{1,0:T(8,128)(2,1)}, b...) custom-call(bf16[64,1536]{1,0:T(8,128)(2,1)} %bitcast.14, ...), custom_call_target="tpu_custom_call" | custom-call | tf_op jit(solution)/shard_map/pallas_call | solution.py:997
  207.1 205.3 %shard_map.221 = (f32[192,1536]{1,0:T(8,128)}, f32[192,1536]{1,0:T(8,128)}, f32[192,384]{1,0:T(8,128)}, f32[192,768]{1,0:T(8,128)}, f32[192,384]{1,0:T(8,128)}, ...) custom-call(bf16[64,1536]{1,0:T(8,128)(2,1)} %bitcast.15, ...), custom_call_target="tpu_custom_call" | custom-call | tf_op jit(solution)/shard_map/pallas_call | solution.py:997
  412.4 4.8 %shard_map.222 = (f32[192,1536]{1,0:T(8,128)}, f32[192,1536]{1,0:T(8,128)}, f32[192,384]{1,0:T(8,128)}, f32[192,768]{1,0:T(8,128)}, f32[192,384]{1,0:T(8,128)}, ...) custom-call(f32[192,1536]{1,0:T(8,128)} %get-tuple-element.77.refs_0, ...), custom_call_target="tpu_custom_call" | custom-call | tf_op jit(solution)/shard_map/pallas_call | solution.py:1992
  417.2 0.8 constant_dynamic-slice_fusion
  417.9 0.6 fusion.6
